TPU v7x, 128 devices: a whole 4x4x4 slice. The times are simulated.
128 devices in a mesh: aux: 64 (over y, z_hi, x, core), ao: 2 (over z_lo).
Axes of the slice: x: 4, y: 4, z: 4 (z_hi: 2, z_lo: 2; z = z_hi * 2 + z_lo), core: 2. Of those that a mesh axis runs over, the one named last changes fastest.
Arguments:
- ints: bfloat16 [1024, 768, 768], P('aux', 'ao'), may hold values from -1.25 to 1.25
- occ_coef: bfloat16 [768, 128], replicated, may hold values from -0.21875 to 0.21875
- vir_coef: bfloat16 [768, 512], P('ao'), may hold values from -0.21875 to 0.21875
- occ_energy: float32 [128], replicated, may hold values from -2 to -0.3
- vir_energy: float32 [512], replicated, may hold values from 0.3 to 3
Outputs:
- density: float32 [128, 512, 512], P('aux', 'ao')
All inputs are finite; a program needn't handle non-finite values.
Results may differ from a plain program's by a relative error of at most 0.0065.
Values may be sent and summed in bfloat16 or wider, within the bound.
No kernel may reach another device: no remote copies, remote signals or barrier semaphores. Data moves between devices by JAX's collectives and lax.ppermute only.
A program may use at most 128 MiB of HBM per device.

v0:
```python
import jax
import jax.numpy as jnp
from jax import lax
from jax.sharding import PartitionSpec as P

CYCLE = 4


def in_blocks(value, dim, length):
    dims = value.shape
    tiles = value.reshape(*dims[:dim], length, dims[dim] // length, *dims[dim + 1 :])
    return jnp.moveaxis(tiles, dim, 0)


def sum_at_owner(value, axis, dim):
    tiles = in_blocks(value, dim, lax.axis_size(axis))
    arrived = lax.all_to_all(tiles, axis, split_axis=0, concat_axis=0, tiled=True)
    return arrived.astype(jnp.float32).sum(axis=0)


def from_everyone(value, axis):
    copies = jnp.broadcast_to(value, (lax.axis_size(axis), *value.shape))
    return lax.all_to_all(copies, axis, split_axis=0, concat_axis=0, tiled=True)


def laid_out(tiles, dim):
    dims = list(tiles.shape[1:])
    dims[dim] *= tiles.shape[0]
    return jnp.moveaxis(tiles, 0, dim).reshape(dims)


def collect(value, axis, dim):
    tiles = from_everyone(value, axis)
    return laid_out(tiles, dim)


def passed_along(block, axis, distance):
    devices = range(lax.axis_size(axis))
    route = [((i - distance) % len(devices), i) for i in devices]
    return lax.ppermute(block, axis, route)


def shards(ints, occ_coef, vir_coef, occ_energy, vir_energy):
    aux_index = lax.axis_index("aux")
    ao_index = lax.axis_index("ao")
    aux_count = lax.axis_size("aux")
    ao_count = lax.axis_size("ao")
    occ_block = occ_coef.shape[1] // aux_count
    occ_share = occ_block // ao_count
    half_ints = jnp.einsum(
        "qmn,ni->qmi", ints, occ_coef, preferred_element_type=jnp.float32
    ).astype(jnp.bfloat16)
    partial_sum = jnp.einsum("qmi,ma->qia", half_ints, vir_coef, preferred_element_type=jnp.float32)
    summed_half = sum_at_owner(partial_sum.astype(jnp.bfloat16), "ao", 2).astype(jnp.bfloat16)
    grouped = lax.all_to_all(summed_half, "aux", split_axis=1, concat_axis=0, tiled=True)
    own_block = collect(grouped, "ao", 2)
    own_energy = lax.dynamic_slice_in_dim(occ_energy, aux_index * occ_block, occ_block)
    pair_piece = lax.dynamic_slice_in_dim(own_block, ao_index * occ_share, occ_share, 1)
    vir_pairs = vir_energy[:, None] + vir_energy[None, :]
    nvir_full = own_block.shape[2]

    def add_pairs(density_sum, visitor, block_index):
        pair_energy = lax.dynamic_slice_in_dim(
            occ_energy, block_index * occ_block + ao_index * occ_share, occ_share
        )
        integrals = jnp.einsum(
            "qia,qjb->ijab", own_block, visitor, preferred_element_type=jnp.float32
        )
        energy_gap = (
            own_energy[:, None, None, None]
            + pair_energy[None, :, None, None]
            - vir_pairs[None, None]
        )
        scaled = integrals / energy_gap
        amplitude = scaled.astype(jnp.bfloat16)
        mixed = (2.0 * scaled - jnp.swapaxes(scaled, 2, 3)).astype(jnp.bfloat16)
        return density_sum + jnp.einsum(
            "ijac,ijbc->iab", amplitude, mixed, preferred_element_type=jnp.float32
        )

    density_start = jnp.zeros((occ_block, nvir_full, nvir_full), jnp.float32)
    density_sum = add_pairs(density_start, pair_piece, aux_index)
    from_below = pair_piece
    from_above = pair_piece
    for offset in range(1, CYCLE + 1):
        from_below = passed_along(from_below, "aux", 1)
        from_above = passed_along(from_above, "aux", -1)
        density_sum = add_pairs(
            density_sum, from_below, (aux_index + aux_count - offset) % aux_count
        )
        density_sum = add_pairs(density_sum, from_above, (aux_index + offset) % aux_count)
    return sum_at_owner(density_sum.astype(jnp.bfloat16), "ao", 1)


def solution(mesh):
    return jax.shard_map(
        shards,
        mesh=mesh,
        in_specs=(P("aux", "ao", None), P(), P("ao", None), P(), P()),
        out_specs=P("aux", "ao", None),
        check_vma=False,
    )
```

profile of v0, /device:TPU:0, one launch (start us, length us, event | category | flops | bytes accessed | tf_op | source)
XLA Modules:
  0.0 227.9 jit_solution(1639875431510653476)
XLA Ops:
  0.0 1.0 copy-done
  1.0 9.2 %convolution_convert_fusion = bf16[16,128,512]{2,1,0:T(8,128)(2,1)S(1)} fusion(bf16[16,384,768]{2,1,0:T(8,128)(2,1)} %param.5, bf16[384,512]{1,0:T(8,128)(2,1)S(1)} %copy-done, bf16[768,128]{1,0:T(8,128)(2,1)} %param.6), kind=kOutput, calls=%fused_computation.30 | convolution fusion | flops 2015100928 | bytes 12124160 | tf_op jit(solution)/shard_map/qmi,ma->qia/dot_general | solution.py:53
  10.2 0.3 copy.189
  10.4 27.9 %all_to_all.33 = bf16[2,16,128,256]{3,2,1,0:T(8,128)(2,1)S(1)} all-to-all(bf16[2,16,128,256]{3,2,1,0:T(8,128)(2,1)S(1)} %bitcast.243), channel_id=1, replica_groups=mesh['aux'=64,'ao'=2] {'ao'}, dimensions={0} | all-to-all | bytes 4194304 | tf_op jit(solution)/shard_map/all_to_all | solution.py:17
  38.4 0.7 reduce_sum.21
  39.0 0.6 copy.125
  39.6 30.4 %all_to_all.34 = bf16[16,128,256]{2,0,1:T(8,128)(2,1)S(1)} all-to-all(bf16[16,128,256]{2,0,1:T(8,128)(2,1)S(1)} %copy.125), channel_id=1, replica_groups=mesh['aux'=64,'ao'=2] {'aux'}, dimensions={1} | all-to-all | bytes 2097152 | tf_op jit(solution)/shard_map/all_to_all | solution.py:55
  70.1 1.5 broadcast_in_dim.2
  71.6 3.9 %all-to-all-start.2 = ((bf16[2,1024,2,256]{3,1,2,0:T(8,128)(2,1)}), bf16[2,1024,2,256]{3,1,2,0:T(8,128)(2,1)S(1)}, u32[]{:S(2)}, u32[]{:S(2)}) async-start(bf16[2,1024,2,256]{3,1,2,0:T(8,128)(2,1)} %broadcast_in_dim.2), calls=%async_computation.2 | async-start | bytes 4194304 | tf_op jit(solution)/shard_map/all_to_all | solution.py:23
  75.6 0.7 fusion.83
  76.3 0.7 broadcast_add_fusion.1
  77.0 1.1 broadcast_add_fusion
  78.2 22.7 %all-to-all-done.2 = bf16[2,1024,2,256]{3,1,2,0:T(8,128)(2,1)S(1)} async-done(((bf16[2,1024,2,256]{3,1,2,0:T(8,128)(2,1)}), bf16[2,1024,2,256]{3,1,2,0:T(8,128)(2,1)S(1)}, u32[]{:S(2)}, u32[]{:S(2)}) %all-to-all-start.2) | async-done | bytes 2097184 | tf_op jit(solution)/shard_map/all_to_all | solution.py:23
  100.8 0.2 copy.186
  101.2 0.5 collective-permute-start
  101.7 5.4 %broadcast_add_fusion.8 = (f32[2]{0:T(128)S(1)}, f32[2]{0:T(128)S(1)}, f32[2]{0:T(128)S(1)}, f32[2]{0:T(128)S(1)}, f32[2]{0:T(128)S(1)}, /*index=5*/f32[2]{0:T(128)S(1)}, f32[2]{0:T(128)S(1)}, f32[2]{0:T(128)S(1)}) fusion(f32[2]{0:T(128)S(1)} %get-tuple-element.6, f32[]{:T(128)} %bitcast.19, f32[]{:T(128)} %bitcast.67, f32[]{:T(128)} %bitcast.59, ...), kind=kLoop, calls=%fused_computation.96 | loop fusion | flops 16 | bytes 104 | tf_op jit(solution)/shard_map/add | solution.py:70
  107.1 1.3 bitcast_divide_fusion.8
  108.4 1.8 copy.129
  110.2 4.0 %fusion.10 = f32[2,512,512]{2,1,0:T(8,128)} fusion(f32[2,1,512,512]{2,3,0,1:T(8,128)S(1)} %bitcast_divide_fusion.8, f32[2,1,512,512]{3,2,0,1:T(8,128)} %copy.129), kind=kOutput, calls=%fused_computation.33 | convolution fusion | flops 538968064 | bytes 6291456 | tf_op jit(solution)/shard_map/ijac,ijbc->iab/dot_general | solution.py:77
  114.2 7.0 %collective-permute-start.3 = (bf16[1024,1,512]{2,0,1:T(8,128)(2,1)}, bf16[1024,1,512]{2,0,1:T(8,128)(2,1)}, u32[]{:S(2)}, u32[]{:S(2)}) collective-permute-start(bf16[1024,1,512]{2,0,1:T(8,128)(2,1)} %collective-permute-done.1), channel_id=1, source_target_pairs={{2,0},{4,2},{6,4},{8,6},{10,8},{12,10},{14,12},{16,14},{18,16},{20... | collective-permute-start | bytes 3145736 | tf_op jit(solution)/shard_map/ppermute | solution.py:40
  121.3 2.5 %bitcast_divide_fusion.7 = f32[2,1,512,512]{2,3,0,1:T(8,128)S(1)} fusion(bf16[1024,2,512]{2,0,1:T(8,128)(2,1)S(1)} %bitcast.247, bf16[1024,1,512]{2,0,1:T(8,128)(2,1)} %collective-permute-done, f32[2]{0:T(128)S(1)} %get-tuple-element.7, f32[512,512]{0,1:T(8,128)S(1)} %copy-done.11), kind=kOutput, calls=%fused_computation.8 | convolution fusion | flops 1074790400 | bytes 6291464 | tf_op jit(solution)/shard_map/qia,qjb->ijab/dot_general | solution.py:66
  123.8 3.9 %bitcast_divide_fusion.6 = f32[2,1,512,512]{2,3,0,1:T(8,128)} fusion(bf16[1024,2,512]{2,0,1:T(8,128)(2,1)S(1)} %bitcast.248, bf16[1024,1,512]{2,0,1:T(8,128)(2,1)} %collective-permute-done.1, f32[2]{0:T(128)S(1)} %get-tuple-element.13, f32[512,512]{0,1:T(8,128)S(1)} %copy-done.11), kind=kOutput, calls=%fused_computation.7 | convolution fusion | flops 1074790400 | bytes 6291464 | tf_op jit(solution)/shard_map/qia,qjb->ijab/dot_general | solution.py:66
  127.7 3.0 %copy.135 = f32[2,1,512,512]{3,2,0,1:T(8,128)} copy(f32[2,1,512,512]{2,3,0,1:T(8,128)} %bitcast_divide_fusion.6) | data formatting | bytes 4194304 | tf_op jit(solution)/shard_map/div | solution.py:74
  130.7 1.8 copy.132
  132.5 5.3 %fusion.16 = f32[2,512,512]{2,1,0:T(8,128)} fusion(f32[2,1,512,512]{2,3,0,1:T(8,128)} %bitcast_divide_fusion.6, f32[2,1,512,512]{3,2,0,1:T(8,128)} %copy.135), kind=kOutput, calls=%fused_computation.37 | convolution fusion | flops 538968064 | bytes 6291456 | tf_op jit(solution)/shard_map/ijac,ijbc->iab/dot_general | solution.py:77
  137.8 2.4 %fusion.13 = f32[2,512,512]{2,1,0:T(8,128)} fusion(f32[2,1,512,512]{2,3,0,1:T(8,128)S(1)} %bitcast_divide_fusion.7, f32[2,1,512,512]{3,2,0,1:T(8,128)S(1)} %copy-done.3), kind=kOutput, calls=%fused_computation.35 | convolution fusion | flops 538968064 | bytes 6291456 | tf_op jit(solution)/shard_map/ijac,ijbc->iab/dot_general | solution.py:77
  140.2 7.5 %collective-permute-start.5 = (bf16[1024,1,512]{2,0,1:T(8,128)(2,1)}, bf16[1024,1,512]{2,0,1:T(8,128)(2,1)}, u32[]{:S(2)}, u32[]{:S(2)}) collective-permute-start(bf16[1024,1,512]{2,0,1:T(8,128)(2,1)} %collective-permute-done.3), channel_id=1, source_target_pairs={{2,0},{4,2},{6,4},{8,6},{10,8},{12,10},{14,12},{16,14},{18,16},{20... | collective-permute-start | bytes 3145736 | tf_op jit(solution)/shard_map/ppermute | solution.py:40
  147.7 2.5 %bitcast_divide_fusion.5 = f32[2,1,512,512]{2,3,0,1:T(8,128)S(1)} fusion(bf16[1024,2,512]{2,0,1:T(8,128)(2,1)S(1)} %bitcast.249, bf16[1024,1,512]{2,0,1:T(8,128)(2,1)} %collective-permute-done.2, f32[2]{0:T(128)S(1)} %get-tuple-element.12, f32[512,512]{0,1:T(8,128)S(1)} %copy-done.12), kind=kOutput, calls=%fused_computation.6 | convolution fusion | flops 1074790400 | bytes 6291464 | tf_op jit(solution)/shard_map/qia,qjb->ijab/dot_general | solution.py:66
  150.2 3.8 %bitcast_divide_fusion.4 = f32[2,1,512,512]{2,3,0,1:T(8,128)} fusion(bf16[1024,2,512]{2,0,1:T(8,128)(2,1)S(1)} %bitcast.250, bf16[1024,1,512]{2,0,1:T(8,128)(2,1)} %collective-permute-done.3, f32[2]{0:T(128)S(1)} %get-tuple-element.11, f32[512,512]{0,1:T(8,128)S(1)} %copy-done.12), kind=kOutput, calls=%fused_computation.5 | convolution fusion | flops 1074790400 | bytes 6291464 | tf_op jit(solution)/shard_map/qia,qjb->ijab/dot_general | solution.py:66
  154.0 2.9 %copy.141 = f32[2,1,512,512]{3,2,0,1:T(8,128)} copy(f32[2,1,512,512]{2,3,0,1:T(8,128)} %bitcast_divide_fusion.4) | data formatting | bytes 4194304 | tf_op jit(solution)/shard_map/div | solution.py:74
  156.9 5.2 %fusion.22 = f32[2,512,512]{2,1,0:T(8,128)} fusion(f32[2,1,512,512]{2,3,0,1:T(8,128)} %bitcast_divide_fusion.4, f32[2,1,512,512]{3,2,0,1:T(8,128)} %copy.141), kind=kOutput, calls=%fused_computation.41 | convolution fusion | flops 538968064 | bytes 6291456 | tf_op jit(solution)/shard_map/ijac,ijbc->iab/dot_general | solution.py:77
  162.1 1.8 copy.138
  163.9 4.0 %fusion.19 = f32[2,512,512]{2,1,0:T(8,128)} fusion(f32[2,1,512,512]{2,3,0,1:T(8,128)S(1)} %bitcast_divide_fusion.5, f32[2,1,512,512]{3,2,0,1:T(8,128)} %copy.138), kind=kOutput, calls=%fused_computation.39 | convolution fusion | flops 538968064 | bytes 6291456 | tf_op jit(solution)/shard_map/ijac,ijbc->iab/dot_general | solution.py:77
  167.9 2.5 %bitcast_divide_fusion.3 = f32[2,1,512,512]{2,3,0,1:T(8,128)S(1)} fusion(bf16[1024,2,512]{2,0,1:T(8,128)(2,1)S(1)} %bitcast.251, bf16[1024,1,512]{2,0,1:T(8,128)(2,1)} %collective-permute-done.4, f32[2]{0:T(128)S(1)} %get-tuple-element.10, f32[512,512]{0,1:T(8,128)S(1)} %copy-done.12), kind=kOutput, calls=%fused_computation.4 | convolution fusion | flops 1074790400 | bytes 6291464 | tf_op jit(solution)/shard_map/qia,qjb->ijab/dot_general | solution.py:66
  170.4 3.8 %bitcast_divide_fusion.2 = f32[2,1,512,512]{2,3,0,1:T(8,128)} fusion(bf16[1024,2,512]{2,0,1:T(8,128)(2,1)S(1)} %bitcast.252, bf16[1024,1,512]{2,0,1:T(8,128)(2,1)} %collective-permute-done.5, f32[2]{0:T(128)S(1)} %get-tuple-element.9, f32[512,512]{0,1:T(8,128)S(1)} %copy-done.12), kind=kOutput, calls=%fused_computation.3 | convolution fusion | flops 1074790400 | bytes 6291464 | tf_op jit(solution)/shard_map/qia,qjb->ijab/dot_general | solution.py:66
  174.3 2.9 %copy.147 = f32[2,1,512,512]{3,2,0,1:T(8,128)} copy(f32[2,1,512,512]{2,3,0,1:T(8,128)} %bitcast_divide_fusion.2) | data formatting | bytes 4194304 | tf_op jit(solution)/shard_map/div | solution.py:74
  177.1 1.8 copy.144
  179.0 7.5 %collective-permute-start.7 = (bf16[1024,1,512]{2,0,1:T(8,128)(2,1)}, bf16[1024,1,512]{2,0,1:T(8,128)(2,1)}, u32[]{:S(2)}, u32[]{:S(2)}) collective-permute-start(bf16[1024,1,512]{2,0,1:T(8,128)(2,1)} %collective-permute-done.5), channel_id=1, source_target_pairs={{2,0},{4,2},{6,4},{8,6},{10,8},{12,10},{14,12},{16,14},{18,16},{20... | collective-permute-start | bytes 3145736 | tf_op jit(solution)/shard_map/ppermute | solution.py:40
  186.5 5.1 %fusion.28 = f32[2,512,512]{2,1,0:T(8,128)} fusion(f32[2,1,512,512]{2,3,0,1:T(8,128)} %bitcast_divide_fusion.2, f32[2,1,512,512]{3,2,0,1:T(8,128)} %copy.147), kind=kOutput, calls=%fused_computation.45 | convolution fusion | flops 538968064 | bytes 6291456 | tf_op jit(solution)/shard_map/ijac,ijbc->iab/dot_general | solution.py:77
  191.6 2.3 %fusion.25 = f32[2,512,512]{2,1,0:T(8,128)} fusion(f32[2,1,512,512]{2,3,0,1:T(8,128)S(1)} %bitcast_divide_fusion.3, f32[2,1,512,512]{3,2,0,1:T(8,128)S(1)} %copy-done.2), kind=kOutput, calls=%fused_computation.43 | convolution fusion | flops 538968064 | bytes 6291456 | tf_op jit(solution)/shard_map/ijac,ijbc->iab/dot_general | solution.py:77
  193.9 2.5 %bitcast_divide_fusion.1 = f32[2,1,512,512]{2,3,0,1:T(8,128)S(1)} fusion(bf16[1024,2,512]{2,0,1:T(8,128)(2,1)S(1)} %bitcast.253, bf16[1024,1,512]{2,0,1:T(8,128)(2,1)} %collective-permute-done.6, f32[2]{0:T(128)S(1)} %get-tuple-element.8, f32[512,512]{0,1:T(8,128)S(1)} %copy-done.12), kind=kOutput, calls=%fused_computation.2 | convolution fusion | flops 1074790400 | bytes 6291464 | tf_op jit(solution)/shard_map/qia,qjb->ijab/dot_general | solution.py:66
  196.4 1.8 copy.150
  198.2 4.0 %fusion.31 = f32[2,512,512]{2,1,0:T(8,128)} fusion(f32[2,1,512,512]{2,3,0,1:T(8,128)S(1)} %bitcast_divide_fusion.1, f32[2,1,512,512]{3,2,0,1:T(8,128)} %copy.150), kind=kOutput, calls=%fused_computation.47 | convolution fusion | flops 538968064 | bytes 6291456 | tf_op jit(solution)/shard_map/ijac,ijbc->iab/dot_general | solution.py:77
  202.2 2.5 %bitcast_divide_fusion = f32[2,1,512,512]{2,3,0,1:T(8,128)S(1)} fusion(bf16[1024,2,512]{2,0,1:T(8,128)(2,1)S(1)} %bitcast.254, bf16[1024,1,512]{2,0,1:T(8,128)(2,1)} %collective-permute-done.7, f32[2]{0:T(128)S(1)} %get-tuple-element.5, f32[512,512]{0,1:T(8,128)S(1)} %copy-done.12), kind=kOutput, calls=%fused_computation.1 | convolution fusion | flops 1074790400 | bytes 6291464 | tf_op jit(solution)/shard_map/qia,qjb->ijab/dot_general | solution.py:66
  204.7 1.8 copy.153
  206.6 8.1 %add_convert_fusion = bf16[2,512,512]{2,1,0:T(8,128)(2,1)S(1)} fusion(f32[2,512,512]{2,1,0:T(8,128)} %fusion.31, f32[2,512,512]{2,1,0:T(8,128)} %fusion.28, f32[2,512,512]{2,1,0:T(8,128)} %fusion.25, f32[2,512,512]{2,1,0:T(8,128)} %fusion.22, f32[2,512,512]{2,1,0:T(8,128)} %fusion.19, f32[2,512,512]{2,1,0:T(8,128)} %fusion.16, f32[2,512,512]{2,1,0:T(8,128)} %fusion.10, ...), kind=kOutput, calls=%fused_computation.29 | convolution fusion | flops 543686656 | bytes 22020096 | tf_op jit(solution)/shard_map/ijac,ijbc->iab/dot_general | solution.py:77
  214.8 12.0 %all_to_all.35 = bf16[2,2,256,512]{3,2,1,0:T(8,128)(2,1)S(1)} all-to-all(bf16[2,2,256,512]{3,2,1,0:T(8,128)(2,1)S(1)} %bitcast.258), channel_id=1, replica_groups=mesh['aux'=64,'ao'=2] {'ao'}, dimensions={0} | all-to-all | bytes 2097152 | tf_op jit(solution)/shard_map/all_to_all | solution.py:17
  226.7 1.1 convert_reduce_fusion
  (44 shorter events, 0.5 us)
Async XLA Ops:
  0.0 1.0 copy-start
  71.6 4.1 %copy-start.13 = (f32[128]{0:T(128)S(1)}, f32[128]{0:T(128)}, u32[]{:S(2)}) copy-start(f32[128]{0:T(128)} %param.8) | copy-start | bytes 1540
  71.6 5.5 %copy-start.14 = (f32[512]{0:T(512)S(1)}, f32[512]{0:T(512)}, u32[]{:S(2)}) copy-start(f32[512]{0:T(512)} %param.9) | copy-start | bytes 6148
  71.6 29.3 %all-to-all-start.2 = ((bf16[2,1024,2,256]{3,1,2,0:T(8,128)(2,1)}), bf16[2,1024,2,256]{3,1,2,0:T(8,128)(2,1)S(1)}, u32[]{:S(2)}, u32[]{:S(2)}) async-start(bf16[2,1024,2,256]{3,1,2,0:T(8,128)(2,1)} %broadcast_in_dim.2), calls=%async_computation.2 | async-start | bytes 4194304 | tf_op jit(solution)/shard_map/all_to_all | solution.py:23
  101.0 6.1 %copy-start.4 = (bf16[2,2,128,8,256]{4,3,0,2,1:T(8,128)(2,1)}, bf16[2,2,128,8,256]{4,3,0,2,1:T(8,128)(2,1)S(1)}, u32[]{:S(2)}) copy-start(bf16[2,2,128,8,256]{4,3,0,2,1:T(8,128)(2,1)S(1)} %copy.186) | copy-start | bytes 6291460
  101.0 6.1 %copy-start.10 = (f32[512,512]{0,1:T(8,128)S(1)}, f32[512,512]{0,1:T(8,128)}, u32[]{:S(2)}) copy-start(f32[512,512]{0,1:T(8,128)} %broadcast_add_fusion) | copy-start | bytes 3145732
  101.1 13.1 %collective-permute-start.1 = (bf16[1024,1,512]{2,0,1:T(8,128)(2,1)S(1)}, bf16[1024,1,512]{2,0,1:T(8,128)(2,1)}, u32[]{:S(2)}, u32[]{:S(2)}) collective-permute-start(bf16[1024,1,512]{2,0,1:T(8,128)(2,1)S(1)} %constant_dynamic-slice_fusion), channel_id=1, source_target_pairs={{2,0},{4,2},{6,4},{8,6},{10,8},{12,10},{14,12},{16,14},{18,16},{20... | collective-permute-start | bytes 3145736 | tf_op jit(solution)/shard_map/ppermute | solution.py:40
  101.2 20.1 %collective-permute-start = (bf16[1024,1,512]{2,0,1:T(8,128)(2,1)S(1)}, bf16[1024,1,512]{2,0,1:T(8,128)(2,1)}, u32[]{:S(2)}, u32[]{:S(2)}) collective-permute-start(bf16[1024,1,512]{2,0,1:T(8,128)(2,1)S(1)} %constant_dynamic-slice_fusion), channel_id=1, source_target_pairs={{126,0},{0,2},{2,4},{4,6},{6,8},{8,10},{10,12},{12,14},{14,16},{16... | collective-permute-start | bytes 3145736 | tf_op jit(solution)/shard_map/ppermute | solution.py:40
  110.2 11.1 %copy-start.5 = (bf16[2,2,128,8,256]{4,3,0,2,1:T(8,128)(2,1)S(1)}, bf16[2,2,128,8,256]{4,3,0,2,1:T(8,128)(2,1)}, u32[]{:S(2)}) copy-start(bf16[2,2,128,8,256]{4,3,0,2,1:T(8,128)(2,1)} %copy-done.4) | copy-start | bytes 6291460
  110.2 11.1 %copy-start.11 = (f32[512,512]{0,1:T(8,128)S(1)}, f32[512,512]{0,1:T(8,128)}, u32[]{:S(2)}) copy-start(f32[512,512]{0,1:T(8,128)} %broadcast_add_fusion) | copy-start | bytes 3145732
  114.2 26.0 %collective-permute-start.3 = (bf16[1024,1,512]{2,0,1:T(8,128)(2,1)}, bf16[1024,1,512]{2,0,1:T(8,128)(2,1)}, u32[]{:S(2)}, u32[]{:S(2)}) collective-permute-start(bf16[1024,1,512]{2,0,1:T(8,128)(2,1)} %collective-permute-done.1), channel_id=1, source_target_pairs={{2,0},{4,2},{6,4},{8,6},{10,8},{12,10},{14,12},{16,14},{18,16},{20... | collective-permute-start | bytes 3145736 | tf_op jit(solution)/shard_map/ppermute | solution.py:40
  121.3 26.3 %collective-permute-start.2 = (bf16[1024,1,512]{2,0,1:T(8,128)(2,1)}, bf16[1024,1,512]{2,0,1:T(8,128)(2,1)}, u32[]{:S(2)}, u32[]{:S(2)}) collective-permute-start(bf16[1024,1,512]{2,0,1:T(8,128)(2,1)} %collective-permute-done), channel_id=1, source_target_pairs={{126,0},{0,2},{2,4},{4,6},{6,8},{8,10},{10,12},{12,14},{14,16},{16... | collective-permute-start | bytes 3145736 | tf_op jit(solution)/shard_map/ppermute | solution.py:40
  132.5 5.3 %copy-start.3 = (f32[2,1,512,512]{3,2,0,1:T(8,128)S(1)}, f32[2,1,512,512]{3,2,0,1:T(8,128)}, u32[]{:S(2)}) copy-start(f32[2,1,512,512]{3,2,0,1:T(8,128)} %copy.132) | copy-start | bytes 6291460
  137.8 9.9 %copy-start.6 = (bf16[2,2,128,8,256]{4,3,0,2,1:T(8,128)(2,1)S(1)}, bf16[2,2,128,8,256]{4,3,0,2,1:T(8,128)(2,1)}, u32[]{:S(2)}) copy-start(bf16[2,2,128,8,256]{4,3,0,2,1:T(8,128)(2,1)} %copy-done.4) | copy-start | bytes 6291460
  137.8 9.9 %copy-start.12 = (f32[512,512]{0,1:T(8,128)S(1)}, f32[512,512]{0,1:T(8,128)}, u32[]{:S(2)}) copy-start(f32[512,512]{0,1:T(8,128)} %broadcast_add_fusion) | copy-start | bytes 3145732
  140.2 30.3 %collective-permute-start.5 = (bf16[1024,1,512]{2,0,1:T(8,128)(2,1)}, bf16[1024,1,512]{2,0,1:T(8,128)(2,1)}, u32[]{:S(2)}, u32[]{:S(2)}) collective-permute-start(bf16[1024,1,512]{2,0,1:T(8,128)(2,1)} %collective-permute-done.3), channel_id=1, source_target_pairs={{2,0},{4,2},{6,4},{8,6},{10,8},{12,10},{14,12},{16,14},{18,16},{20... | collective-permute-start | bytes 3145736 | tf_op jit(solution)/shard_map/ppermute | solution.py:40
  147.6 20.3 %collective-permute-start.4 = (bf16[1024,1,512]{2,0,1:T(8,128)(2,1)}, bf16[1024,1,512]{2,0,1:T(8,128)(2,1)}, u32[]{:S(2)}, u32[]{:S(2)}) collective-permute-start(bf16[1024,1,512]{2,0,1:T(8,128)(2,1)} %collective-permute-done.2), channel_id=1, source_target_pairs={{126,0},{0,2},{2,4},{4,6},{6,8},{8,10},{10,12},{12,14},{14,16},{16... | collective-permute-start | bytes 3145736 | tf_op jit(solution)/shard_map/ppermute | solution.py:40
  163.9 4.0 %copy-start.7 = (bf16[2,2,128,8,256]{4,3,0,2,1:T(8,128)(2,1)S(1)}, bf16[2,2,128,8,256]{4,3,0,2,1:T(8,128)(2,1)}, u32[]{:S(2)}) copy-start(bf16[2,2,128,8,256]{4,3,0,2,1:T(8,128)(2,1)} %copy-done.4) | copy-start | bytes 6291460
  167.9 26.0 %collective-permute-start.6 = (bf16[1024,1,512]{2,0,1:T(8,128)(2,1)}, bf16[1024,1,512]{2,0,1:T(8,128)(2,1)}, u32[]{:S(2)}, u32[]{:S(2)}) collective-permute-start(bf16[1024,1,512]{2,0,1:T(8,128)(2,1)} %collective-permute-done.4), channel_id=1, source_target_pairs={{126,0},{0,2},{2,4},{4,6},{6,8},{8,10},{10,12},{12,14},{14,16},{16... | collective-permute-start | bytes 3145736 | tf_op jit(solution)/shard_map/ppermute | solution.py:40
  179.0 12.6 %copy-start.2 = (f32[2,1,512,512]{3,2,0,1:T(8,128)S(1)}, f32[2,1,512,512]{3,2,0,1:T(8,128)}, u32[]{:S(2)}) copy-start(f32[2,1,512,512]{3,2,0,1:T(8,128)} %copy.144) | copy-start | bytes 6291460
  179.0 23.3 %collective-permute-start.7 = (bf16[1024,1,512]{2,0,1:T(8,128)(2,1)}, bf16[1024,1,512]{2,0,1:T(8,128)(2,1)}, u32[]{:S(2)}, u32[]{:S(2)}) collective-permute-start(bf16[1024,1,512]{2,0,1:T(8,128)(2,1)} %collective-permute-done.5), channel_id=1, source_target_pairs={{2,0},{4,2},{6,4},{8,6},{10,8},{12,10},{14,12},{16,14},{18,16},{20... | collective-permute-start | bytes 3145736 | tf_op jit(solution)/shard_map/ppermute | solution.py:40
  191.6 2.3 %copy-start.8 = (bf16[2,2,128,8,256]{4,3,0,2,1:T(8,128)(2,1)S(1)}, bf16[2,2,128,8,256]{4,3,0,2,1:T(8,128)(2,1)}, u32[]{:S(2)}) copy-start(bf16[2,2,128,8,256]{4,3,0,2,1:T(8,128)(2,1)} %copy-done.4) | copy-start | bytes 6291460
  198.2 4.0 %copy-start.9 = (bf16[2,2,128,8,256]{4,3,0,2,1:T(8,128)(2,1)S(1)}, bf16[2,2,128,8,256]{4,3,0,2,1:T(8,128)(2,1)}, u32[]{:S(2)}) copy-start(bf16[2,2,128,8,256]{4,3,0,2,1:T(8,128)(2,1)} %copy-done.4) | copy-start | bytes 6291460
  214.7 13.1 %copy-start.1 = (bf16[384,512]{1,0:T(8,128)(2,1)S(1)}, bf16[384,512]{1,0:T(8,128)(2,1)}, u32[]{:S(2)}) copy-start(bf16[384,512]{1,0:T(8,128)(2,1)} %param.7) | copy-start | bytes 1179652
where the time goes:
time: 229 us; the launch traced here: 228 us
  matrix products  74.7 us (33%)
  blocking collectives  70.3 us (31%)
  starting transfers between devices  26.5 us (12%)
  local copies, waits for them, and re-layouts  24.2 us (11%)
  waiting for transfers between devices  22.8 us (10%)
  other arithmetic  9.03 us (4%)
    dot_general x9, matrix products, add_pairs(): jnp.einsum('ijac,ijbc->iab', amplitude, mixed, preferred_element_type=jnp...  40.2 us
    all_to_all x2, blocking collectives, sum_at_owner(): lax.all_to_all(tiles, axis, split_axis=0, concat_axis=0, tiled=True)  39.9 us
    all_to_all x1, blocking collectives, shards(): lax.all_to_all(summed_half, 'aux', split_axis=1, concat_axis=0, tiled=True)  30.4 us
    dot_general x9, matrix products, add_pairs(): jnp.einsum('qia,qjb->ijab', own_block, visitor, preferred_element_type=jn...  25.3 us
    all_to_all x1, waiting for transfers between devices, from_everyone(): return lax.all_to_all(copies, axis, split_axis=0, concat_axis=0, tiled=True)  22.7 us
    ppermute x8, starting transfers between devices, passed_along(): return lax.ppermute(block, axis, route)  22.6 us
    div x9, local copies, waits for them, and re-layouts, add_pairs(): scaled = integrals / energy_gap  19.7 us
    dot_general x1, matrix products, shards(): jnp.einsum('qmi,ma->qia', half_ints, vir_coef, preferred_element_type=jnp...  9.17 us
  transfers between devices with their start and end apart: 9, of which 2 were waited for; matrix products, arithmetic and copies ran while one was open for 35% of the time, Pallas kernels for 0%

commit v1 on v0

v1 whole, which is shorter than its diff:
```python
import jax
import jax.numpy as jnp
from jax import lax
from jax.experimental import pallas as pl
from jax.experimental.pallas import tpu as pltpu
from jax.sharding import PartitionSpec as P

CYCLE = 4
ROW = 8
LANES = 128
BOTH = ("aux", "ao")
VMEM_LIMIT = 56 * 1024 * 1024


def flipped(block):
    return (block // ROW) % 2


def transform_kernel(slots, ints_ref, occ_ref, vir_ref, out_ref, held_ref):
    step = pl.program_id(0)
    chunk, rows, width = ints_ref.shape
    nocc = occ_ref.shape[1]
    slab = ints_ref[...].reshape(chunk * rows, width)
    half = jnp.dot(slab, occ_ref[...], preferred_element_type=jnp.float32).astype(jnp.bfloat16)
    for k in range(chunk):
        part = lax.dot_general(
            half[k * rows : (k + 1) * rows],
            vir_ref[...],
            (((0,), (0,)), ((), ())),
            preferred_element_type=jnp.float32,
        )
        start = pl.multiple_of((step * chunk + k) * nocc, nocc)
        for column in range(0, part.shape[1], LANES):
            row = column // LANES * (held_ref.shape[0] * LANES // part.shape[1])
            held_ref[pl.ds(row + start, nocc), :] = part[:, column : column + LANES]

    @pl.when(step == pl.num_programs(0) - 1)
    def _():
        count, nvir = out_ref.shape[1:]
        for orbital in range(nocc):
            for column in range(0, nvir, LANES):
                row = column // LANES * count * nocc + orbital
                tile = held_ref[pl.ds(row, count, stride=nocc), :]
                out_ref[slots[orbital], :, column : column + LANES] = tile.astype(jnp.bfloat16)


def transform(ints, occ_coef, vir_coef, slots, chunk=4):
    count, rows, width = ints.shape
    nocc, nvir = occ_coef.shape[1], vir_coef.shape[1]
    return pl.pallas_call(
        lambda *refs: transform_kernel(slots, *refs),
        grid=(count // chunk,),
        in_specs=[
            pl.BlockSpec((chunk, rows, width), lambda s: (s, 0, 0)),
            pl.BlockSpec((width, nocc), lambda s: (0, 0)),
            pl.BlockSpec((rows, nvir), lambda s: (0, 0)),
        ],
        out_specs=pl.BlockSpec((nocc, count, nvir), lambda s: (0, 0, 0)),
        out_shape=jax.ShapeDtypeStruct((nocc, count, nvir), jnp.bfloat16),
        scratch_shapes=[pltpu.VMEM((count * nocc * nvir // LANES, LANES), jnp.float32)],
        compiler_params=pltpu.CompilerParams(vmem_limit_bytes=VMEM_LIMIT),
        name="transform",
    )(ints, occ_coef, vir_coef)


def combine_kernel(in_ref, own_ref, turned_ref):
    tiles = in_ref[...].astype(jnp.float32)
    total = tiles[:, 0] + tiles[:, 1]
    total = total.reshape(own_ref.shape)
    own_ref[...] = total.astype(jnp.bfloat16)
    turned_ref[...] = total.T.astype(jnp.bfloat16)


def combine(arrived, chunk=16):
    owners, halves, count, nvir = arrived.shape
    naux = owners * count
    return pl.pallas_call(
        combine_kernel,
        grid=(owners // chunk,),
        in_specs=[pl.BlockSpec((chunk, halves, count, nvir), lambda s: (s, 0, 0, 0))],
        out_specs=[
            pl.BlockSpec((chunk * count, nvir), lambda s: (s, 0)),
            pl.BlockSpec((nvir, chunk * count), lambda s: (0, s)),
        ],
        out_shape=[
            jax.ShapeDtypeStruct((naux, nvir), jnp.bfloat16),
            jax.ShapeDtypeStruct((nvir, naux), jnp.bfloat16),
        ],
        compiler_params=pltpu.CompilerParams(vmem_limit_bytes=VMEM_LIMIT),
        name="combine",
    )(arrived)


def pair_kernel(visitors, energy_ref, column_ref, row_ref, turned_ref, *refs):
    visitor_refs, rest = refs[:visitors], refs[visitors:]
    out_ref = rest[-1]
    vir_pairs = column_ref[...] + row_ref[...]
    total = rest[0][...] if len(rest) > 1 else None
    for k in range(visitors):
        integrals = jnp.dot(
            turned_ref[...], visitor_refs[k][...], preferred_element_type=jnp.float32
        )
        scaled = integrals / (energy_ref[k] - vir_pairs)
        amplitude = scaled.astype(jnp.bfloat16)
        mixed = (2.0 * scaled.T - scaled).astype(jnp.bfloat16)
        term = jnp.dot(amplitude, mixed, preferred_element_type=jnp.float32)
        total = term if total is None else total + term
    out_ref[...] = total


def add_pairs(density, turned, visitors, energies, column, row):
    nvir = turned.shape[0]
    whole = pl.BlockSpec(memory_space=pltpu.VMEM)
    operands = [energies, column, row, turned, *visitors]
    specs = [pl.BlockSpec(memory_space=pltpu.SMEM)] + [whole] * (len(operands) - 1)
    aliases = {}
    if density is not None:
        aliases = {len(operands): 0}
        operands.append(density)
        specs.append(whole)
    return pl.pallas_call(
        lambda *refs: pair_kernel(len(visitors), *refs),
        in_specs=specs,
        out_specs=whole,
        out_shape=jax.ShapeDtypeStruct((nvir, nvir), jnp.float32),
        input_output_aliases=aliases,
        compiler_params=pltpu.CompilerParams(vmem_limit_bytes=VMEM_LIMIT),
        name="pairs",
    )(*operands)


def shards(ints, occ_coef, vir_coef, occ_energy, vir_energy):
    aux_count, ao_count = lax.axis_size("aux"), lax.axis_size("ao")
    block, side = lax.axis_index("aux"), lax.axis_index("ao")
    parity = side ^ flipped(block)
    nvir = vir_coef.shape[1]

    slots = [0] * (aux_count * ao_count)
    for b in range(aux_count):
        for s in range(ao_count):
            slots[b * ao_count + (s ^ flipped(b))] = b * ao_count + s
    tiles = transform(ints, occ_coef, vir_coef, slots)
    arrived = lax.all_to_all(tiles, BOTH, split_axis=0, concat_axis=0, tiled=True)
    own, turned = combine(arrived.reshape(aux_count, ao_count, *arrived.shape[1:]))

    def shifted(value, distance):
        route = []
        for b in range(aux_count):
            source = (b - distance) % aux_count
            for s in range(ao_count):
                p = s ^ flipped(b)
                route.append((source * ao_count + (p ^ flipped(source)), b * ao_count + s))
        return lax.ppermute(value, BOTH, route)

    swap = [(0, 1), (1, 0)]
    below, above = shifted(own, 1), shifted(own, -1)
    turned_other = lax.ppermute(turned, "ao", swap)

    column, row = vir_energy[:, None], vir_energy[None, :]

    def occupied(b, p):
        return occ_energy[((b + aux_count) % aux_count) * ao_count + p]

    e_own, e_other = occupied(block, parity), occupied(block, 1 - parity)

    def energies(first, distances):
        return jnp.stack([first + occupied(block + d, parity) for d in distances])

    dens = add_pairs(None, turned, [own], energies(e_own, [0]), column, row)
    dens_other = None
    visitors, distances = [own], [0]
    for offset in range(1, CYCLE + 1):
        if offset > 1:
            visitors, distances = [], []
        pair, gaps = [below, above], [-offset, offset]
        if offset < CYCLE:
            below, above = shifted(below, 1), shifted(above, -1)
        dens = add_pairs(dens, turned, pair, energies(e_own, gaps), column, row)
        dens_other = add_pairs(
            dens_other,
            turned_other,
            visitors + pair,
            energies(e_other, distances + gaps),
            column,
            row,
        )

    half = nvir // ao_count

    def exchanged(kept, sent):
        sent = lax.dynamic_slice_in_dim(sent, (1 - side) * half, half).astype(jnp.bfloat16)
        kept = lax.dynamic_slice_in_dim(kept, side * half, half)
        return kept + lax.ppermute(sent, "ao", swap).astype(jnp.float32)

    results = [exchanged(dens, dens_other), exchanged(dens_other, dens)]
    low = jnp.where(parity == 0, results[0], results[1])
    high = jnp.where(parity == 0, results[1], results[0])
    return jnp.stack([low, high])


def solution(mesh):
    return jax.shard_map(
        shards,
        mesh=mesh,
        in_specs=(P("aux", "ao", None), P(), P("ao", None), P(), P()),
        out_specs=P("aux", "ao", None),
        check_vma=False,
    )
```

time: 229 us -> 208 us (0.908)
  matrix products: 74.7 us -> 0 us
  Pallas kernels: 0 us -> 64.8 us
  blocking collectives: 70.3 us -> 41.2 us
  between operations: 0.39 us -> 22.4 us
  local copies, waits for them, and re-layouts: 24.2 us -> 4.76 us
  waiting for transfers between devices: 22.8 us -> 41.6 us
    dot_general x19 -> x0, matrix products: 74.7 us -> none  [the longest x9 40.2 us: add_pairs(): jnp.einsum('ijac,ijbc->iab', amplitude, mixed, preferred_element_type=jnp...]
    pallas_call x0 -> x11, Pallas kernels: none -> 64.8 us  [the longest x9 49.3 us: add_pairs(): pl.pallas_call(lambda *refs: pair_kernel(len(visitors), *refs), in_specs=...]
    ppermute x8 -> x11, waiting for transfers between devices: 0.12 us -> 41.6 us  [the longest x8 37.2 us: shifted(): return lax.ppermute(value, BOTH, route)]
    all_to_all x3 -> x1, blocking collectives: 70.3 us -> 41.2 us  [shards(): lax.all_to_all(tiles, BOTH, split_axis=0, concat_axis=0, tiled=True)]
    all_to_all x1 -> x0, waiting for transfers between devices: 22.7 us -> none  [from_everyone(): return lax.all_to_all(copies, axis, split_axis=0, concat_axis=0, tiled=True)]
    div x9 -> x0, local copies, waits for them, and re-layouts: 19.7 us -> none  [add_pairs(): scaled = integrals / energy_gap]
    add x3 -> x0, other arithmetic: 7.23 us -> none  [the longest x2 6.12 us: add_pairs(): own_energy[:, None, None, None] + pair_energy[None, :, None, None]]
    another operation x0 -> x10, other arithmetic: none -> 7.17 us  [the longest x8 4.92 us: energies(): return jnp.stack([first + occupied(block + d, parity) for d in distances])]
  transfers between devices with their start and end apart: 9 -> 11, of which waited for: 2 -> 4; matrix products, arithmetic and copies ran while one was open for 35% -> 4% of each run, Pallas kernels for 0% -> 21%
where the time goes in v1:
time: 208 us; the launch traced here: 207 us
  Pallas kernels  64.8 us (31%)
  waiting for transfers between devices  41.6 us (20%)
  blocking collectives  41.2 us (20%)
  starting transfers between devices  25.4 us (12%)
  between operations  22.4 us (11%)
  other arithmetic  7.17 us (3%)
  local copies, waits for them, and re-layouts  4.76 us (2%)
    pallas_call x9, Pallas kernels, add_pairs(): pl.pallas_call(lambda *refs: pair_kernel(len(visitors), *refs), in_specs=...  49.3 us
    all_to_all x1, blocking collectives, shards(): lax.all_to_all(tiles, BOTH, split_axis=0, concat_axis=0, tiled=True)  41.2 us
    ppermute x8, waiting for transfers between devices, shifted(): return lax.ppermute(value, BOTH, route)  37.2 us
    ppermute x8, starting transfers between devices, shifted(): return lax.ppermute(value, BOTH, route)  23.2 us
    pallas_call x1, Pallas kernels, transform(): pl.pallas_call(lambda *refs: transform_kernel(slots, *refs), grid=(count...  11.5 us
    another operation x8, other arithmetic, energies(): return jnp.stack([first + occupied(block + d, parity) for d in distances])  4.92 us
    ppermute x2, waiting for transfers between devices, exchanged(): return kept + lax.ppermute(sent, 'ao', swap).astype(jnp.float32)  4.43 us
  transfers between devices with their start and end apart: 11, of which 4 were waited for; matrix products, arithmetic and copies ran while one was open for 4% of the time, Pallas kernels for 21%

profile of v1, /device:TPU:0, one launch (start us, length us, event | category | flops | bytes accessed | tf_op | source)
XLA Modules:
  0.0 207.4 jit_solution(2527705451910429112)
XLA Ops:
  0.0 11.5 %transform.1 = bf16[128,16,512]{2,1,0:T(8,128)(2,1)} custom-call(bf16[16,384,768]{2,1,0:T(8,128)(2,1)} %refs_0_.1, bf16[768,128]{1,0:T(8,128)(2,1)} %refs_1_.1, bf16[384,512]{1,0:T(8,128)(2,1)} %refs_2_.1), custom_call_target="tpu_custom_call" | custom-call | tf_op jit(solution)/shard_map/transform/pallas_call | solution.py:50
  11.5 41.2 %all_to_all.5 = bf16[128,16,512]{2,1,0:T(8,128)(2,1)} all-to-all(bf16[128,16,512]{2,1,0:T(8,128)(2,1)} %transform.1), channel_id=1, replica_groups=mesh['aux'=64,'ao'=2] {'aux','ao'}, dimensions={0} | all-to-all | bytes 4194304 | tf_op jit(solution)/shard_map/all_to_all | solution.py:143
  52.7 3.9 %combine.1 = (bf16[1024,512]{1,0:T(8,128)(2,1)}, bf16[512,1024]{1,0:T(8,128)(2,1)}) custom-call(bf16[64,2,16,512]{3,2,1,0:T(8,128)(2,1)} %bitcast.7), custom_call_target="tpu_custom_call" | custom-call | tf_op jit(solution)/shard_map/combine/pallas_call | solution.py:77
  56.6 1.2 collective-permute-start.4
  57.9 0.0 collective-permute-start
  57.9 12.6 %collective-permute-done.4.refs_5_.refs_6_ = bf16[1024,512]{1,0:T(8,128)(2,1)S(1)} collective-permute-done((bf16[1024,512]{1,0:T(8,128)(2,1)}, bf16[1024,512]{1,0:T(8,128)(2,1)S(1)}, u32[]{:S(2)}, u32[]{:S(2)}) %collective-permute-start.4) | collective-permute-done | bytes 1048608 | tf_op jit(solution)/shard_map/ppermute | solution.py:153
  70.5 7.2 %collective-permute-start.5 = (bf16[1024,512]{1,0:T(8,128)(2,1)S(1)}, bf16[1024,512]{1,0:T(8,128)(2,1)S(1)}, u32[]{:S(2)}, u32[]{:S(2)}) collective-permute-start(bf16[1024,512]{1,0:T(8,128)(2,1)S(1)} %collective-permute-done.4.refs_5_.refs_6_), channel_id=1, source_target_pairs={{2,0},{3,1},{4,2},{5,3},{6,4},{7,5},{8,6},{9,7},{10,8},{11,9},{12,... | collective-permute-start | bytes 3145736 | tf_op jit(solution)/shard_map/ppermute | solution.py:153
  77.7 0.0 collective-permute-done.refs_4_.refs_5_
  77.7 0.0 collective-permute-start.1
  77.7 12.3 %collective-permute-done.5.refs_5_ = bf16[1024,512]{1,0:T(8,128)(2,1)S(1)} collective-permute-done((bf16[1024,512]{1,0:T(8,128)(2,1)S(1)}, bf16[1024,512]{1,0:T(8,128)(2,1)S(1)}, u32[]{:S(2)}, u32[]{:S(2)}) %collective-permute-start.5) | collective-permute-done | bytes 1048608 | tf_op jit(solution)/shard_map/ppermute | solution.py:153
  90.1 7.3 %collective-permute-start.6 = (bf16[1024,512]{1,0:T(8,128)(2,1)S(1)}, bf16[1024,512]{1,0:T(8,128)(2,1)}, u32[]{:S(2)}, u32[]{:S(2)}) collective-permute-start(bf16[1024,512]{1,0:T(8,128)(2,1)S(1)} %collective-permute-done.5.refs_5_), channel_id=1, source_target_pairs={{2,0},{3,1},{4,2},{5,3},{6,4},{7,5},{8,6},{9,7},{10,8},{11,9},{12,... | collective-permute-start | bytes 3145736 | tf_op jit(solution)/shard_map/ppermute | solution.py:153
  97.4 0.0 collective-permute-done.1.refs_4_
  97.4 0.0 collective-permute-start.2
  97.4 0.1 collective-permute-start.8
  97.5 12.2 %collective-permute-done.6.refs_5_ = bf16[1024,512]{1,0:T(8,128)(2,1)} collective-permute-done((bf16[1024,512]{1,0:T(8,128)(2,1)S(1)}, bf16[1024,512]{1,0:T(8,128)(2,1)}, u32[]{:S(2)}, u32[]{:S(2)}) %collective-permute-start.6) | collective-permute-done | bytes 1048608 | tf_op jit(solution)/shard_map/ppermute | solution.py:153
  109.7 7.4 %collective-permute-start.7 = (bf16[1024,512]{1,0:T(8,128)(2,1)}, bf16[1024,512]{1,0:T(8,128)(2,1)}, u32[]{:S(2)}, u32[]{:S(2)}) collective-permute-start(bf16[1024,512]{1,0:T(8,128)(2,1)} %collective-permute-done.6.refs_5_), channel_id=1, source_target_pairs={{2,0},{3,1},{4,2},{5,3},{6,4},{7,5},{8,6},{9,7},{10,8},{11,9},{12,... | collective-permute-start | bytes 3145736 | tf_op jit(solution)/shard_map/ppermute | solution.py:153
  117.2 0.0 collective-permute-done.2.refs_4_
  117.2 0.0 collective-permute-start.3
  117.2 0.7 fusion
  140.2 0.9 copy.17.refs_1_
  141.1 0.7 pad_maximum_fusion.1.refs_0_
  141.8 0.6 pad_maximum_fusion.2.refs_0_
  142.4 0.6 pad_maximum_fusion.3.refs_0_
  143.0 0.6 pad_maximum_fusion.4.refs_0_
  143.6 0.6 pad_maximum_fusion.7.refs_0_
  144.2 0.6 pad_maximum_fusion.6.refs_0_
  144.8 0.6 pad_maximum_fusion.5.refs_0_
  145.4 0.6 pad_maximum_fusion.8.refs_0_
  146.1 3.9 %pairs.9.refs_6_ = f32[512,512]{1,0:T(8,128)} custom-call(f32[1]{0:T(128)S(6)} %add.324.refs_0_, f32[512,1]{1,0:T(8,128)} %copy.17.refs_1_, f32[1,512]{1,0:T(1,128)} %bitcast.8, bf16[512,1024]{1,0:T(8,128)(2,1)} %get-tuple-element.7.refs_3_, bf16[1024,512]{1,0:T(8,128)(2,1)} %get-tuple-element.8.refs_4_), custom_call_target="tpu_custom_call" | custom-call | tf_op jit(solution)/shard_map/pairs/pallas_call | solution.py:121
  149.9 5.6 %pairs.10.refs_6_ = f32[512,512]{1,0:T(8,128)} custom-call(f32[2]{0:T(128)} %pad_maximum_fusion.4.refs_0_, f32[512,1]{1,0:T(8,128)} %copy.17.refs_1_, f32[1,512]{1,0:T(1,128)} %bitcast.9, bf16[512,1024]{1,0:T(8,128)(2,1)} %get-tuple-element.7.refs_3_, bf16[1024,512]{1,0:T(8,128)(2,1)} %copy-done.3, ...), custom_call_target="tpu_custom_call", output_to_operand_aliasing={{}: (6, {})} | custom-call | tf_op jit(solution)/shard_map/pairs/pallas_call | solution.py:121
  155.5 0.0 collective-permute-done.8.refs_3_
  155.5 1.0 copy-done.1
  156.5 6.4 %pairs.14.refs_6_ = f32[512,512]{1,0:T(8,128)} custom-call(f32[3]{0:T(128)} %pad_maximum_fusion.8.refs_0_, f32[512,1]{1,0:T(8,128)} %copy.17.refs_1_, f32[1,512]{1,0:T(1,128)} %bitcast.10, bf16[512,1024]{1,0:T(8,128)(2,1)} %copy-done.1, bf16[1024,512]{1,0:T(8,128)(2,1)} %get-tuple-element.8.refs_4_, bf16[1024,512]{1,0:T(8,128)(2,1)} %copy-done.3, ...), custom_call_target="tpu_custom_call" | custom-call | tf_op jit(solution)/shard_map/pairs/pallas_call | solution.py:121
  162.9 5.5 %pairs.11.refs_6_ = f32[512,512]{1,0:T(8,128)} custom-call(f32[2]{0:T(128)} %pad_maximum_fusion.3.refs_0_, f32[512,1]{1,0:T(8,128)} %copy.17.refs_1_, f32[1,512]{1,0:T(1,128)} %bitcast.11, bf16[512,1024]{1,0:T(8,128)(2,1)} %get-tuple-element.7.refs_3_, bf16[1024,512]{1,0:T(8,128)(2,1)} %copy-done.5, ...), custom_call_target="tpu_custom_call", output_to_operand_aliasing={{}: (6, {})} | custom-call | tf_op jit(solution)/shard_map/pairs/pallas_call | solution.py:121
  168.4 5.5 %pairs.15.refs_6_ = f32[512,512]{1,0:T(8,128)} custom-call(f32[2]{0:T(128)} %pad_maximum_fusion.7.refs_0_, f32[512,1]{1,0:T(8,128)} %copy.17.refs_1_, f32[1,512]{1,0:T(1,128)} %bitcast.12, bf16[512,1024]{1,0:T(8,128)(2,1)} %copy-done.1, bf16[1024,512]{1,0:T(8,128)(2,1)} %copy-done.5, bf16[1024,512]{1,0:T(8,128)(2,1)} %copy-done.4, ...), custom_call_target="tpu_custom_call", output_to_operand_aliasing={{}: (6, {})} | custom-call | tf_op jit(solution)/shard_map/pairs/pallas_call | solution.py:121
  174.0 5.5 %pairs.12.refs_6_ = f32[512,512]{1,0:T(8,128)} custom-call(f32[2]{0:T(128)} %pad_maximum_fusion.2.refs_0_, f32[512,1]{1,0:T(8,128)} %copy.17.refs_1_, f32[1,512]{1,0:T(1,128)} %bitcast.13, bf16[512,1024]{1,0:T(8,128)(2,1)} %get-tuple-element.7.refs_3_, bf16[1024,512]{1,0:T(8,128)(2,1)} %collective-permute-done.2.refs_4_, ...), custom_call_target="tpu_custom_call", output_to_operand_aliasing={{}: (6, {})} | custom-call | tf_op jit(solution)/shard_map/pairs/pallas_call | solution.py:121
  179.5 5.7 %pairs.16.refs_6_ = f32[512,512]{1,0:T(8,128)} custom-call(f32[2]{0:T(128)} %pad_maximum_fusion.6.refs_0_, f32[512,1]{1,0:T(8,128)} %copy.17.refs_1_, f32[1,512]{1,0:T(1,128)} %bitcast.14, bf16[512,1024]{1,0:T(8,128)(2,1)} %copy-done.1, bf16[1024,512]{1,0:T(8,128)(2,1)} %collective-permute-done.2.refs_4_, ...), custom_call_target="tpu_custom_call", output_to_operand_aliasing={{}: (6, {})} | custom-call | tf_op jit(solution)/shard_map/pairs/pallas_call | solution.py:121
  185.3 0.0 collective-permute-done.7.refs_5_
  185.3 5.6 %pairs.13 = f32[512,512]{1,0:T(8,128)} custom-call(f32[2]{0:T(128)} %pad_maximum_fusion.1.refs_0_, f32[512,1]{1,0:T(8,128)} %copy.17.refs_1_, f32[1,512]{1,0:T(1,128)} %bitcast.15, bf16[512,1024]{1,0:T(8,128)(2,1)} %get-tuple-element.7.refs_3_, bf16[1024,512]{1,0:T(8,128)(2,1)} %collective-permute-done.3.refs_4_, ...), custom_call_target="tpu_custom_call", output_to_operand_aliasing={{}: (6, {})} | custom-call | tf_op jit(solution)/shard_map/pairs/pallas_call | solution.py:121
  190.8 1.1 dynamic-slice_convert_fusion
  191.9 0.1 collective-permute-start.10
  192.0 5.6 %pairs.17 = f32[512,512]{1,0:T(8,128)} custom-call(f32[2]{0:T(128)} %pad_maximum_fusion.5.refs_0_, f32[512,1]{1,0:T(8,128)} %copy.17.refs_1_, f32[1,512]{1,0:T(1,128)} %bitcast.16, bf16[512,1024]{1,0:T(8,128)(2,1)} %copy-done.1, bf16[1024,512]{1,0:T(8,128)(2,1)} %collective-permute-done.3.refs_4_, ...), custom_call_target="tpu_custom_call", output_to_operand_aliasing={{}: (6, {})} | custom-call | tf_op jit(solution)/shard_map/pairs/pallas_call | solution.py:121
  197.6 1.1 dynamic-slice_convert_fusion.1
  198.7 2.0 collective-permute-start.9
  200.7 0.0 collective-permute-done.10
  200.7 4.4 %collective-permute-done.9 = bf16[256,512]{1,0:T(8,128)(2,1)S(1)} collective-permute-done((bf16[256,512]{1,0:T(8,128)(2,1)S(1)}, bf16[256,512]{1,0:T(8,128)(2,1)S(1)}, u32[]{:S(2)}, u32[]{:S(2)}) %collective-permute-start.9) | collective-permute-done | bytes 262176 | tf_op jit(solution)/shard_map/ppermute | solution.py:193
  205.1 1.2 select_bitcast_fusion.1
  206.3 1.0 pad_maximum_fusion
  (16 shorter events, 0.0 us)
Async XLA Ops:
  52.7 64.5 %copy-start.7 = (f32[128]{0:T(128)S(1)}, f32[128]{0:T(128)}, u32[]{:S(2)}) copy-start(f32[128]{0:T(128)} %param.8) | copy-start | bytes 1540
  52.7 87.5 %copy-start.6 = (f32[512]{0:T(512)S(1)}, f32[512]{0:T(512)}, u32[]{:S(2)}) copy-start(f32[512]{0:T(512)} %param.9) | copy-start | bytes 6148
  56.6 13.9 %collective-permute-start.4 = (bf16[1024,512]{1,0:T(8,128)(2,1)}, bf16[1024,512]{1,0:T(8,128)(2,1)S(1)}, u32[]{:S(2)}, u32[]{:S(2)}) collective-permute-start(bf16[1024,512]{1,0:T(8,128)(2,1)} %get-tuple-element.8.refs_4_), channel_id=1, source_target_pairs={{2,0},{3,1},{4,2},{5,3},{6,4},{7,5},{8,6},{9,7},{10,8},{11,9},{12,... | collective-permute-start | bytes 3145736 | tf_op jit(solution)/shard_map/ppermute | solution.py:153
  57.9 19.9 %collective-permute-start = (bf16[1024,512]{1,0:T(8,128)(2,1)}, bf16[1024,512]{1,0:T(8,128)(2,1)S(1)}, u32[]{:S(2)}, u32[]{:S(2)}) collective-permute-start(bf16[1024,512]{1,0:T(8,128)(2,1)} %get-tuple-element.8.refs_4_), channel_id=1, source_target_pairs={{127,0},{126,1},{0,2},{1,3},{2,4},{3,5},{4,6},{5,7},{6,8},{7,9},{8... | collective-permute-start | bytes 3145736 | tf_op jit(solution)/shard_map/ppermute | solution.py:153
  70.5 79.4 %copy-start.2 = (bf16[1024,512]{1,0:T(8,128)(2,1)}, bf16[1024,512]{1,0:T(8,128)(2,1)S(1)}, u32[]{:S(2)}) copy-start(bf16[1024,512]{1,0:T(8,128)(2,1)S(1)} %collective-permute-done.4.refs_5_.refs_6_) | copy-start | bytes 3145732
  70.5 19.5 %collective-permute-start.5 = (bf16[1024,512]{1,0:T(8,128)(2,1)S(1)}, bf16[1024,512]{1,0:T(8,128)(2,1)S(1)}, u32[]{:S(2)}, u32[]{:S(2)}) collective-permute-start(bf16[1024,512]{1,0:T(8,128)(2,1)S(1)} %collective-permute-done.4.refs_5_.refs_6_), channel_id=1, source_target_pairs={{2,0},{3,1},{4,2},{5,3},{6,4},{7,5},{8,6},{9,7},{10,8},{11,9},{12,... | collective-permute-start | bytes 3145736 | tf_op jit(solution)/shard_map/ppermute | solution.py:153
  77.7 72.2 %copy-start.3 = (bf16[1024,512]{1,0:T(8,128)(2,1)}, bf16[1024,512]{1,0:T(8,128)(2,1)S(1)}, u32[]{:S(2)}) copy-start(bf16[1024,512]{1,0:T(8,128)(2,1)S(1)} %collective-permute-done.refs_4_.refs_5_) | copy-start | bytes 3145732
  77.7 19.7 %collective-permute-start.1 = (bf16[1024,512]{1,0:T(8,128)(2,1)S(1)}, bf16[1024,512]{1,0:T(8,128)(2,1)S(1)}, u32[]{:S(2)}, u32[]{:S(2)}) collective-permute-start(bf16[1024,512]{1,0:T(8,128)(2,1)S(1)} %collective-permute-done.refs_4_.refs_5_), channel_id=1, source_target_pairs={{127,0},{126,1},{0,2},{1,3},{2,4},{3,5},{4,6},{5,7},{6,8},{7,9},{8... | collective-permute-start | bytes 3145736 | tf_op jit(solution)/shard_map/ppermute | solution.py:153
  90.1 7.4 %copy-start.4 = (bf16[1024,512]{1,0:T(8,128)(2,1)}, bf16[1024,512]{1,0:T(8,128)(2,1)S(1)}, u32[]{:S(2)}) copy-start(bf16[1024,512]{1,0:T(8,128)(2,1)S(1)} %collective-permute-done.5.refs_5_) | copy-start | bytes 3145732
  90.1 19.7 %collective-permute-start.6 = (bf16[1024,512]{1,0:T(8,128)(2,1)S(1)}, bf16[1024,512]{1,0:T(8,128)(2,1)}, u32[]{:S(2)}, u32[]{:S(2)}) collective-permute-start(bf16[1024,512]{1,0:T(8,128)(2,1)S(1)} %collective-permute-done.5.refs_5_), channel_id=1, source_target_pairs={{2,0},{3,1},{4,2},{5,3},{6,4},{7,5},{8,6},{9,7},{10,8},{11,9},{12,... | collective-permute-start | bytes 3145736 | tf_op jit(solution)/shard_map/ppermute | solution.py:153
  97.4 12.3 %copy-start.5 = (bf16[1024,512]{1,0:T(8,128)(2,1)}, bf16[1024,512]{1,0:T(8,128)(2,1)S(1)}, u32[]{:S(2)}) copy-start(bf16[1024,512]{1,0:T(8,128)(2,1)S(1)} %collective-permute-done.1.refs_4_) | copy-start | bytes 3145732
  97.4 19.8 %collective-permute-start.2 = (bf16[1024,512]{1,0:T(8,128)(2,1)S(1)}, bf16[1024,512]{1,0:T(8,128)(2,1)}, u32[]{:S(2)}, u32[]{:S(2)}) collective-permute-start(bf16[1024,512]{1,0:T(8,128)(2,1)S(1)} %collective-permute-done.1.refs_4_), channel_id=1, source_target_pairs={{127,0},{126,1},{0,2},{1,3},{2,4},{3,5},{4,6},{5,7},{6,8},{7,9},{8... | collective-permute-start | bytes 3145736 | tf_op jit(solution)/shard_map/ppermute | solution.py:153
  97.4 58.1 %collective-permute-start.8 = (bf16[512,1024]{1,0:T(8,128)(2,1)}, bf16[512,1024]{1,0:T(8,128)(2,1)S(1)}, u32[]{:S(2)}, u32[]{:S(2)}) collective-permute-start(bf16[512,1024]{1,0:T(8,128)(2,1)} %get-tuple-element.7.refs_3_), channel_id=1, source_target_pairs={{0,1},{1,0},{2,3},{3,2},{4,5},{5,4},{6,7},{7,6},{8,9},{9,8},{10,11... | collective-permute-start | bytes 3145736 | tf_op jit(solution)/shard_map/ppermute | solution.py:157
  109.7 75.5 %collective-permute-start.7 = (bf16[1024,512]{1,0:T(8,128)(2,1)}, bf16[1024,512]{1,0:T(8,128)(2,1)}, u32[]{:S(2)}, u32[]{:S(2)}) collective-permute-start(bf16[1024,512]{1,0:T(8,128)(2,1)} %collective-permute-done.6.refs_5_), channel_id=1, source_target_pairs={{2,0},{3,1},{4,2},{5,3},{6,4},{7,5},{8,6},{9,7},{10,8},{11,9},{12,... | collective-permute-start | bytes 3145736 | tf_op jit(solution)/shard_map/ppermute | solution.py:153
  117.2 68.1 %collective-permute-start.3 = (bf16[1024,512]{1,0:T(8,128)(2,1)}, bf16[1024,512]{1,0:T(8,128)(2,1)}, u32[]{:S(2)}, u32[]{:S(2)}) collective-permute-start(bf16[1024,512]{1,0:T(8,128)(2,1)} %collective-permute-done.2.refs_4_), channel_id=1, source_target_pairs={{127,0},{126,1},{0,2},{1,3},{2,4},{3,5},{4,6},{5,7},{6,8},{7,9},{8... | collective-permute-start | bytes 3145736 | tf_op jit(solution)/shard_map/ppermute | solution.py:153
  155.5 1.0 copy-start.1
  191.9 13.2 %copy-start = (f32[512,512]{1,0:T(8,128)S(1)}, f32[512,512]{1,0:T(8,128)}, u32[]{:S(2)}) copy-start(f32[512,512]{1,0:T(8,128)} %pairs.13) | copy-start | bytes 3145732
  191.9 8.8 %collective-permute-start.10 = (bf16[256,512]{1,0:T(8,128)(2,1)S(1)}, bf16[256,512]{1,0:T(8,128)(2,1)S(1)}, u32[]{:S(2)}, u32[]{:S(2)}) collective-permute-start(bf16[256,512]{1,0:T(8,128)(2,1)S(1)} %dynamic-slice_convert_fusion), channel_id=1, source_target_pairs={{0,1},{1,0},{2,3},{3,2},{4,5},{5,4},{6,7},{7,6},{8,9},{9,8},{10,11... | collective-permute-start | bytes 786440 | tf_op jit(solution)/shard_map/ppermute | solution.py:193
  198.7 6.5 %collective-permute-start.9 = (bf16[256,512]{1,0:T(8,128)(2,1)S(1)}, bf16[256,512]{1,0:T(8,128)(2,1)S(1)}, u32[]{:S(2)}, u32[]{:S(2)}) collective-permute-start(bf16[256,512]{1,0:T(8,128)(2,1)S(1)} %dynamic-slice_convert_fusion.1), channel_id=1, source_target_pairs={{0,1},{1,0},{2,3},{3,2},{4,5},{5,4},{6,7},{7,6},{8,9},{9,8},{10,11... | collective-permute-start | bytes 786440 | tf_op jit(solution)/shard_map/ppermute | solution.py:193

commit v2 on v1

v2 whole, which is shorter than its diff:
```python
import jax
import jax.numpy as jnp
from jax import lax
from jax.experimental import pallas as pl
from jax.experimental.pallas import tpu as pltpu
from jax.sharding import PartitionSpec as P

ROW = 8
LANES = 128
BOTH = ("aux", "ao")
MIB = 1024 * 1024
SWAP = [(0, 1), (1, 0)]


def flipped(block):
    return (block // ROW) % 2


def params(mib):
    return pltpu.CompilerParams(vmem_limit_bytes=mib * MIB)


def transform_kernel(slots, ints_ref, occ_ref, vir_ref, out_ref, held_ref):
    step = pl.program_id(0)
    chunk, rows, width = ints_ref.shape
    nocc, nvir = occ_ref.shape[1], vir_ref.shape[1]
    count = out_ref.shape[1]
    stride = nocc + 8
    slab = ints_ref[...].reshape(chunk * rows, width)
    half = jnp.dot(slab, occ_ref[...], preferred_element_type=jnp.float32)
    turned = [half[k * rows : (k + 1) * rows].T.astype(jnp.bfloat16) for k in range(chunk)]
    part = jnp.dot(
        jnp.concatenate(turned, axis=0), vir_ref[...], preferred_element_type=jnp.float32
    )
    for k in range(chunk):
        for column in range(nvir // LANES):
            start = pl.multiple_of((column * count + step * chunk + k) * stride, 8)
            held_ref[pl.ds(start, nocc), :] = part[
                k * nocc : (k + 1) * nocc, column * LANES : (column + 1) * LANES
            ]

    @pl.when(step == pl.num_programs(0) - 1)
    def _():
        for orbital in range(nocc):
            for column in range(nvir // LANES):
                tile = held_ref[pl.ds(column * count * stride + orbital, count, stride=stride), :]
                out_ref[slots[orbital], :, column * LANES : (column + 1) * LANES] = tile.astype(
                    jnp.bfloat16
                )


def transform(ints, occ_coef, vir_coef, slots, chunk=4):
    count, rows, width = ints.shape
    nocc, nvir = occ_coef.shape[1], vir_coef.shape[1]
    return pl.pallas_call(
        lambda *refs: transform_kernel(slots, *refs),
        grid=(count // chunk,),
        in_specs=[
            pl.BlockSpec((chunk, rows, width), lambda s: (s, 0, 0)),
            pl.BlockSpec((width, nocc), lambda s: (0, 0)),
            pl.BlockSpec((rows, nvir), lambda s: (0, 0)),
        ],
        out_specs=pl.BlockSpec((nocc, count, nvir), lambda s: (0, 0, 0)),
        out_shape=jax.ShapeDtypeStruct((nocc, count, nvir), jnp.bfloat16),
        scratch_shapes=[pltpu.VMEM((count * (nocc + 8) * nvir // LANES, LANES), jnp.float32)],
        compiler_params=params(56),
        name="transform",
    )(ints, occ_coef, vir_coef)


def combine_kernel(in_ref, energy_ref, own_ref, turned_ref, column_ref):
    tiles = in_ref[...].astype(jnp.float32)
    total = (tiles[:, 0] + tiles[:, 1]).reshape(own_ref.shape)
    own_ref[...] = total.astype(jnp.bfloat16)
    turned_ref[...] = total.T.astype(jnp.bfloat16)

    @pl.when(pl.program_id(0) == 0)
    def _():
        column_ref[...] = jnp.broadcast_to(energy_ref[...], (LANES, energy_ref.shape[1])).T


def combine(arrived, vir_energy, chunk=16):
    owners, halves, count, nvir = arrived.shape
    naux = owners * count
    return pl.pallas_call(
        combine_kernel,
        grid=(owners // chunk,),
        in_specs=[
            pl.BlockSpec((chunk, halves, count, nvir), lambda s: (s, 0, 0, 0)),
            pl.BlockSpec((1, nvir), lambda s: (0, 0)),
        ],
        out_specs=[
            pl.BlockSpec((chunk * count, nvir), lambda s: (s, 0)),
            pl.BlockSpec((nvir, chunk * count), lambda s: (0, s)),
            pl.BlockSpec((nvir, LANES), lambda s: (0, 0)),
        ],
        out_shape=[
            jax.ShapeDtypeStruct((naux, nvir), jnp.bfloat16),
            jax.ShapeDtypeStruct((nvir, naux), jnp.bfloat16),
            jax.ShapeDtypeStruct((nvir, LANES), jnp.float32),
        ],
        compiler_params=params(24),
        name="combine",
    )(arrived, vir_energy)


def pair_kernel(own_sides, distances, started, last, aux_count, *refs):
    refs = list(refs)
    energy_ref, column_ref, row_ref = refs[:3]
    turned_refs = refs[3 : 3 + len(own_sides)]
    visitor_refs = refs[3 + len(own_sides) :][: len(distances)]
    refs = refs[3 + len(own_sides) + len(distances) :]
    block, side = lax.axis_index("aux"), lax.axis_index("ao")
    parity = lax.rem(side + lax.rem(lax.div(block, ROW), 2), 2)
    odd = lax.rem(block, 2)
    nvir = row_ref.shape[1]
    column = column_ref[...]
    vir_pairs = jnp.concatenate([column] * (nvir // LANES), axis=1) + row_ref[...]
    for n, own_side in enumerate(own_sides):
        mine = parity if own_side == 0 else 1 - parity
        e_own = energy_ref[2 * block + mine]
        total = refs[n][...] if started else None
        for (even_distance, odd_distance), visitor_ref in zip(distances, visitor_refs):
            distance = even_distance + (odd_distance - even_distance) * odd
            visiting = lax.rem(block + distance + aux_count, aux_count)
            e_pair = e_own + energy_ref[2 * visiting + parity]
            integrals = jnp.dot(
                turned_refs[n][...], visitor_ref[...], preferred_element_type=jnp.float32
            )
            scaled = integrals / (e_pair - vir_pairs)
            amplitude = scaled.astype(jnp.bfloat16)
            mixed = (2.0 * scaled.T - scaled).astype(jnp.bfloat16)
            term = jnp.dot(amplitude, mixed, preferred_element_type=jnp.float32)
            total = term if total is None else total + term
        if not last:
            refs[len(own_sides) * started + n][...] = total
        else:
            kept_ref, sent_ref, held_ref = refs[1:]
            half = kept_ref.shape[0]
            held_ref[...] = total
            kept_ref[...] = held_ref[pl.ds(pl.multiple_of(side * half, half), half), :]
            sent_ref[...] = held_ref[
                pl.ds(pl.multiple_of((1 - side) * half, half), half), :
            ].astype(jnp.bfloat16)


def add_pairs(energies, turned, visitors, density, last=False):
    occ_energy, column, row = energies
    sides = sorted(turned)
    nvir, naux = turned[sides[0]].shape
    whole = pl.BlockSpec(memory_space=pltpu.VMEM)
    operands = [occ_energy, column, row]
    operands += [turned[s] for s in sides] + [v for _, v in visitors]
    specs = [pl.BlockSpec(memory_space=pltpu.SMEM)] + [whole] * (len(operands) - 1)
    started = density is not None
    aliases = {}
    square = jax.ShapeDtypeStruct((nvir, nvir), jnp.float32)
    if started:
        if not last:
            aliases = {len(operands) + n: n for n in range(len(sides))}
        operands += [density[s] for s in sides]
        specs += [whole] * len(sides)
    if last:
        out_shape = [
            jax.ShapeDtypeStruct((nvir // 2, nvir), jnp.float32),
            jax.ShapeDtypeStruct((nvir // 2, nvir), jnp.bfloat16),
        ]
        scratch = [pltpu.VMEM((nvir, nvir), jnp.float32)]
    else:
        out_shape = [square] * len(sides)
        scratch = []
    pairs = len(sides) * len(visitors)
    results = pl.pallas_call(
        lambda *refs: pair_kernel(
            sides, [d for d, _ in visitors], started, last, lax.axis_size("aux"), *refs
        ),
        in_specs=specs,
        out_specs=[whole] * len(out_shape),
        out_shape=out_shape,
        scratch_shapes=scratch,
        input_output_aliases=aliases,
        compiler_params=params(16),
        cost_estimate=pl.CostEstimate(
            flops=pairs * 2 * nvir * nvir * (naux + nvir),
            bytes_accessed=pairs * 2 * nvir * naux,
            transcendentals=0,
        ),
        name="pairs",
    )(*operands)
    return results if last else dict(zip(sides, results))


def finish_kernel(kept_own, came_own, kept_other, came_other, out_ref):
    block, side = lax.axis_index("aux"), lax.axis_index("ao")
    parity = lax.rem(side + lax.rem(lax.div(block, ROW), 2), 2)
    out_ref[parity] = kept_own[...] + came_own[...].astype(jnp.float32)
    out_ref[1 - parity] = kept_other[...] + came_other[...].astype(jnp.float32)


def finish(*operands):
    rows, nvir = operands[0].shape
    whole = pl.BlockSpec(memory_space=pltpu.VMEM)
    return pl.pallas_call(
        finish_kernel,
        in_specs=[whole] * 4,
        out_specs=whole,
        out_shape=jax.ShapeDtypeStruct((2, rows, nvir), jnp.float32),
        compiler_params=params(16),
        name="finish",
    )(*operands)


def shards(ints, occ_coef, vir_coef, occ_energy, vir_energy):
    aux_count, ao_count = lax.axis_size("aux"), lax.axis_size("ao")
    odd = lax.axis_index("aux") % 2

    def place(block, parity):
        return block * ao_count + (parity ^ flipped(block))

    every = [(b, p) for b in range(aux_count) for p in range(ao_count)]

    def shifted(value, distance):
        route = [(place((b - distance) % aux_count, p), place(b, p)) for b, p in every]
        return lax.ppermute(value, BOTH, route)

    def across(value):
        return lax.ppermute(value, "aux", [(b ^ 1, b) for b in range(aux_count)])

    def over(value):
        return lax.ppermute(value, "ao", SWAP)

    slots = [place(b, p) for b, p in every]
    tiles = transform(ints, occ_coef, vir_coef, slots)
    arrived = lax.all_to_all(tiles, BOTH, split_axis=0, concat_axis=0, tiled=True)
    row = vir_energy[None, :]
    own, turned, column = combine(arrived.reshape(aux_count, ao_count, *arrived.shape[1:]), row)
    energies = (occ_energy, column, row)

    hold = lax.optimization_barrier
    below, above = shifted(own, 2), shifted(own, -2)
    neighbour = across(own)
    turned_other = over(turned)
    first = [((0, 0), own), ((1, -1), neighbour)]
    density = add_pairs(energies, {0: turned}, first, None)
    turned_other, density = hold((turned_other, density))
    both = {0: turned, 1: turned_other}
    density |= add_pairs(energies, {1: turned_other}, first, None)
    below, above, density = hold((below, above, density))

    far_below, far_above = shifted(below, 2), shifted(above, -2)
    next_below, next_above = across(below), across(above)
    density = add_pairs(energies, both, [((-2, -2), below), ((2, 2), above)], density)
    next_below, next_above, density = hold((next_below, next_above, density))
    density = add_pairs(energies, both, [((-1, -3), next_below), ((3, 1), next_above)], density)
    far_below, far_above, density = hold((far_below, far_above, density))

    remaining = across(jnp.where(odd == 0, far_above, far_below))
    density = add_pairs(energies, both, [((-4, -4), far_below), ((4, 4), far_above)], density)
    remaining, density = hold((remaining, density))
    final = [((-3, 3), remaining)]
    kept_own, sent_own = add_pairs(energies, {0: turned}, final, {0: density[0]}, last=True)
    came_other = over(sent_own)
    kept_other, sent_other = add_pairs(
        energies, {1: turned_other}, final, {1: density[1]}, last=True
    )
    came_own = over(sent_other)
    return finish(kept_own, came_own, kept_other, came_other)


def solution(mesh):
    return jax.shard_map(
        shards,
        mesh=mesh,
        in_specs=(P("aux", "ao", None), P(), P("ao", None), P(), P()),
        out_specs=P("aux", "ao", None),
        check_vma=False,
    )
```

time: 208 us -> 141 us (0.68)
  Pallas kernels: 64.8 us -> 38.9 us
  between operations: 22.4 us -> 0.12 us
  starting transfers between devices: 25.4 us -> 18.9 us
  other arithmetic: 7.17 us -> 1.43 us
  waiting for transfers between devices: 41.6 us -> 36.6 us
    ppermute x8 -> x4, waiting for transfers between devices: 37.2 us -> 12 us  [shifted(): return lax.ppermute(value, BOTH, route)]
    pallas_call x9 -> x8, Pallas kernels: 49.3 us -> 27.6 us  [the longest x7 26.6 us: add_pairs(): pl.pallas_call(lambda *refs: pair_kernel(sides, [d for d, _ in visitors],...]
    ppermute x3 -> x7, waiting for transfers between devices: 4.43 us -> 24.6 us  [the longest x3 24.6 us: over(): return lax.ppermute(value, 'ao', SWAP)]
    ppermute x8 -> x4, starting transfers between devices: 23.2 us -> 14.9 us  [shifted(): return lax.ppermute(value, BOTH, route)]
    another operation x10 -> x0, other arithmetic: 7.17 us -> none  [the longest x8 4.92 us: energies(): return jnp.stack([first + occupied(block + d, parity) for d in distances])]
    pallas_call x1, Pallas kernels: 3.93 us -> 0.84 us  [combine(): pl.pallas_call(combine_kernel, grid=(owners // chunk,), in_specs=[pl.Bloc...]
    unnamed x16 -> x12, local copies, waits for them, and re-layouts: 1.02 us -> 3.17 us
    convert_element_type x2 -> x0, local copies, waits for them, and re-layouts: 2.15 us -> none  [exchanged(): lax.dynamic_slice_in_dim(sent, (1 - side) * half, half).astype(jnp.bfloat16)]
  transfers between devices with their start and end apart: 11 -> 11, of which waited for: 4 -> 5; matrix products, arithmetic and copies ran while one was open for 4% -> 0% of each run, Pallas kernels for 21% -> 18%
where the time goes in v2:
time: 141 us; the launch traced here: 140 us
  blocking collectives  41.1 us (29%)
  Pallas kernels  38.9 us (28%)
  waiting for transfers between devices  36.6 us (26%)
  starting transfers between devices  18.9 us (13%)
  local copies, waits for them, and re-layouts  3.17 us (2%)
  other arithmetic  1.43 us (1%)
    all_to_all x1, blocking collectives, shards(): lax.all_to_all(tiles, BOTH, split_axis=0, concat_axis=0, tiled=True)  41.1 us
    pallas_call x7, Pallas kernels, add_pairs(): pl.pallas_call(lambda *refs: pair_kernel(sides, [d for d, _ in visitors],...  26.6 us
    ppermute x3, waiting for transfers between devices, over(): return lax.ppermute(value, 'ao', SWAP)  24.6 us
    ppermute x4, starting transfers between devices, shifted(): return lax.ppermute(value, BOTH, route)  14.9 us
    ppermute x4, waiting for transfers between devices, shifted(): return lax.ppermute(value, BOTH, route)  12 us
    pallas_call x1, Pallas kernels, transform(): pl.pallas_call(lambda *refs: transform_kernel(slots, *refs), grid=(count...  10.5 us
    unnamed x12, local copies, waits for them, and re-layouts  3.17 us
    ppermute x3, starting transfers between devices, over(): return lax.ppermute(value, 'ao', SWAP)  3.02 us
  transfers between devices with their start and end apart: 11, of which 5 were waited for; matrix products, arithmetic and copies ran while one was open for 0% of the time, Pallas kernels for 18%

profile of v2, /device:TPU:0, one launch (start us, length us, event | category | flops | bytes accessed | tf_op | source)
XLA Modules:
  0.0 140.3 jit_solution(2769196513232703840)
XLA Ops:
  0.0 10.5 %transform.1 = bf16[128,16,512]{2,1,0:T(8,128)(2,1)} custom-call(bf16[16,384,768]{2,1,0:T(8,128)(2,1)} %refs_0_.8, bf16[768,128]{1,0:T(8,128)(2,1)} %refs_1_.1, bf16[384,512]{1,0:T(8,128)(2,1)} %refs_2_.1), custom_call_target="tpu_custom_call" | custom-call | tf_op jit(solution)/shard_map/transform/pallas_call | solution.py:55
  10.5 0.0 copy-start.4
  10.5 41.1 %all_to_all.5 = bf16[128,16,512]{2,1,0:T(8,128)(2,1)S(1)} all-to-all(bf16[128,16,512]{2,1,0:T(8,128)(2,1)} %transform.1), channel_id=1, replica_groups=mesh['aux'=64,'ao'=2] {'aux','ao'}, dimensions={0} | all-to-all | bytes 4194304 | tf_op jit(solution)/shard_map/all_to_all | solution.py:234
  51.6 0.0 copy-start.5
  51.6 0.0 copy-done.4
  51.6 0.8 combine.1
  52.4 0.4 collective-permute-start.3
  52.8 0.8 collective-permute-start.2
  53.7 0.8 collective-permute-start
  54.4 6.7 %collective-permute-start.1 = (bf16[1024,512]{1,0:T(8,128)(2,1)S(1)}, bf16[1024,512]{1,0:T(8,128)(2,1)}, u32[]{:S(2)}, u32[]{:S(2)}) collective-permute-start(bf16[1024,512]{1,0:T(8,128)(2,1)S(1)} %get-tuple-element.37.refs_4_), channel_id=1, source_target_pairs={{4,0},{5,1},{6,2},{7,3},{8,4},{9,5},{10,6},{11,7},{12,8},{13,9},{1... | collective-permute-start | bytes 3145736 | tf_op jit(solution)/shard_map/ppermute | solution.py:224
  61.1 0.0 collective-permute-done.3.refs_5_
  61.1 0.0 copy-done.5
  61.1 2.6 %pairs.7.refs_7_ = f32[512,512]{1,0:T(8,128)S(1)} custom-call(f32[128]{0:T(128)S(1)} %copy-done.5, f32[512,128]{1,0:T(8,128)S(1)} %get-tuple-element.35.refs_1_, f32[1,512]{1,0:T(1,128)S(1)} %bitcast.4, bf16[512,1024]{1,0:T(8,128)(2,1)S(1)} %get-tuple-element.36.refs_3_, bf16[1024,512]{1,0:T(8,128)(2,1)S(1)} %get-tuple-element.37.refs_4_, ...), custom_call_target="tpu_custom_call" | custom-call | flops 1610612736 | bytes 2097152 | tf_op jit(solution)/shard_map/pairs/pallas_call | solution.py:173
  63.7 14.3 %collective-permute-done.2.refs_3_.refs_4_ = bf16[512,1024]{1,0:T(8,128)(2,1)S(1)} collective-permute-done((bf16[512,1024]{1,0:T(8,128)(2,1)S(1)}, bf16[512,1024]{1,0:T(8,128)(2,1)S(1)}, u32[]{:S(2)}, u32[]{:S(2)}) %collective-permute-start.2) | collective-permute-done | bytes 1048608 | tf_op jit(solution)/shard_map/ppermute | solution.py:230
  78.1 2.6 %pairs.8.refs_8_ = f32[512,512]{1,0:T(8,128)S(1)} custom-call(f32[128]{0:T(128)S(1)} %copy-done.5, f32[512,128]{1,0:T(8,128)S(1)} %get-tuple-element.35.refs_1_, f32[1,512]{1,0:T(1,128)S(1)} %bitcast.5, bf16[512,1024]{1,0:T(8,128)(2,1)S(1)} %collective-permute-done.2.refs_3_.refs_4_, bf16[1024,512]{1,0:T(8,128)(2,1)S(1)} %get-tuple-element.37.refs_4_, ...), custom_call_target="tpu_custom_call" | custom-call | flops 1610612736 | bytes 2097152 | tf_op jit(solution)/shard_map/pairs/pallas_call | solution.py:173
  80.7 0.0 copy-start
  80.7 1.0 copy-done
  81.7 2.5 %collective-permute-done.refs_5_ = bf16[1024,512]{1,0:T(8,128)(2,1)} collective-permute-done((bf16[1024,512]{1,0:T(8,128)(2,1)S(1)}, bf16[1024,512]{1,0:T(8,128)(2,1)}, u32[]{:S(2)}, u32[]{:S(2)}) %collective-permute-start) | collective-permute-done | bytes 1048608 | tf_op jit(solution)/shard_map/ppermute | solution.py:224
  84.2 0.0 collective-permute-done.1.refs_6_
  84.2 0.0 collective-permute-start.6
  84.2 0.5 collective-permute-start.7
  84.7 0.0 collective-permute-start.4
  84.7 7.5 %collective-permute-start.5 = (bf16[1024,512]{1,0:T(8,128)(2,1)}, bf16[1024,512]{1,0:T(8,128)(2,1)}, u32[]{:S(2)}, u32[]{:S(2)}) collective-permute-start(bf16[1024,512]{1,0:T(8,128)(2,1)} %collective-permute-done.1.refs_6_), channel_id=1, source_target_pairs={{4,0},{5,1},{6,2},{7,3},{8,4},{9,5},{10,6},{11,7},{12,8},{13,9},{1... | collective-permute-start | bytes 3145736 | tf_op jit(solution)/shard_map/ppermute | solution.py:224
  92.1 0.0 copy-start.1
  92.1 1.2 copy-done.1
  93.4 5.8 %pairs.9 = (f32[512,512]{1,0:T(8,128)S(1)}, f32[512,512]{1,0:T(8,128)S(1)}) custom-call(f32[128]{0:T(128)S(1)} %copy-done.5, f32[512,128]{1,0:T(8,128)S(1)} %get-tuple-element.35.refs_1_, f32[1,512]{1,0:T(1,128)S(1)} %bitcast.6, bf16[512,1024]{1,0:T(8,128)(2,1)S(1)} %get-tuple-element.36.refs_3_, ...), custom_call_target="tpu_custom_call", output_to_operand_aliasing={{0}: (7, {}), {1}: (8, {})} | custom-call | flops 3221225472 | bytes 4194304 | tf_op jit(solution)/shard_map/pairs/pallas_call | solution.py:173
  99.2 0.0 collective-permute-done.6.refs_5_
  99.2 0.0 collective-permute-done.7.refs_6_
  99.2 5.8 %pairs.10 = (f32[512,512]{1,0:T(8,128)S(1)}, f32[512,512]{1,0:T(8,128)S(1)}) custom-call(f32[128]{0:T(128)S(1)} %copy-done.5, f32[512,128]{1,0:T(8,128)S(1)} %get-tuple-element.35.refs_1_, f32[1,512]{1,0:T(1,128)S(1)} %bitcast.7, bf16[512,1024]{1,0:T(8,128)(2,1)S(1)} %get-tuple-element.36.refs_3_, ...), custom_call_target="tpu_custom_call", output_to_operand_aliasing={{0}: (7, {}), {1}: (8, {})} | custom-call | flops 3221225472 | bytes 4194304 | tf_op jit(solution)/shard_map/pairs/pallas_call | solution.py:173
  105.0 0.0 copy-start.2
  105.0 1.0 copy-done.2
  106.0 9.5 %collective-permute-done.4.refs_5_ = bf16[1024,512]{1,0:T(8,128)(2,1)} collective-permute-done((bf16[1024,512]{1,0:T(8,128)(2,1)}, bf16[1024,512]{1,0:T(8,128)(2,1)}, u32[]{:S(2)}, u32[]{:S(2)}) %collective-permute-start.4) | collective-permute-done | bytes 1048608 | tf_op jit(solution)/shard_map/ppermute | solution.py:224
  115.5 0.0 copy-start.3
  115.5 0.0 collective-permute-done.5.refs_6_
  115.5 1.4 %broadcast_select_fusion = bf16[1024,512]{1,0:T(8,128)(2,1)S(1)} fusion(bf16[1024,512]{1,0:T(8,128)(2,1)} %collective-permute-done.5.refs_6_, bf16[1024,512]{1,0:T(8,128)(2,1)} %collective-permute-done.4.refs_5_, pred[]{:T(512)S(6)} %eq.5), kind=kLoop, calls=%fused_computation | loop fusion | flops 524288 | bytes 3145729 | tf_op jit(solution)/shard_map/jit(_where)/select_n | solution.py:257
  116.9 0.1 collective-permute-start.8
  117.0 0.0 copy-done.3
  117.0 5.8 %pairs.11 = (f32[512,512]{1,0:T(8,128)S(1)}, f32[512,512]{1,0:T(8,128)S(1)}) custom-call(f32[128]{0:T(128)S(1)} %copy-done.5, f32[512,128]{1,0:T(8,128)S(1)} %get-tuple-element.35.refs_1_, f32[1,512]{1,0:T(1,128)S(1)} %bitcast.8, bf16[512,1024]{1,0:T(8,128)(2,1)S(1)} %get-tuple-element.36.refs_3_, ...), custom_call_target="tpu_custom_call", output_to_operand_aliasing={{0}: (7, {}), {1}: (8, {})} | custom-call | flops 3221225472 | bytes 4194304 | tf_op jit(solution)/shard_map/pairs/pallas_call | solution.py:173
  122.9 0.0 collective-permute-done.8.refs_4_
  122.9 2.0 %pairs.13 = (f32[256,512]{1,0:T(8,128)S(1)}, bf16[256,512]{1,0:T(8,128)(2,1)S(1)}) custom-call(f32[128]{0:T(128)S(1)} %copy-done.5, f32[512,128]{1,0:T(8,128)S(1)} %get-tuple-element.35.refs_1_, f32[1,512]{1,0:T(1,128)S(1)} %bitcast.9, bf16[512,1024]{1,0:T(8,128)(2,1)S(1)} %collective-permute-done.2.refs_3_.refs_4_, ...), custom_call_target="tpu_custom_call" | custom-call | flops 805306368 | bytes 1048576 | tf_op jit(solution)/shard_map/pairs/pallas_call | solution.py:173
  124.8 0.1 collective-permute-start.9
  124.9 2.0 %pairs.12 = (f32[256,512]{1,0:T(8,128)S(1)}, bf16[256,512]{1,0:T(8,128)(2,1)S(1)}) custom-call(f32[128]{0:T(128)S(1)} %copy-done.5, f32[512,128]{1,0:T(8,128)S(1)} %get-tuple-element.35.refs_1_, f32[1,512]{1,0:T(1,128)S(1)} %bitcast.10, bf16[512,1024]{1,0:T(8,128)(2,1)S(1)} %get-tuple-element.36.refs_3_, ...), custom_call_target="tpu_custom_call" | custom-call | flops 805306368 | bytes 1048576 | tf_op jit(solution)/shard_map/pairs/pallas_call | solution.py:173
  126.9 2.1 %collective-permute-start.10 = (bf16[256,512]{1,0:T(8,128)(2,1)S(1)}, bf16[256,512]{1,0:T(8,128)(2,1)S(1)}, u32[]{:S(2)}, u32[]{:S(2)}) collective-permute-start(bf16[256,512]{1,0:T(8,128)(2,1)S(1)} %get-tuple-element.64), channel_id=1, source_target_pairs={{0,1},{1,0},{2,3},{3,2},{4,5},{5,4},{6,7},{7,6},{8,9},{9,8},{10,11... | collective-permute-start | bytes 786440 | tf_op jit(solution)/shard_map/ppermute | solution.py:230
  129.0 5.0 %collective-permute-done.9.came_own = bf16[256,512]{1,0:T(8,128)(2,1)S(1)} collective-permute-done((bf16[256,512]{1,0:T(8,128)(2,1)S(1)}, bf16[256,512]{1,0:T(8,128)(2,1)S(1)}, u32[]{:S(2)}, u32[]{:S(2)}) %collective-permute-start.9) | collective-permute-done | bytes 262176 | tf_op jit(solution)/shard_map/ppermute | solution.py:230
  134.0 5.2 %collective-permute-done.10.came_other = bf16[256,512]{1,0:T(8,128)(2,1)S(1)} collective-permute-done((bf16[256,512]{1,0:T(8,128)(2,1)S(1)}, bf16[256,512]{1,0:T(8,128)(2,1)S(1)}, u32[]{:S(2)}, u32[]{:S(2)}) %collective-permute-start.10) | collective-permute-done | bytes 262176 | tf_op jit(solution)/shard_map/ppermute | solution.py:230
  139.2 1.1 finish.1
Async XLA Ops:
  10.5 41.1 %copy-start.4 = (f32[512]{0:T(512)S(1)}, f32[512]{0:T(512)}, u32[]{:S(2)}) copy-start(f32[512]{0:T(512)} %param.9) | copy-start | bytes 6148
  51.6 9.5 %copy-start.5 = (f32[128]{0:T(128)S(1)}, f32[128]{0:T(128)}, u32[]{:S(2)}) copy-start(f32[128]{0:T(128)} %refs_0_.15) | copy-start | bytes 1540
  52.4 8.7 %collective-permute-start.3 = (bf16[1024,512]{1,0:T(8,128)(2,1)S(1)}, bf16[1024,512]{1,0:T(8,128)(2,1)S(1)}, u32[]{:S(2)}, u32[]{:S(2)}) collective-permute-start(bf16[1024,512]{1,0:T(8,128)(2,1)S(1)} %get-tuple-element.37.refs_4_), channel_id=1, source_target_pairs={{2,0},{0,2},{6,4},{4,6},{10,8},{8,10},{14,12},{12,14},{18,16},{16,... | collective-permute-start | bytes 3145736 | tf_op jit(solution)/shard_map/ppermute | solution.py:227
  52.8 25.3 %collective-permute-start.2 = (bf16[512,1024]{1,0:T(8,128)(2,1)S(1)}, bf16[512,1024]{1,0:T(8,128)(2,1)S(1)}, u32[]{:S(2)}, u32[]{:S(2)}) collective-permute-start(bf16[512,1024]{1,0:T(8,128)(2,1)S(1)} %get-tuple-element.36.refs_3_), channel_id=1, source_target_pairs={{0,1},{1,0},{2,3},{3,2},{4,5},{5,4},{6,7},{7,6},{8,9},{9,8},{10,11... | collective-permute-start | bytes 3145736 | tf_op jit(solution)/shard_map/ppermute | solution.py:230
  53.7 30.5 %collective-permute-start = (bf16[1024,512]{1,0:T(8,128)(2,1)S(1)}, bf16[1024,512]{1,0:T(8,128)(2,1)}, u32[]{:S(2)}, u32[]{:S(2)}) collective-permute-start(bf16[1024,512]{1,0:T(8,128)(2,1)S(1)} %get-tuple-element.37.refs_4_), channel_id=1, source_target_pairs={{125,0},{124,1},{127,2},{126,3},{0,4},{1,5},{2,6},{3,7},{4,8},{5,9... | collective-permute-start | bytes 3145736 | tf_op jit(solution)/shard_map/ppermute | solution.py:224
  54.4 29.8 %collective-permute-start.1 = (bf16[1024,512]{1,0:T(8,128)(2,1)S(1)}, bf16[1024,512]{1,0:T(8,128)(2,1)}, u32[]{:S(2)}, u32[]{:S(2)}) collective-permute-start(bf16[1024,512]{1,0:T(8,128)(2,1)S(1)} %get-tuple-element.37.refs_4_), channel_id=1, source_target_pairs={{4,0},{5,1},{6,2},{7,3},{8,4},{9,5},{10,6},{11,7},{12,8},{13,9},{1... | collective-permute-start | bytes 3145736 | tf_op jit(solution)/shard_map/ppermute | solution.py:224
  80.7 1.0 copy-start
  84.2 15.0 %collective-permute-start.6 = (bf16[1024,512]{1,0:T(8,128)(2,1)}, bf16[1024,512]{1,0:T(8,128)(2,1)}, u32[]{:S(2)}, u32[]{:S(2)}) collective-permute-start(bf16[1024,512]{1,0:T(8,128)(2,1)} %collective-permute-done.refs_5_), channel_id=1, source_target_pairs={{2,0},{0,2},{6,4},{4,6},{10,8},{8,10},{14,12},{12,14},{18,16},{16,... | collective-permute-start | bytes 3145736 | tf_op jit(solution)/shard_map/ppermute | solution.py:227
  84.2 15.0 %collective-permute-start.7 = (bf16[1024,512]{1,0:T(8,128)(2,1)}, bf16[1024,512]{1,0:T(8,128)(2,1)}, u32[]{:S(2)}, u32[]{:S(2)}) collective-permute-start(bf16[1024,512]{1,0:T(8,128)(2,1)} %collective-permute-done.1.refs_6_), channel_id=1, source_target_pairs={{2,0},{0,2},{6,4},{4,6},{10,8},{8,10},{14,12},{12,14},{18,16},{16,... | collective-permute-start | bytes 3145736 | tf_op jit(solution)/shard_map/ppermute | solution.py:227
  84.7 30.8 %collective-permute-start.4 = (bf16[1024,512]{1,0:T(8,128)(2,1)}, bf16[1024,512]{1,0:T(8,128)(2,1)}, u32[]{:S(2)}, u32[]{:S(2)}) collective-permute-start(bf16[1024,512]{1,0:T(8,128)(2,1)} %collective-permute-done.refs_5_), channel_id=1, source_target_pairs={{125,0},{124,1},{127,2},{126,3},{0,4},{1,5},{2,6},{3,7},{4,8},{5,9... | collective-permute-start | bytes 3145736 | tf_op jit(solution)/shard_map/ppermute | solution.py:224
  84.7 30.8 %collective-permute-start.5 = (bf16[1024,512]{1,0:T(8,128)(2,1)}, bf16[1024,512]{1,0:T(8,128)(2,1)}, u32[]{:S(2)}, u32[]{:S(2)}) collective-permute-start(bf16[1024,512]{1,0:T(8,128)(2,1)} %collective-permute-done.1.refs_6_), channel_id=1, source_target_pairs={{4,0},{5,1},{6,2},{7,3},{8,4},{9,5},{10,6},{11,7},{12,8},{13,9},{1... | collective-permute-start | bytes 3145736 | tf_op jit(solution)/shard_map/ppermute | solution.py:224
  92.1 1.2 copy-start.1
  105.0 1.0 copy-start.2
  115.5 1.5 %copy-start.3 = (f32[512,512]{1,0:T(8,128)S(1)}, f32[512,512]{1,0:T(8,128)}, u32[]{:S(2)}) copy-start(f32[512,512]{1,0:T(8,128)} %copy-done.2) | copy-start | bytes 3145732
  116.9 5.9 %collective-permute-start.8 = (bf16[1024,512]{1,0:T(8,128)(2,1)S(1)}, bf16[1024,512]{1,0:T(8,128)(2,1)S(1)}, u32[]{:S(2)}, u32[]{:S(2)}) collective-permute-start(bf16[1024,512]{1,0:T(8,128)(2,1)S(1)} %broadcast_select_fusion), channel_id=1, source_target_pairs={{2,0},{0,2},{6,4},{4,6},{10,8},{8,10},{14,12},{12,14},{18,16},{16,... | collective-permute-start | bytes 3145736 | tf_op jit(solution)/shard_map/ppermute | solution.py:227
  124.8 9.2 %collective-permute-start.9 = (bf16[256,512]{1,0:T(8,128)(2,1)S(1)}, bf16[256,512]{1,0:T(8,128)(2,1)S(1)}, u32[]{:S(2)}, u32[]{:S(2)}) collective-permute-start(bf16[256,512]{1,0:T(8,128)(2,1)S(1)} %get-tuple-element.62), channel_id=1, source_target_pairs={{0,1},{1,0},{2,3},{3,2},{4,5},{5,4},{6,7},{7,6},{8,9},{9,8},{10,11... | collective-permute-start | bytes 786440 | tf_op jit(solution)/shard_map/ppermute | solution.py:230
  126.9 12.3 %collective-permute-start.10 = (bf16[256,512]{1,0:T(8,128)(2,1)S(1)}, bf16[256,512]{1,0:T(8,128)(2,1)S(1)}, u32[]{:S(2)}, u32[]{:S(2)}) collective-permute-start(bf16[256,512]{1,0:T(8,128)(2,1)S(1)} %get-tuple-element.64), channel_id=1, source_target_pairs={{0,1},{1,0},{2,3},{3,2},{4,5},{5,4},{6,7},{7,6},{8,9},{9,8},{10,11... | collective-permute-start | bytes 786440 | tf_op jit(solution)/shard_map/ppermute | solution.py:230

commit v3 on v2

v3 whole, which is shorter than its diff:
```python
import jax
import jax.numpy as jnp
from jax import lax
from jax.experimental import pallas as pl
from jax.experimental.pallas import tpu as pltpu
from jax.sharding import PartitionSpec as P

ROW = 8
LANES = 128
BOTH = ("aux", "ao")
MIB = 1024 * 1024
SWAP = [(0, 1), (1, 0)]


def flipped(block):
    return (block // ROW) % 2


def params(mib):
    return pltpu.CompilerParams(vmem_limit_bytes=mib * MIB)


def transform_kernel(slots, group, ints_ref, occ_ref, out_ref, held_ref):
    step = pl.program_id(0)
    chunk, rows, width = ints_ref.shape
    nocc = occ_ref.shape[1]
    stride = nocc + 8
    slab = ints_ref[...].reshape(chunk * rows, width)
    half = jnp.dot(slab, occ_ref[...], preferred_element_type=jnp.float32)
    for k in range(chunk):
        turned = half[k * rows : (k + 1) * rows].T
        for column in range(rows // LANES):
            start = (column * group + lax.rem(step * chunk, group) + k) * stride
            held_ref[pl.ds(pl.multiple_of(start, 8), nocc), :] = turned[
                :, column * LANES : (column + 1) * LANES
            ]

    @pl.when(lax.rem((step + 1) * chunk, group) == 0)
    def _():
        first = pl.multiple_of((step + 1) * chunk - group, group)
        for orbital in range(nocc):
            for column in range(rows // LANES):
                tile = held_ref[pl.ds(column * group * stride + orbital, group, stride=stride), :]
                out_ref[
                    slots[orbital], pl.ds(first, group), column * LANES : (column + 1) * LANES
                ] = tile.astype(jnp.bfloat16)


def transform(ints, occ_coef, slots, chunk=8, group=8):
    count, rows, width = ints.shape
    nocc = occ_coef.shape[1]
    return pl.pallas_call(
        lambda *refs: transform_kernel(slots, group, *refs),
        grid=(count // chunk,),
        in_specs=[
            pl.BlockSpec((chunk, rows, width), lambda s: (s, 0, 0)),
            pl.BlockSpec((width, nocc), lambda s: (0, 0)),
        ],
        out_specs=pl.BlockSpec((nocc, count, rows), lambda s: (0, 0, 0)),
        out_shape=jax.ShapeDtypeStruct((nocc, count, rows), jnp.bfloat16),
        scratch_shapes=[pltpu.VMEM((group * (nocc + 8) * rows // LANES, LANES), jnp.float32)],
        compiler_params=params(56),
        name="transform",
    )(ints, occ_coef)


def combine_kernel(in_ref, vir_ref, vir_other_ref, energy_ref, own_ref, turned_ref, column_ref):
    side = lax.axis_index("ao")
    owners, halves, count, rows = in_ref.shape
    mine = in_ref[:, side].reshape(owners * count, rows)
    others = in_ref[:, 1 - side].reshape(owners * count, rows)
    total = jnp.dot(mine, vir_ref[...], preferred_element_type=jnp.float32)
    total += jnp.dot(others, vir_other_ref[...], preferred_element_type=jnp.float32)
    own_ref[...] = total.astype(jnp.bfloat16)
    turned_ref[...] = total.T.astype(jnp.bfloat16)
    column_ref[...] = jnp.broadcast_to(energy_ref[...], (LANES, energy_ref.shape[1])).T


def combine(arrived, vir, vir_other, vir_energy):
    owners, halves, count, rows = arrived.shape
    naux, nvir = owners * count, vir.shape[1]
    whole = pl.BlockSpec(memory_space=pltpu.VMEM)
    return pl.pallas_call(
        combine_kernel,
        in_specs=[whole] * 4,
        out_specs=[whole] * 3,
        out_shape=[
            jax.ShapeDtypeStruct((naux, nvir), jnp.bfloat16),
            jax.ShapeDtypeStruct((nvir, naux), jnp.bfloat16),
            jax.ShapeDtypeStruct((nvir, LANES), jnp.float32),
        ],
        compiler_params=params(16),
        name="combine",
    )(arrived, vir, vir_other, vir_energy)


def pair_kernel(sides, plan, started, last, aux_count, *refs):
    energy_ref, column_ref, row_ref, *refs = refs
    turned_refs = dict(zip(sides, refs))
    refs = refs[len(sides) :]
    visitor_refs, refs = refs[: len(plan)], refs[len(plan) :]
    started_refs = dict(zip(started, refs))
    refs = refs[len(started) :]
    block, side = lax.axis_index("aux"), lax.axis_index("ao")
    parity = lax.rem(side + lax.rem(lax.div(block, ROW), 2), 2)
    odd = lax.rem(block, 2)
    nvir = row_ref.shape[1]
    vir_pairs = jnp.concatenate([column_ref[...]] * (nvir // LANES), axis=1) + row_ref[...]
    for n, own_side in enumerate(sides):
        mine = parity if own_side == 0 else 1 - parity
        e_own = energy_ref[2 * block + mine]
        total = started_refs[own_side][...] if own_side in started_refs else None
        for ((even_distance, odd_distance), wanted), visitor_ref in zip(plan, visitor_refs):
            if own_side not in wanted:
                continue
            distance = even_distance + (odd_distance - even_distance) * odd
            visiting = lax.rem(block + distance + aux_count, aux_count)
            e_pair = e_own + energy_ref[2 * visiting + parity]
            integrals = jnp.dot(
                turned_refs[own_side][...], visitor_ref[...], preferred_element_type=jnp.float32
            )
            scaled = integrals / (e_pair - vir_pairs)
            amplitude = scaled.astype(jnp.bfloat16)
            mixed = (2.0 * scaled.T - scaled).astype(jnp.bfloat16)
            term = jnp.dot(amplitude, mixed, preferred_element_type=jnp.float32)
            total = term if total is None else total + term
        if not last:
            refs[n][...] = total
        else:
            kept_ref, *sent_refs, held_ref = refs
            half = kept_ref.shape[0]
            held_ref[...] = total
            kept_ref[...] = held_ref[pl.ds(pl.multiple_of(side * half, half), half), :]
            start = (1 - side) * half
            for sent_ref in sent_refs:
                rows = sent_ref.shape[0]
                sent_ref[...] = held_ref[pl.ds(pl.multiple_of(start, rows), rows), :].astype(
                    jnp.bfloat16
                )
                start = start + rows


def add_pairs(energies, turned, visitors, density, last=0):
    sides, started = sorted(turned), sorted(density)
    nvir, naux = turned[sides[0]].shape
    plan = [(d, w) for d, _, w in visitors]
    operands = [*energies] + [turned[s] for s in sides] + [v for _, v, _ in visitors]
    aliases = {}
    if not last:
        aliases = {len(operands) + n: sides.index(s) for n, s in enumerate(started)}
    operands += [density[s] for s in started]
    whole = pl.BlockSpec(memory_space=pltpu.VMEM)
    specs = [pl.BlockSpec(memory_space=pltpu.SMEM)] + [whole] * (len(operands) - 1)
    if last:
        half = nvir // 2
        out_shape = [jax.ShapeDtypeStruct((half, nvir), jnp.float32)]
        out_shape += [jax.ShapeDtypeStruct((half // last, nvir), jnp.bfloat16)] * last
        scratch = [pltpu.VMEM((nvir, nvir), jnp.float32)]
    else:
        out_shape = [jax.ShapeDtypeStruct((nvir, nvir), jnp.float32)] * len(sides)
        scratch = []
    pairs = sum(len(w) for _, w in plan)
    results = pl.pallas_call(
        lambda *refs: pair_kernel(sides, plan, started, last, lax.axis_size("aux"), *refs),
        in_specs=specs,
        out_specs=[whole] * len(out_shape),
        out_shape=out_shape,
        scratch_shapes=scratch,
        input_output_aliases=aliases,
        compiler_params=params(16),
        cost_estimate=pl.CostEstimate(
            flops=pairs * 2 * nvir * nvir * (naux + nvir),
            bytes_accessed=pairs * 2 * nvir * naux,
            transcendentals=0,
        ),
        name="pairs",
    )(*operands)
    return results if last else dict(zip(sides, results))


def finish_kernel(kept_own, kept_other, *refs):
    *came_refs, out_ref = refs
    block, side = lax.axis_index("aux"), lax.axis_index("ao")
    parity = lax.rem(side + lax.rem(lax.div(block, ROW), 2), 2)
    out_ref[parity] = kept_own[...] + came_refs[0][...].astype(jnp.float32)
    start = 0
    for came_ref in came_refs[1:]:
        rows = came_ref.shape[0]
        out_ref[1 - parity, start : start + rows] = kept_other[
            start : start + rows
        ] + came_ref[...].astype(jnp.float32)
        start += rows


def finish(*operands):
    rows, nvir = operands[0].shape
    whole = pl.BlockSpec(memory_space=pltpu.VMEM)
    return pl.pallas_call(
        finish_kernel,
        in_specs=[whole] * len(operands),
        out_specs=whole,
        out_shape=jax.ShapeDtypeStruct((2, rows, nvir), jnp.float32),
        compiler_params=params(16),
        name="finish",
    )(*operands)


def shards(ints, occ_coef, vir_coef, occ_energy, vir_energy):
    aux_count, ao_count = lax.axis_size("aux"), lax.axis_size("ao")
    odd = lax.axis_index("aux") % 2

    def place(block, parity):
        return block * ao_count + (parity ^ flipped(block))

    every = [(b, p) for b in range(aux_count) for p in range(ao_count)]

    def shifted(value, distance):
        route = [(place((b - distance) % aux_count, p), place(b, p)) for b, p in every]
        return lax.ppermute(value, BOTH, route)

    def across(value):
        return lax.ppermute(value, "aux", [(b ^ 1, b) for b in range(aux_count)])

    def over(value):
        return lax.ppermute(value, "ao", SWAP)

    hold = lax.optimization_barrier
    slots = [place(b, p) for b, p in every]
    vir_other = over(vir_coef)
    tiles = transform(ints, occ_coef, slots)
    arrived = lax.all_to_all(tiles, BOTH, split_axis=0, concat_axis=0, tiled=True)
    arrived = arrived.reshape(aux_count, ao_count, *arrived.shape[1:])
    arrived, vir_other = hold((arrived, vir_other))
    row = vir_energy[None, :]
    own, turned, column = combine(arrived, vir_coef, vir_other, row)
    energies = (occ_energy, column, row)

    below, above = shifted(own, 2), shifted(own, -2)
    neighbour, turned_other = across(own), over(turned)
    own_pairs = [((0, 0), own), ((1, -1), neighbour)]
    mine = add_pairs(energies, {0: turned}, [(*v, (0,)) for v in own_pairs], {})
    below, above, mine = hold((below, above, mine))
    far_below, far_above = shifted(below, 2), shifted(above, -2)
    next_below, next_above = across(below), across(above)

    turned_other, mine = hold((turned_other, mine))
    both = {0: turned, 1: turned_other}
    near = [((-2, -2), below), ((2, 2), above), ((-1, -3), next_below), ((3, 1), next_above)]
    plan = [(*v, (1,)) for v in own_pairs] + [(*v, (0, 1)) for v in near]
    density = add_pairs(energies, both, plan, mine)
    far_below, far_above, density = hold((far_below, far_above, density))

    remaining = across(jnp.where(odd == 0, far_above, far_below))
    far = [((-4, -4), far_below), ((4, 4), far_above)]
    final = [((-3, 3), remaining)]
    other = add_pairs(energies, {1: turned_other}, [(*v, (1,)) for v in far], {1: density[1]})
    remaining, other = hold((remaining, other))
    kept_other, sent = add_pairs(
        energies, {1: turned_other}, [(*v, (1,)) for v in final], other, last=1
    )
    came_own = over(sent)
    turned, sent = hold((turned, sent))
    kept_own, *sent = add_pairs(
        energies, {0: turned}, [(*v, (0,)) for v in far + final], {0: density[0]}, last=2
    )
    return finish(kept_own, kept_other, came_own, *[over(piece) for piece in sent])


def solution(mesh):
    return jax.shard_map(
        shards,
        mesh=mesh,
        in_specs=(P("aux", "ao", None), P(), P("ao", None), P(), P()),
        out_specs=P("aux", "ao", None),
        check_vma=False,
    )
```

time: 141 us -> 132 us (0.936)
  blocking collectives: 41.1 us -> 0 us
  waiting for transfers between devices: 36.6 us -> 59.5 us
  starting transfers between devices: 18.9 us -> 30.3 us
  Pallas kernels: 38.9 us -> 36 us
  local copies, waits for them, and re-layouts: 3.17 us -> 4.65 us
    all_to_all x1 -> x0, blocking collectives: 41.1 us -> none  [shards(): lax.all_to_all(tiles, BOTH, split_axis=0, concat_axis=0, tiled=True)]
    ppermute x4, waiting for transfers between devices: 12 us -> 26.1 us  [shifted(): return lax.ppermute(value, BOTH, route)]
    all_to_all x0 -> x1, starting transfers between devices: none -> 11.1 us  [shards(): lax.all_to_all(tiles, BOTH, split_axis=0, concat_axis=0, tiled=True)]
    ppermute x3 -> x5, waiting for transfers between devices: 24.6 us -> 33.4 us  [over(): return lax.ppermute(value, 'ao', SWAP)]
    pallas_call x10 -> x8, Pallas kernels: 38.9 us -> 36 us  [the longest x5 25.5 us: add_pairs(): pl.pallas_call(lambda *refs: pair_kernel(sides, plan, started, last, lax....]
    unnamed x12 -> x22, local copies, waits for them, and re-layouts: 3.17 us -> 4.65 us
    ppermute x3 -> x5, starting transfers between devices: 3.02 us -> 3.65 us  [over(): return lax.ppermute(value, 'ao', SWAP)]
  transfers between devices with their start and end apart: 11 -> 14, of which waited for: 5 -> 5; matrix products, arithmetic and copies ran while one was open for 0% -> 0% of each run, Pallas kernels for 18% -> 18%
where the time goes in v3:
time: 132 us; the launch traced here: 131 us
  waiting for transfers between devices  59.5 us (45%)
  Pallas kernels  36 us (27%)
  starting transfers between devices  30.3 us (23%)
  local copies, waits for them, and re-layouts  4.65 us (4%)
    ppermute x5, waiting for transfers between devices, over(): return lax.ppermute(value, 'ao', SWAP)  33.4 us
    ppermute x4, waiting for transfers between devices, shifted(): return lax.ppermute(value, BOTH, route)  26.1 us
    pallas_call x5, Pallas kernels, add_pairs(): pl.pallas_call(lambda *refs: pair_kernel(sides, plan, started, last, lax....  25.5 us
    ppermute x4, starting transfers between devices, shifted(): return lax.ppermute(value, BOTH, route)  14.9 us
    all_to_all x1, starting transfers between devices, shards(): lax.all_to_all(tiles, BOTH, split_axis=0, concat_axis=0, tiled=True)  11.1 us
    pallas_call x1, Pallas kernels, transform(): pl.pallas_call(lambda *refs: transform_kernel(slots, group, *refs), grid=...  7.09 us
    unnamed x22, local copies, waits for them, and re-layouts  4.65 us
    ppermute x5, starting transfers between devices, over(): return lax.ppermute(value, 'ao', SWAP)  3.65 us
  transfers between devices with their start and end apart: 14, of which 5 were waited for; matrix products, arithmetic and copies ran while one was open for 0% of the time, Pallas kernels for 18%

profile of v3, /device:TPU:0, one launch (start us, length us, event | category | flops | bytes accessed | tf_op | source)
XLA Modules:
  0.0 130.7 jit_solution(3574582388217744717)
XLA Ops:
  0.0 7.1 %transform.1 = bf16[128,16,384]{2,1,0:T(8,128)(2,1)} custom-call(bf16[16,384,768]{2,1,0:T(8,128)(2,1)} %refs_0_.6, bf16[768,128]{1,0:T(8,128)(2,1)} %refs_1_.1), custom_call_target="tpu_custom_call" | custom-call | tf_op jit(solution)/shard_map/transform/pallas_call | solution.py:52
  7.1 11.1 %all-to-all-start = ((bf16[128,16,384]{2,1,0:T(8,128)(2,1)}), bf16[128,16,384]{2,1,0:T(8,128)(2,1)S(1)}, u32[]{:S(2)}, u32[]{:S(2)}) async-start(bf16[128,16,384]{2,1,0:T(8,128)(2,1)} %transform.1), calls=%async_computation | async-start | bytes 3145728 | tf_op jit(solution)/shard_map/all_to_all | solution.py:231
  18.2 0.0 copy-done
  18.3 0.0 copy-start.2
  18.3 1.2 collective-permute-start
  19.4 25.9 %collective-permute-done.vir_other_ref = bf16[384,512]{1,0:T(8,128)(2,1)S(1)} collective-permute-done((bf16[384,512]{1,0:T(8,128)(2,1)S(1)}, bf16[384,512]{1,0:T(8,128)(2,1)S(1)}, u32[]{:S(2)}, u32[]{:S(2)}) %collective-permute-start) | collective-permute-done | bytes 393248 | tf_op jit(solution)/shard_map/ppermute | solution.py:225
  45.4 0.0 all-to-all-done
  45.4 0.0 copy-done.1
  45.4 2.3 %combine.1 = (bf16[1024,512]{1,0:T(8,128)(2,1)S(1)}, bf16[512,1024]{1,0:T(8,128)(2,1)}, f32[512,128]{1,0:T(8,128)S(1)}) custom-call(bf16[64,2,16,384]{3,2,1,0:T(8,128)(2,1)S(1)} %bitcast.2, bf16[384,512]{1,0:T(8,128)(2,1)S(1)} %copy-done, bf16[384,512]{1,0:T(8,128)(2,1)S(1)} %collective-permute-done.vir_other_ref, f32[1,512]{1,0:T(1,128)S(1)} %bitcast.3), custom_call_target="tpu_custom_call" | custom-call | tf_op jit(solution)/shard_map/combine/pallas_call | solution.py:83
  47.7 0.0 collective-permute-start.4
  47.7 1.5 %collective-permute-start.2 = (bf16[1024,512]{1,0:T(8,128)(2,1)S(1)}, bf16[1024,512]{1,0:T(8,128)(2,1)}, u32[]{:S(2)}, u32[]{:S(2)}) collective-permute-start(bf16[1024,512]{1,0:T(8,128)(2,1)S(1)} %get-tuple-element.32.refs_4_.refs_5_), channel_id=1, source_target_pairs={{125,0},{124,1},{127,2},{126,3},{0,4},{1,5},{2,6},{3,7},{4,8},{5,9... | collective-permute-start | bytes 3145736 | tf_op jit(solution)/shard_map/ppermute | solution.py:219
  49.2 6.0 %collective-permute-start.3 = (bf16[1024,512]{1,0:T(8,128)(2,1)S(1)}, bf16[1024,512]{1,0:T(8,128)(2,1)}, u32[]{:S(2)}, u32[]{:S(2)}) collective-permute-start(bf16[1024,512]{1,0:T(8,128)(2,1)S(1)} %get-tuple-element.32.refs_4_.refs_5_), channel_id=1, source_target_pairs={{4,0},{5,1},{6,2},{7,3},{8,4},{9,5},{10,6},{11,7},{12,8},{13,9},{1... | collective-permute-start | bytes 3145736 | tf_op jit(solution)/shard_map/ppermute | solution.py:219
  55.2 0.0 collective-permute-start.1
  55.2 0.0 collective-permute-done.4.refs_5_.refs_6_
  55.2 0.0 copy-done.2
  55.2 3.7 %pairs.5.refs_11_ = f32[512,512]{1,0:T(8,128)S(1)} custom-call(f32[128]{0:T(128)S(1)} %copy-done.2, f32[512,128]{1,0:T(8,128)S(1)} %get-tuple-element.30.refs_1_, f32[1,512]{1,0:T(1,128)S(1)} %bitcast.4, bf16[512,1024]{1,0:T(8,128)(2,1)} %get-tuple-element.45.refs_3_, bf16[1024,512]{1,0:T(8,128)(2,1)S(1)} %get-tuple-element.32.refs_4_.refs_5_, ...), custom_call_target="tpu_custom_call" | custom-call | flops 1610612736 | bytes 2097152 | tf_op jit(solution)/shard_map/pairs/pallas_call | solution.py:163
  58.9 0.0 copy-done.3
  58.9 0.0 copy-done.5
  58.9 0.0 copy-start.7
  58.9 0.9 copy-done.7
  59.9 19.0 %collective-permute-done.2.refs_7_ = bf16[1024,512]{1,0:T(8,128)(2,1)} collective-permute-done((bf16[1024,512]{1,0:T(8,128)(2,1)S(1)}, bf16[1024,512]{1,0:T(8,128)(2,1)}, u32[]{:S(2)}, u32[]{:S(2)}) %collective-permute-start.2) | collective-permute-done | bytes 1048608 | tf_op jit(solution)/shard_map/ppermute | solution.py:219
  78.8 0.0 collective-permute-done.3.refs_8_
  78.8 0.0 collective-permute-start.7
  78.8 0.5 collective-permute-start.8
  79.3 0.0 collective-permute-start.5
  79.3 7.5 %collective-permute-start.6 = (bf16[1024,512]{1,0:T(8,128)(2,1)}, bf16[1024,512]{1,0:T(8,128)(2,1)S(1)}, u32[]{:S(2)}, u32[]{:S(2)}) collective-permute-start(bf16[1024,512]{1,0:T(8,128)(2,1)} %collective-permute-done.3.refs_8_), channel_id=1, source_target_pairs={{4,0},{5,1},{6,2},{7,3},{8,4},{9,5},{10,6},{11,7},{12,8},{13,9},{1... | collective-permute-start | bytes 3145736 | tf_op jit(solution)/shard_map/ppermute | solution.py:219
  86.8 0.0 collective-permute-done.1.refs_4_.refs_3_
  86.8 0.0 collective-permute-done.7.refs_9_
  86.8 0.0 collective-permute-done.8.refs_10_
  86.8 1.2 copy-done.4
  88.0 1.2 copy-done.6
  89.2 1.2 copy-done.8
  90.5 12.4 %pairs.6 = (f32[512,512]{1,0:T(8,128)S(1)}, f32[512,512]{1,0:T(8,128)S(1)}) custom-call(f32[128]{0:T(128)S(1)} %copy-done.2, f32[512,128]{1,0:T(8,128)S(1)} %get-tuple-element.30.refs_1_, f32[1,512]{1,0:T(1,128)S(1)} %bitcast.5, bf16[512,1024]{1,0:T(8,128)(2,1)} %get-tuple-element.45.refs_3_, ...), custom_call_target="tpu_custom_call", output_to_operand_aliasing={{0}: (11, {})} | custom-call | flops 8053063680 | bytes 10485760 | tf_op jit(solution)/shard_map/pairs/pallas_call | solution.py:163
  102.9 7.1 %collective-permute-done.5.refs_4_ = bf16[1024,512]{1,0:T(8,128)(2,1)S(1)} collective-permute-done((bf16[1024,512]{1,0:T(8,128)(2,1)}, bf16[1024,512]{1,0:T(8,128)(2,1)S(1)}, u32[]{:S(2)}, u32[]{:S(2)}) %collective-permute-start.5) | collective-permute-done | bytes 1048608 | tf_op jit(solution)/shard_map/ppermute | solution.py:219
  110.0 0.0 collective-permute-done.6.refs_5_
  110.0 0.1 broadcast_select_fusion
  110.2 0.1 collective-permute-start.9
  110.3 2.8 %pairs.7.refs_5_ = f32[512,512]{1,0:T(8,128)S(1)} custom-call(f32[128]{0:T(128)S(1)} %copy-done.2, f32[512,128]{1,0:T(8,128)S(1)} %get-tuple-element.30.refs_1_, f32[1,512]{1,0:T(1,128)S(1)} %bitcast.6, bf16[512,1024]{1,0:T(8,128)(2,1)S(1)} %collective-permute-done.1.refs_4_.refs_3_, ...), custom_call_target="tpu_custom_call", output_to_operand_aliasing={{}: (6, {})} | custom-call | flops 1610612736 | bytes 2097152 | tf_op jit(solution)/shard_map/pairs/pallas_call | solution.py:163
  113.0 0.0 collective-permute-done.9.refs_4_.refs_6_
  113.1 2.0 %pairs.8 = (f32[256,512]{1,0:T(8,128)S(1)}, bf16[256,512]{1,0:T(8,128)(2,1)S(1)}) custom-call(f32[128]{0:T(128)S(1)} %copy-done.2, f32[512,128]{1,0:T(8,128)S(1)} %get-tuple-element.30.refs_1_, f32[1,512]{1,0:T(1,128)S(1)} %bitcast.7, bf16[512,1024]{1,0:T(8,128)(2,1)S(1)} %collective-permute-done.1.refs_4_.refs_3_, ...), custom_call_target="tpu_custom_call" | custom-call | flops 805306368 | bytes 1048576 | tf_op jit(solution)/shard_map/pairs/pallas_call | solution.py:163
  115.0 0.3 collective-permute-start.10
  115.3 4.6 %pairs.9 = (f32[256,512]{1,0:T(8,128)S(1)}, bf16[128,512]{1,0:T(8,128)(2,1)S(1)}, bf16[128,512]{1,0:T(8,128)(2,1)S(1)}) custom-call(f32[128]{0:T(128)S(1)} %copy-done.2, f32[512,128]{1,0:T(8,128)S(1)} %get-tuple-element.30.refs_1_, f32[1,512]{1,0:T(1,128)S(1)} %bitcast.8, bf16[512,1024]{1,0:T(8,128)(2,1)} %get-tuple-element.45.refs_3_, ...), custom_call_target="tpu_custom_call" | custom-call | flops 2415919104 | bytes 3145728 | tf_op jit(solution)/shard_map/pairs/pallas_call | solution.py:163
  119.9 2.1 %collective-permute-start.11 = (bf16[128,512]{1,0:T(8,128)(2,1)S(1)}, bf16[128,512]{1,0:T(8,128)(2,1)S(1)}, u32[]{:S(2)}, u32[]{:S(2)}) collective-permute-start(bf16[128,512]{1,0:T(8,128)(2,1)S(1)} %get-tuple-element.49), channel_id=1, source_target_pairs={{0,1},{1,0},{2,3},{3,2},{4,5},{5,4},{6,7},{7,6},{8,9},{9,8},{10,11... | collective-permute-start | bytes 393224 | tf_op jit(solution)/shard_map/ppermute | solution.py:225
  122.0 0.1 collective-permute-start.12
  122.1 5.1 %collective-permute-done.11.refs_1_ = bf16[128,512]{1,0:T(8,128)(2,1)S(1)} collective-permute-done((bf16[128,512]{1,0:T(8,128)(2,1)S(1)}, bf16[128,512]{1,0:T(8,128)(2,1)S(1)}, u32[]{:S(2)}, u32[]{:S(2)}) %collective-permute-start.11) | collective-permute-done | bytes 131104 | tf_op jit(solution)/shard_map/ppermute | solution.py:225
  127.2 2.4 %collective-permute-done.12.refs_2_ = bf16[128,512]{1,0:T(8,128)(2,1)S(1)} collective-permute-done((bf16[128,512]{1,0:T(8,128)(2,1)S(1)}, bf16[128,512]{1,0:T(8,128)(2,1)S(1)}, u32[]{:S(2)}, u32[]{:S(2)}) %collective-permute-start.12) | collective-permute-done | bytes 131104 | tf_op jit(solution)/shard_map/ppermute | solution.py:225
  129.6 0.0 collective-permute-done.10.refs_0_
  129.6 1.1 finish.1
  (11 shorter events, 0.0 us)
Async XLA Ops:
  7.1 11.2 %copy-start = (bf16[384,512]{1,0:T(8,128)(2,1)S(1)}, bf16[384,512]{1,0:T(8,128)(2,1)}, u32[]{:S(2)}) copy-start(bf16[384,512]{1,0:T(8,128)(2,1)} %vir_ref.1) | copy-start | bytes 1179652
  7.1 38.3 %copy-start.1 = (f32[512]{0:T(512)S(1)}, f32[512]{0:T(512)}, u32[]{:S(2)}) copy-start(f32[512]{0:T(512)} %param.9) | copy-start | bytes 6148
  7.1 38.3 %all-to-all-start = ((bf16[128,16,384]{2,1,0:T(8,128)(2,1)}), bf16[128,16,384]{2,1,0:T(8,128)(2,1)S(1)}, u32[]{:S(2)}, u32[]{:S(2)}) async-start(bf16[128,16,384]{2,1,0:T(8,128)(2,1)} %transform.1), calls=%async_computation | async-start | bytes 3145728 | tf_op jit(solution)/shard_map/all_to_all | solution.py:231
  18.3 36.9 %copy-start.2 = (f32[128]{0:T(128)S(1)}, f32[128]{0:T(128)}, u32[]{:S(2)}) copy-start(f32[128]{0:T(128)} %refs_0_.11) | copy-start | bytes 1540
  18.3 27.1 %collective-permute-start = (bf16[384,512]{1,0:T(8,128)(2,1)S(1)}, bf16[384,512]{1,0:T(8,128)(2,1)S(1)}, u32[]{:S(2)}, u32[]{:S(2)}) collective-permute-start(bf16[384,512]{1,0:T(8,128)(2,1)S(1)} %copy-done), channel_id=1, source_target_pairs={{0,1},{1,0},{2,3},{3,2},{4,5},{5,4},{6,7},{7,6},{8,9},{9,8},{10,11... | collective-permute-start | bytes 1179656 | tf_op jit(solution)/shard_map/ppermute | solution.py:225
  47.7 11.2 %copy-start.3 = (bf16[1024,512]{1,0:T(8,128)(2,1)}, bf16[1024,512]{1,0:T(8,128)(2,1)S(1)}, u32[]{:S(2)}) copy-start(bf16[1024,512]{1,0:T(8,128)(2,1)S(1)} %get-tuple-element.32.refs_4_.refs_5_) | copy-start | bytes 3145732
  47.7 7.5 %collective-permute-start.4 = (bf16[1024,512]{1,0:T(8,128)(2,1)S(1)}, bf16[1024,512]{1,0:T(8,128)(2,1)S(1)}, u32[]{:S(2)}, u32[]{:S(2)}) collective-permute-start(bf16[1024,512]{1,0:T(8,128)(2,1)S(1)} %get-tuple-element.32.refs_4_.refs_5_), channel_id=1, source_target_pairs={{2,0},{0,2},{6,4},{4,6},{10,8},{8,10},{14,12},{12,14},{18,16},{16,... | collective-permute-start | bytes 3145736 | tf_op jit(solution)/shard_map/ppermute | solution.py:222
  47.7 31.1 %collective-permute-start.2 = (bf16[1024,512]{1,0:T(8,128)(2,1)S(1)}, bf16[1024,512]{1,0:T(8,128)(2,1)}, u32[]{:S(2)}, u32[]{:S(2)}) collective-permute-start(bf16[1024,512]{1,0:T(8,128)(2,1)S(1)} %get-tuple-element.32.refs_4_.refs_5_), channel_id=1, source_target_pairs={{125,0},{124,1},{127,2},{126,3},{0,4},{1,5},{2,6},{3,7},{4,8},{5,9... | collective-permute-start | bytes 3145736 | tf_op jit(solution)/shard_map/ppermute | solution.py:219
  49.2 29.6 %collective-permute-start.3 = (bf16[1024,512]{1,0:T(8,128)(2,1)S(1)}, bf16[1024,512]{1,0:T(8,128)(2,1)}, u32[]{:S(2)}, u32[]{:S(2)}) collective-permute-start(bf16[1024,512]{1,0:T(8,128)(2,1)S(1)} %get-tuple-element.32.refs_4_.refs_5_), channel_id=1, source_target_pairs={{4,0},{5,1},{6,2},{7,3},{8,4},{9,5},{10,6},{11,7},{12,8},{13,9},{1... | collective-permute-start | bytes 3145736 | tf_op jit(solution)/shard_map/ppermute | solution.py:219
  55.2 31.6 %collective-permute-start.1 = (bf16[512,1024]{1,0:T(8,128)(2,1)}, bf16[512,1024]{1,0:T(8,128)(2,1)S(1)}, u32[]{:S(2)}, u32[]{:S(2)}) collective-permute-start(bf16[512,1024]{1,0:T(8,128)(2,1)} %get-tuple-element.45.refs_3_), channel_id=1, source_target_pairs={{0,1},{1,0},{2,3},{3,2},{4,5},{5,4},{6,7},{7,6},{8,9},{9,8},{10,11... | collective-permute-start | bytes 3145736 | tf_op jit(solution)/shard_map/ppermute | solution.py:225
  55.2 3.7 %copy-start.5 = (bf16[1024,512]{1,0:T(8,128)(2,1)}, bf16[1024,512]{1,0:T(8,128)(2,1)S(1)}, u32[]{:S(2)}) copy-start(bf16[1024,512]{1,0:T(8,128)(2,1)S(1)} %collective-permute-done.4.refs_5_.refs_6_) | copy-start | bytes 3145732
  58.9 1.0 copy-start.7
  78.8 8.0 %collective-permute-start.7 = (bf16[1024,512]{1,0:T(8,128)(2,1)}, bf16[1024,512]{1,0:T(8,128)(2,1)}, u32[]{:S(2)}, u32[]{:S(2)}) collective-permute-start(bf16[1024,512]{1,0:T(8,128)(2,1)} %collective-permute-done.2.refs_7_), channel_id=1, source_target_pairs={{2,0},{0,2},{6,4},{4,6},{10,8},{8,10},{14,12},{12,14},{18,16},{16,... | collective-permute-start | bytes 3145736 | tf_op jit(solution)/shard_map/ppermute | solution.py:222
  78.8 8.0 %collective-permute-start.8 = (bf16[1024,512]{1,0:T(8,128)(2,1)}, bf16[1024,512]{1,0:T(8,128)(2,1)}, u32[]{:S(2)}, u32[]{:S(2)}) collective-permute-start(bf16[1024,512]{1,0:T(8,128)(2,1)} %collective-permute-done.3.refs_8_), channel_id=1, source_target_pairs={{2,0},{0,2},{6,4},{4,6},{10,8},{8,10},{14,12},{12,14},{18,16},{16,... | collective-permute-start | bytes 3145736 | tf_op jit(solution)/shard_map/ppermute | solution.py:222
  79.3 30.7 %collective-permute-start.5 = (bf16[1024,512]{1,0:T(8,128)(2,1)}, bf16[1024,512]{1,0:T(8,128)(2,1)S(1)}, u32[]{:S(2)}, u32[]{:S(2)}) collective-permute-start(bf16[1024,512]{1,0:T(8,128)(2,1)} %collective-permute-done.2.refs_7_), channel_id=1, source_target_pairs={{125,0},{124,1},{127,2},{126,3},{0,4},{1,5},{2,6},{3,7},{4,8},{5,9... | collective-permute-start | bytes 3145736 | tf_op jit(solution)/shard_map/ppermute | solution.py:219
  79.3 30.7 %collective-permute-start.6 = (bf16[1024,512]{1,0:T(8,128)(2,1)}, bf16[1024,512]{1,0:T(8,128)(2,1)S(1)}, u32[]{:S(2)}, u32[]{:S(2)}) collective-permute-start(bf16[1024,512]{1,0:T(8,128)(2,1)} %collective-permute-done.3.refs_8_), channel_id=1, source_target_pairs={{4,0},{5,1},{6,2},{7,3},{8,4},{9,5},{10,6},{11,7},{12,8},{13,9},{1... | collective-permute-start | bytes 3145736 | tf_op jit(solution)/shard_map/ppermute | solution.py:219
  86.8 1.2 copy-start.4
  88.0 1.2 copy-start.6
  89.2 1.2 copy-start.8
  102.9 7.2 %copy-start.9 = (f32[512,512]{1,0:T(8,128)}, f32[512,512]{1,0:T(8,128)S(1)}, u32[]{:S(2)}) copy-start(f32[512,512]{1,0:T(8,128)S(1)} %get-tuple-element.46.refs_7_) | copy-start | bytes 3145732
  110.2 2.9 %collective-permute-start.9 = (bf16[1024,512]{1,0:T(8,128)(2,1)S(1)}, bf16[1024,512]{1,0:T(8,128)(2,1)S(1)}, u32[]{:S(2)}, u32[]{:S(2)}) collective-permute-start(bf16[1024,512]{1,0:T(8,128)(2,1)S(1)} %broadcast_select_fusion), channel_id=1, source_target_pairs={{2,0},{0,2},{6,4},{4,6},{10,8},{8,10},{14,12},{12,14},{18,16},{16,... | collective-permute-start | bytes 3145736 | tf_op jit(solution)/shard_map/ppermute | solution.py:222
  113.0 2.3 %copy-start.10 = (f32[512,512]{1,0:T(8,128)S(1)}, f32[512,512]{1,0:T(8,128)}, u32[]{:S(2)}) copy-start(f32[512,512]{1,0:T(8,128)} %copy-done.9) | copy-start | bytes 3145732
  115.0 14.6 %collective-permute-start.10 = (bf16[256,512]{1,0:T(8,128)(2,1)S(1)}, bf16[256,512]{1,0:T(8,128)(2,1)S(1)}, u32[]{:S(2)}, u32[]{:S(2)}) collective-permute-start(bf16[256,512]{1,0:T(8,128)(2,1)S(1)} %get-tuple-element.44), channel_id=1, source_target_pairs={{0,1},{1,0},{2,3},{3,2},{4,5},{5,4},{6,7},{7,6},{8,9},{9,8},{10,11... | collective-permute-start | bytes 786440 | tf_op jit(solution)/shard_map/ppermute | solution.py:225
  119.9 7.3 %collective-permute-start.11 = (bf16[128,512]{1,0:T(8,128)(2,1)S(1)}, bf16[128,512]{1,0:T(8,128)(2,1)S(1)}, u32[]{:S(2)}, u32[]{:S(2)}) collective-permute-start(bf16[128,512]{1,0:T(8,128)(2,1)S(1)} %get-tuple-element.49), channel_id=1, source_target_pairs={{0,1},{1,0},{2,3},{3,2},{4,5},{5,4},{6,7},{7,6},{8,9},{9,8},{10,11... | collective-permute-start | bytes 393224 | tf_op jit(solution)/shard_map/ppermute | solution.py:225
  122.0 7.6 %collective-permute-start.12 = (bf16[128,512]{1,0:T(8,128)(2,1)S(1)}, bf16[128,512]{1,0:T(8,128)(2,1)S(1)}, u32[]{:S(2)}, u32[]{:S(2)}) collective-permute-start(bf16[128,512]{1,0:T(8,128)(2,1)S(1)} %get-tuple-element.50), channel_id=1, source_target_pairs={{0,1},{1,0},{2,3},{3,2},{4,5},{5,4},{6,7},{7,6},{8,9},{9,8},{10,11... | collective-permute-start | bytes 393224 | tf_op jit(solution)/shard_map/ppermute | solution.py:225

commit v4 on v3

--- a/solution.py
+++ b/solution.py
@@ -106,24 +106,35 @@
     odd = lax.rem(block, 2)
     nvir = row_ref.shape[1]
     vir_pairs = jnp.concatenate([column_ref[...]] * (nvir // LANES), axis=1) + row_ref[...]
-    for n, own_side in enumerate(sides):
+    jobs = []
+    for own_side in sides:
         mine = parity if own_side == 0 else 1 - parity
         e_own = energy_ref[2 * block + mine]
-        total = started_refs[own_side][...] if own_side in started_refs else None
         for ((even_distance, odd_distance), wanted), visitor_ref in zip(plan, visitor_refs):
-            if own_side not in wanted:
-                continue
-            distance = even_distance + (odd_distance - even_distance) * odd
-            visiting = lax.rem(block + distance + aux_count, aux_count)
-            e_pair = e_own + energy_ref[2 * visiting + parity]
-            integrals = jnp.dot(
-                turned_refs[own_side][...], visitor_ref[...], preferred_element_type=jnp.float32
-            )
-            scaled = integrals / (e_pair - vir_pairs)
-            amplitude = scaled.astype(jnp.bfloat16)
-            mixed = (2.0 * scaled.T - scaled).astype(jnp.bfloat16)
-            term = jnp.dot(amplitude, mixed, preferred_element_type=jnp.float32)
-            total = term if total is None else total + term
+            if own_side in wanted:
+                distance = even_distance + (odd_distance - even_distance) * odd
+                visiting = lax.rem(block + distance + aux_count, aux_count)
+                e_pair = e_own + energy_ref[2 * visiting + parity]
+                jobs.append((own_side, e_pair, visitor_ref))
+
+    def integrals_of(own_side, e_pair, visitor_ref):
+        return jnp.dot(
+            turned_refs[own_side][...], visitor_ref[...], preferred_element_type=jnp.float32
+        )
+
+    totals = {s: started_refs[s][...] if s in started_refs else None for s in sides}
+    upcoming = integrals_of(*jobs[0])
+    for k, (own_side, e_pair, _) in enumerate(jobs):
+        integrals = upcoming
+        if k + 1 < len(jobs):
+            upcoming = integrals_of(*jobs[k + 1])
+        scaled = integrals / (e_pair - vir_pairs)
+        amplitude = scaled.astype(jnp.bfloat16)
+        mixed = (2.0 * scaled.T - scaled).astype(jnp.bfloat16)
+        term = jnp.dot(amplitude, mixed, preferred_element_type=jnp.float32)
+        totals[own_side] = term if totals[own_side] is None else totals[own_side] + term
+    for n, own_side in enumerate(sides):
+        total = totals[own_side]
         if not last:
             refs[n][...] = total
         else:

time: 132 us -> 131 us (level)
  Pallas kernels: 36 us -> 33.5 us
  waiting for transfers between devices: 59.5 us -> 61.6 us
    pallas_call x5, Pallas kernels: 25.5 us -> 23 us  [add_pairs(): pl.pallas_call(lambda *refs: pair_kernel(sides, plan, started, last, lax....]
    ppermute x4, waiting for transfers between devices: 26.1 us -> 27.6 us  [shifted(): return lax.ppermute(value, BOTH, route)]
  transfers between devices with their start and end apart: 14 -> 14, of which waited for: 5 -> 6; matrix products, arithmetic and copies ran while one was open for 0% -> 0% of each run, Pallas kernels for 18% -> 16%
where the time goes in v4:
time: 131 us; the launch traced here: 130 us
  waiting for transfers between devices  61.6 us (47%)
  Pallas kernels  33.5 us (26%)
  starting transfers between devices  30.3 us (23%)
  local copies, waits for them, and re-layouts  4.65 us (4%)
    ppermute x5, waiting for transfers between devices, over(): return lax.ppermute(value, 'ao', SWAP)  33.8 us
    ppermute x4, waiting for transfers between devices, shifted(): return lax.ppermute(value, BOTH, route)  27.6 us
    pallas_call x5, Pallas kernels, add_pairs(): pl.pallas_call(lambda *refs: pair_kernel(sides, plan, started, last, lax....  23 us
    ppermute x4, starting transfers between devices, shifted(): return lax.ppermute(value, BOTH, route)  14.9 us
    all_to_all x1, starting transfers between devices, shards(): lax.all_to_all(tiles, BOTH, split_axis=0, concat_axis=0, tiled=True)  11.1 us
    pallas_call x1, Pallas kernels, transform(): pl.pallas_call(lambda *refs: transform_kernel(slots, group, *refs), grid=...  7.09 us
    unnamed x22, local copies, waits for them, and re-layouts  4.65 us
    ppermute x5, starting transfers between devices, over(): return lax.ppermute(value, 'ao', SWAP)  3.64 us
  transfers between devices with their start and end apart: 14, of which 6 were waited for; matrix products, arithmetic and copies ran while one was open for 0% of the time, Pallas kernels for 16%

profile of v4, /device:TPU:0, one launch (start us, length us, event | category | flops | bytes accessed | tf_op | source)
XLA Modules:
  0.0 130.3 jit_solution(15022891198422487350)
XLA Ops:
  0.0 7.1 %transform.1 = bf16[128,16,384]{2,1,0:T(8,128)(2,1)} custom-call(bf16[16,384,768]{2,1,0:T(8,128)(2,1)} %refs_0_.6, bf16[768,128]{1,0:T(8,128)(2,1)} %refs_1_.1), custom_call_target="tpu_custom_call" | custom-call | tf_op jit(solution)/shard_map/transform/pallas_call | solution.py:52
  7.1 11.1 %all-to-all-start = ((bf16[128,16,384]{2,1,0:T(8,128)(2,1)}), bf16[128,16,384]{2,1,0:T(8,128)(2,1)S(1)}, u32[]{:S(2)}, u32[]{:S(2)}) async-start(bf16[128,16,384]{2,1,0:T(8,128)(2,1)} %transform.1), calls=%async_computation | async-start | bytes 3145728 | tf_op jit(solution)/shard_map/all_to_all | solution.py:242
  18.2 0.0 copy-done
  18.3 0.0 copy-start.2
  18.3 1.2 collective-permute-start
  19.4 25.9 %collective-permute-done.vir_other_ref = bf16[384,512]{1,0:T(8,128)(2,1)S(1)} collective-permute-done((bf16[384,512]{1,0:T(8,128)(2,1)S(1)}, bf16[384,512]{1,0:T(8,128)(2,1)S(1)}, u32[]{:S(2)}, u32[]{:S(2)}) %collective-permute-start) | collective-permute-done | bytes 393248 | tf_op jit(solution)/shard_map/ppermute | solution.py:236
  45.4 0.0 all-to-all-done
  45.4 0.0 copy-done.1
  45.4 2.3 %combine.1 = (bf16[1024,512]{1,0:T(8,128)(2,1)S(1)}, bf16[512,1024]{1,0:T(8,128)(2,1)}, f32[512,128]{1,0:T(8,128)S(1)}) custom-call(bf16[64,2,16,384]{3,2,1,0:T(8,128)(2,1)S(1)} %bitcast.2, bf16[384,512]{1,0:T(8,128)(2,1)S(1)} %copy-done, bf16[384,512]{1,0:T(8,128)(2,1)S(1)} %collective-permute-done.vir_other_ref, f32[1,512]{1,0:T(1,128)S(1)} %bitcast.3), custom_call_target="tpu_custom_call" | custom-call | tf_op jit(solution)/shard_map/combine/pallas_call | solution.py:83
  47.7 0.0 collective-permute-start.4
  47.7 1.5 %collective-permute-start.2 = (bf16[1024,512]{1,0:T(8,128)(2,1)S(1)}, bf16[1024,512]{1,0:T(8,128)(2,1)}, u32[]{:S(2)}, u32[]{:S(2)}) collective-permute-start(bf16[1024,512]{1,0:T(8,128)(2,1)S(1)} %get-tuple-element.32.refs_4_.refs_5_), channel_id=1, source_target_pairs={{125,0},{124,1},{127,2},{126,3},{0,4},{1,5},{2,6},{3,7},{4,8},{5,9... | collective-permute-start | bytes 3145736 | tf_op jit(solution)/shard_map/ppermute | solution.py:230
  49.2 6.0 %collective-permute-start.3 = (bf16[1024,512]{1,0:T(8,128)(2,1)S(1)}, bf16[1024,512]{1,0:T(8,128)(2,1)}, u32[]{:S(2)}, u32[]{:S(2)}) collective-permute-start(bf16[1024,512]{1,0:T(8,128)(2,1)S(1)} %get-tuple-element.32.refs_4_.refs_5_), channel_id=1, source_target_pairs={{4,0},{5,1},{6,2},{7,3},{8,4},{9,5},{10,6},{11,7},{12,8},{13,9},{1... | collective-permute-start | bytes 3145736 | tf_op jit(solution)/shard_map/ppermute | solution.py:230
  55.2 0.0 collective-permute-start.1
  55.2 0.0 collective-permute-done.4.refs_5_.refs_6_
  55.2 0.0 copy-done.2
  55.2 3.7 %pairs.5.refs_11_ = f32[512,512]{1,0:T(8,128)S(1)} custom-call(f32[128]{0:T(128)S(1)} %copy-done.2, f32[512,128]{1,0:T(8,128)S(1)} %get-tuple-element.30.refs_1_, f32[1,512]{1,0:T(1,128)S(1)} %bitcast.4, bf16[512,1024]{1,0:T(8,128)(2,1)} %get-tuple-element.45.refs_3_, bf16[1024,512]{1,0:T(8,128)(2,1)S(1)} %get-tuple-element.32.refs_4_.refs_5_, ...), custom_call_target="tpu_custom_call" | custom-call | flops 1610612736 | bytes 2097152 | tf_op jit(solution)/shard_map/pairs/pallas_call | solution.py:174
  58.9 0.9 copy-done.7
  59.9 19.0 %collective-permute-done.2.refs_7_ = bf16[1024,512]{1,0:T(8,128)(2,1)} collective-permute-done((bf16[1024,512]{1,0:T(8,128)(2,1)S(1)}, bf16[1024,512]{1,0:T(8,128)(2,1)}, u32[]{:S(2)}, u32[]{:S(2)}) %collective-permute-start.2) | collective-permute-done | bytes 1048608 | tf_op jit(solution)/shard_map/ppermute | solution.py:230
  78.8 0.0 collective-permute-done.3.refs_8_
  78.8 0.0 collective-permute-start.7
  78.8 0.5 collective-permute-start.8
  79.3 0.0 collective-permute-start.5
  79.3 7.5 %collective-permute-start.6 = (bf16[1024,512]{1,0:T(8,128)(2,1)}, bf16[1024,512]{1,0:T(8,128)(2,1)S(1)}, u32[]{:S(2)}, u32[]{:S(2)}) collective-permute-start(bf16[1024,512]{1,0:T(8,128)(2,1)} %collective-permute-done.3.refs_8_), channel_id=1, source_target_pairs={{4,0},{5,1},{6,2},{7,3},{8,4},{9,5},{10,6},{11,7},{12,8},{13,9},{1... | collective-permute-start | bytes 3145736 | tf_op jit(solution)/shard_map/ppermute | solution.py:230
  86.8 0.0 collective-permute-done.1.refs_4_.refs_3_
  86.8 0.0 collective-permute-done.7.refs_9_
  86.8 0.0 collective-permute-done.8.refs_10_
  86.8 0.0 copy-start.4
  86.8 1.2 copy-done.4
  88.0 1.2 copy-done.6
  89.2 1.2 copy-done.8
  90.5 10.9 %pairs.6 = (f32[512,512]{1,0:T(8,128)S(1)}, f32[512,512]{1,0:T(8,128)S(1)}) custom-call(f32[128]{0:T(128)S(1)} %copy-done.2, f32[512,128]{1,0:T(8,128)S(1)} %get-tuple-element.30.refs_1_, f32[1,512]{1,0:T(1,128)S(1)} %bitcast.5, bf16[512,1024]{1,0:T(8,128)(2,1)} %get-tuple-element.45.refs_3_, ...), custom_call_target="tpu_custom_call", output_to_operand_aliasing={{0}: (11, {})} | custom-call | flops 8053063680 | bytes 10485760 | tf_op jit(solution)/shard_map/pairs/pallas_call | solution.py:174
  101.4 8.6 %collective-permute-done.5.refs_4_ = bf16[1024,512]{1,0:T(8,128)(2,1)S(1)} collective-permute-done((bf16[1024,512]{1,0:T(8,128)(2,1)}, bf16[1024,512]{1,0:T(8,128)(2,1)S(1)}, u32[]{:S(2)}, u32[]{:S(2)}) %collective-permute-start.5) | collective-permute-done | bytes 1048608 | tf_op jit(solution)/shard_map/ppermute | solution.py:230
  110.0 0.0 collective-permute-done.6.refs_5_
  110.0 0.1 broadcast_select_fusion
  110.2 0.0 copy-done.9
  110.2 0.1 collective-permute-start.9
  110.3 2.4 %pairs.7.refs_5_ = f32[512,512]{1,0:T(8,128)S(1)} custom-call(f32[128]{0:T(128)S(1)} %copy-done.2, f32[512,128]{1,0:T(8,128)S(1)} %get-tuple-element.30.refs_1_, f32[1,512]{1,0:T(1,128)S(1)} %bitcast.6, bf16[512,1024]{1,0:T(8,128)(2,1)S(1)} %collective-permute-done.1.refs_4_.refs_3_, ...), custom_call_target="tpu_custom_call", output_to_operand_aliasing={{}: (6, {})} | custom-call | flops 1610612736 | bytes 2097152 | tf_op jit(solution)/shard_map/pairs/pallas_call | solution.py:174
  112.6 0.3 collective-permute-done.9.refs_4_.refs_6_
  112.9 2.0 %pairs.8 = (f32[256,512]{1,0:T(8,128)S(1)}, bf16[256,512]{1,0:T(8,128)(2,1)S(1)}) custom-call(f32[128]{0:T(128)S(1)} %copy-done.2, f32[512,128]{1,0:T(8,128)S(1)} %get-tuple-element.30.refs_1_, f32[1,512]{1,0:T(1,128)S(1)} %bitcast.7, bf16[512,1024]{1,0:T(8,128)(2,1)S(1)} %collective-permute-done.1.refs_4_.refs_3_, ...), custom_call_target="tpu_custom_call" | custom-call | flops 805306368 | bytes 1048576 | tf_op jit(solution)/shard_map/pairs/pallas_call | solution.py:174
  114.9 0.3 collective-permute-start.10
  115.2 0.0 copy-done.10
  115.2 4.0 %pairs.9 = (f32[256,512]{1,0:T(8,128)S(1)}, bf16[128,512]{1,0:T(8,128)(2,1)S(1)}, bf16[128,512]{1,0:T(8,128)(2,1)S(1)}) custom-call(f32[128]{0:T(128)S(1)} %copy-done.2, f32[512,128]{1,0:T(8,128)S(1)} %get-tuple-element.30.refs_1_, f32[1,512]{1,0:T(1,128)S(1)} %bitcast.8, bf16[512,1024]{1,0:T(8,128)(2,1)} %get-tuple-element.45.refs_3_, ...), custom_call_target="tpu_custom_call" | custom-call | flops 2415919104 | bytes 3145728 | tf_op jit(solution)/shard_map/pairs/pallas_call | solution.py:174
  119.2 2.1 %collective-permute-start.11 = (bf16[128,512]{1,0:T(8,128)(2,1)S(1)}, bf16[128,512]{1,0:T(8,128)(2,1)S(1)}, u32[]{:S(2)}, u32[]{:S(2)}) collective-permute-start(bf16[128,512]{1,0:T(8,128)(2,1)S(1)} %get-tuple-element.49), channel_id=1, source_target_pairs={{0,1},{1,0},{2,3},{3,2},{4,5},{5,4},{6,7},{7,6},{8,9},{9,8},{10,11... | collective-permute-start | bytes 393224 | tf_op jit(solution)/shard_map/ppermute | solution.py:236
  121.3 0.1 collective-permute-start.12
  121.4 5.7 %collective-permute-done.11.refs_1_ = bf16[128,512]{1,0:T(8,128)(2,1)S(1)} collective-permute-done((bf16[128,512]{1,0:T(8,128)(2,1)S(1)}, bf16[128,512]{1,0:T(8,128)(2,1)S(1)}, u32[]{:S(2)}, u32[]{:S(2)}) %collective-permute-start.11) | collective-permute-done | bytes 131104 | tf_op jit(solution)/shard_map/ppermute | solution.py:236
  127.1 2.1 %collective-permute-done.12.refs_2_ = bf16[128,512]{1,0:T(8,128)(2,1)S(1)} collective-permute-done((bf16[128,512]{1,0:T(8,128)(2,1)S(1)}, bf16[128,512]{1,0:T(8,128)(2,1)S(1)}, u32[]{:S(2)}, u32[]{:S(2)}) %collective-permute-start.12) | collective-permute-done | bytes 131104 | tf_op jit(solution)/shard_map/ppermute | solution.py:236
  129.2 0.0 collective-permute-done.10.refs_0_
  129.2 1.1 finish.1
  (11 shorter events, 0.0 us)
Async XLA Ops:
  7.1 11.2 %copy-start = (bf16[384,512]{1,0:T(8,128)(2,1)S(1)}, bf16[384,512]{1,0:T(8,128)(2,1)}, u32[]{:S(2)}) copy-start(bf16[384,512]{1,0:T(8,128)(2,1)} %vir_ref.1) | copy-start | bytes 1179652
  7.1 38.3 %copy-start.1 = (f32[512]{0:T(512)S(1)}, f32[512]{0:T(512)}, u32[]{:S(2)}) copy-start(f32[512]{0:T(512)} %param.9) | copy-start | bytes 6148
  7.1 38.3 %all-to-all-start = ((bf16[128,16,384]{2,1,0:T(8,128)(2,1)}), bf16[128,16,384]{2,1,0:T(8,128)(2,1)S(1)}, u32[]{:S(2)}, u32[]{:S(2)}) async-start(bf16[128,16,384]{2,1,0:T(8,128)(2,1)} %transform.1), calls=%async_computation | async-start | bytes 3145728 | tf_op jit(solution)/shard_map/all_to_all | solution.py:242
  18.3 36.9 %copy-start.2 = (f32[128]{0:T(128)S(1)}, f32[128]{0:T(128)}, u32[]{:S(2)}) copy-start(f32[128]{0:T(128)} %refs_0_.11) | copy-start | bytes 1540
  18.3 27.1 %collective-permute-start = (bf16[384,512]{1,0:T(8,128)(2,1)S(1)}, bf16[384,512]{1,0:T(8,128)(2,1)S(1)}, u32[]{:S(2)}, u32[]{:S(2)}) collective-permute-start(bf16[384,512]{1,0:T(8,128)(2,1)S(1)} %copy-done), channel_id=1, source_target_pairs={{0,1},{1,0},{2,3},{3,2},{4,5},{5,4},{6,7},{7,6},{8,9},{9,8},{10,11... | collective-permute-start | bytes 1179656 | tf_op jit(solution)/shard_map/ppermute | solution.py:236
  47.7 11.2 %copy-start.3 = (bf16[1024,512]{1,0:T(8,128)(2,1)}, bf16[1024,512]{1,0:T(8,128)(2,1)S(1)}, u32[]{:S(2)}) copy-start(bf16[1024,512]{1,0:T(8,128)(2,1)S(1)} %get-tuple-element.32.refs_4_.refs_5_) | copy-start | bytes 3145732
  47.7 7.5 %collective-permute-start.4 = (bf16[1024,512]{1,0:T(8,128)(2,1)S(1)}, bf16[1024,512]{1,0:T(8,128)(2,1)S(1)}, u32[]{:S(2)}, u32[]{:S(2)}) collective-permute-start(bf16[1024,512]{1,0:T(8,128)(2,1)S(1)} %get-tuple-element.32.refs_4_.refs_5_), channel_id=1, source_target_pairs={{2,0},{0,2},{6,4},{4,6},{10,8},{8,10},{14,12},{12,14},{18,16},{16,... | collective-permute-start | bytes 3145736 | tf_op jit(solution)/shard_map/ppermute | solution.py:233
  47.7 31.1 %collective-permute-start.2 = (bf16[1024,512]{1,0:T(8,128)(2,1)S(1)}, bf16[1024,512]{1,0:T(8,128)(2,1)}, u32[]{:S(2)}, u32[]{:S(2)}) collective-permute-start(bf16[1024,512]{1,0:T(8,128)(2,1)S(1)} %get-tuple-element.32.refs_4_.refs_5_), channel_id=1, source_target_pairs={{125,0},{124,1},{127,2},{126,3},{0,4},{1,5},{2,6},{3,7},{4,8},{5,9... | collective-permute-start | bytes 3145736 | tf_op jit(solution)/shard_map/ppermute | solution.py:230
  49.2 29.6 %collective-permute-start.3 = (bf16[1024,512]{1,0:T(8,128)(2,1)S(1)}, bf16[1024,512]{1,0:T(8,128)(2,1)}, u32[]{:S(2)}, u32[]{:S(2)}) collective-permute-start(bf16[1024,512]{1,0:T(8,128)(2,1)S(1)} %get-tuple-element.32.refs_4_.refs_5_), channel_id=1, source_target_pairs={{4,0},{5,1},{6,2},{7,3},{8,4},{9,5},{10,6},{11,7},{12,8},{13,9},{1... | collective-permute-start | bytes 3145736 | tf_op jit(solution)/shard_map/ppermute | solution.py:230
  55.2 31.6 %collective-permute-start.1 = (bf16[512,1024]{1,0:T(8,128)(2,1)}, bf16[512,1024]{1,0:T(8,128)(2,1)S(1)}, u32[]{:S(2)}, u32[]{:S(2)}) collective-permute-start(bf16[512,1024]{1,0:T(8,128)(2,1)} %get-tuple-element.45.refs_3_), channel_id=1, source_target_pairs={{0,1},{1,0},{2,3},{3,2},{4,5},{5,4},{6,7},{7,6},{8,9},{9,8},{10,11... | collective-permute-start | bytes 3145736 | tf_op jit(solution)/shard_map/ppermute | solution.py:236
  55.2 3.7 %copy-start.5 = (bf16[1024,512]{1,0:T(8,128)(2,1)}, bf16[1024,512]{1,0:T(8,128)(2,1)S(1)}, u32[]{:S(2)}) copy-start(bf16[1024,512]{1,0:T(8,128)(2,1)S(1)} %collective-permute-done.4.refs_5_.refs_6_) | copy-start | bytes 3145732
  58.9 1.0 copy-start.7
  78.8 8.0 %collective-permute-start.7 = (bf16[1024,512]{1,0:T(8,128)(2,1)}, bf16[1024,512]{1,0:T(8,128)(2,1)}, u32[]{:S(2)}, u32[]{:S(2)}) collective-permute-start(bf16[1024,512]{1,0:T(8,128)(2,1)} %collective-permute-done.2.refs_7_), channel_id=1, source_target_pairs={{2,0},{0,2},{6,4},{4,6},{10,8},{8,10},{14,12},{12,14},{18,16},{16,... | collective-permute-start | bytes 3145736 | tf_op jit(solution)/shard_map/ppermute | solution.py:233
  78.8 8.0 %collective-permute-start.8 = (bf16[1024,512]{1,0:T(8,128)(2,1)}, bf16[1024,512]{1,0:T(8,128)(2,1)}, u32[]{:S(2)}, u32[]{:S(2)}) collective-permute-start(bf16[1024,512]{1,0:T(8,128)(2,1)} %collective-permute-done.3.refs_8_), channel_id=1, source_target_pairs={{2,0},{0,2},{6,4},{4,6},{10,8},{8,10},{14,12},{12,14},{18,16},{16,... | collective-permute-start | bytes 3145736 | tf_op jit(solution)/shard_map/ppermute | solution.py:233
  79.3 30.7 %collective-permute-start.5 = (bf16[1024,512]{1,0:T(8,128)(2,1)}, bf16[1024,512]{1,0:T(8,128)(2,1)S(1)}, u32[]{:S(2)}, u32[]{:S(2)}) collective-permute-start(bf16[1024,512]{1,0:T(8,128)(2,1)} %collective-permute-done.2.refs_7_), channel_id=1, source_target_pairs={{125,0},{124,1},{127,2},{126,3},{0,4},{1,5},{2,6},{3,7},{4,8},{5,9... | collective-permute-start | bytes 3145736 | tf_op jit(solution)/shard_map/ppermute | solution.py:230
  79.3 30.7 %collective-permute-start.6 = (bf16[1024,512]{1,0:T(8,128)(2,1)}, bf16[1024,512]{1,0:T(8,128)(2,1)S(1)}, u32[]{:S(2)}, u32[]{:S(2)}) collective-permute-start(bf16[1024,512]{1,0:T(8,128)(2,1)} %collective-permute-done.3.refs_8_), channel_id=1, source_target_pairs={{4,0},{5,1},{6,2},{7,3},{8,4},{9,5},{10,6},{11,7},{12,8},{13,9},{1... | collective-permute-start | bytes 3145736 | tf_op jit(solution)/shard_map/ppermute | solution.py:230
  86.8 1.2 copy-start.4
  88.0 1.2 copy-start.6
  89.2 1.2 copy-start.8
  101.4 8.7 %copy-start.9 = (f32[512,512]{1,0:T(8,128)}, f32[512,512]{1,0:T(8,128)S(1)}, u32[]{:S(2)}) copy-start(f32[512,512]{1,0:T(8,128)S(1)} %get-tuple-element.46.refs_7_) | copy-start | bytes 3145732
  110.2 2.7 %collective-permute-start.9 = (bf16[1024,512]{1,0:T(8,128)(2,1)S(1)}, bf16[1024,512]{1,0:T(8,128)(2,1)S(1)}, u32[]{:S(2)}, u32[]{:S(2)}) collective-permute-start(bf16[1024,512]{1,0:T(8,128)(2,1)S(1)} %broadcast_select_fusion), channel_id=1, source_target_pairs={{2,0},{0,2},{6,4},{4,6},{10,8},{8,10},{14,12},{12,14},{18,16},{16,... | collective-permute-start | bytes 3145736 | tf_op jit(solution)/shard_map/ppermute | solution.py:233
  112.6 2.5 %copy-start.10 = (f32[512,512]{1,0:T(8,128)S(1)}, f32[512,512]{1,0:T(8,128)}, u32[]{:S(2)}) copy-start(f32[512,512]{1,0:T(8,128)} %copy-done.9) | copy-start | bytes 3145732
  114.9 14.4 %collective-permute-start.10 = (bf16[256,512]{1,0:T(8,128)(2,1)S(1)}, bf16[256,512]{1,0:T(8,128)(2,1)S(1)}, u32[]{:S(2)}, u32[]{:S(2)}) collective-permute-start(bf16[256,512]{1,0:T(8,128)(2,1)S(1)} %get-tuple-element.44), channel_id=1, source_target_pairs={{0,1},{1,0},{2,3},{3,2},{4,5},{5,4},{6,7},{7,6},{8,9},{9,8},{10,11... | collective-permute-start | bytes 786440 | tf_op jit(solution)/shard_map/ppermute | solution.py:236
  119.2 7.9 %collective-permute-start.11 = (bf16[128,512]{1,0:T(8,128)(2,1)S(1)}, bf16[128,512]{1,0:T(8,128)(2,1)S(1)}, u32[]{:S(2)}, u32[]{:S(2)}) collective-permute-start(bf16[128,512]{1,0:T(8,128)(2,1)S(1)} %get-tuple-element.49), channel_id=1, source_target_pairs={{0,1},{1,0},{2,3},{3,2},{4,5},{5,4},{6,7},{7,6},{8,9},{9,8},{10,11... | collective-permute-start | bytes 393224 | tf_op jit(solution)/shard_map/ppermute | solution.py:236
  121.3 7.9 %collective-permute-start.12 = (bf16[128,512]{1,0:T(8,128)(2,1)S(1)}, bf16[128,512]{1,0:T(8,128)(2,1)S(1)}, u32[]{:S(2)}, u32[]{:S(2)}) collective-permute-start(bf16[128,512]{1,0:T(8,128)(2,1)S(1)} %get-tuple-element.50), channel_id=1, source_target_pairs={{0,1},{1,0},{2,3},{3,2},{4,5},{5,4},{6,7},{7,6},{8,9},{9,8},{10,11... | collective-permute-start | bytes 393224 | tf_op jit(solution)/shard_map/ppermute | solution.py:236

commit v5 on v4

--- a/solution.py
+++ b/solution.py
@@ -64,7 +64,7 @@
     )(ints, occ_coef)
 
 
-def combine_kernel(in_ref, vir_ref, vir_other_ref, energy_ref, own_ref, turned_ref, column_ref):
+def combine_kernel(in_ref, vir_ref, vir_other_ref, energy_ref, own_ref, column_ref):
     side = lax.axis_index("ao")
     owners, halves, count, rows = in_ref.shape
     mine = in_ref[:, side].reshape(owners * count, rows)
@@ -72,7 +72,6 @@
     total = jnp.dot(mine, vir_ref[...], preferred_element_type=jnp.float32)
     total += jnp.dot(others, vir_other_ref[...], preferred_element_type=jnp.float32)
     own_ref[...] = total.astype(jnp.bfloat16)
-    turned_ref[...] = total.T.astype(jnp.bfloat16)
     column_ref[...] = jnp.broadcast_to(energy_ref[...], (LANES, energy_ref.shape[1])).T
 
 
@@ -83,10 +82,9 @@
     return pl.pallas_call(
         combine_kernel,
         in_specs=[whole] * 4,
-        out_specs=[whole] * 3,
+        out_specs=[whole] * 2,
         out_shape=[
             jax.ShapeDtypeStruct((naux, nvir), jnp.bfloat16),
-            jax.ShapeDtypeStruct((nvir, naux), jnp.bfloat16),
             jax.ShapeDtypeStruct((nvir, LANES), jnp.float32),
         ],
         compiler_params=params(16),
@@ -94,11 +92,16 @@
     )(arrived, vir, vir_other, vir_energy)
 
 
-def pair_kernel(sides, plan, started, last, aux_count, *refs):
+def pair_kernel(sides, plan, started, last, turn, aux_count, *refs):
     energy_ref, column_ref, row_ref, *refs = refs
-    turned_refs = dict(zip(sides, refs))
-    refs = refs[len(sides) :]
+    turned_refs = {}
+    if not turn:
+        turned_refs = dict(zip(sides, refs))
+        refs = refs[len(sides) :]
     visitor_refs, refs = refs[: len(plan)], refs[len(plan) :]
+    if turn:
+        turned_refs = {sides[0]: refs[-1]}
+        refs[-1][...] = visitor_refs[0][...].T
     started_refs = dict(zip(started, refs))
     refs = refs[len(started) :]
     block, side = lax.axis_index("aux"), lax.axis_index("ao")
@@ -151,11 +154,11 @@
                 start = start + rows
 
 
-def add_pairs(energies, turned, visitors, density, last=0):
-    sides, started = sorted(turned), sorted(density)
-    nvir, naux = turned[sides[0]].shape
+def add_pairs(energies, turned, visitors, density, last=0, turn=False):
+    sides, started = [0] if turn else sorted(turned), sorted(density)
+    naux, nvir = visitors[0][1].shape
     plan = [(d, w) for d, _, w in visitors]
-    operands = [*energies] + [turned[s] for s in sides] + [v for _, v, _ in visitors]
+    operands = [*energies] + ([] if turn else [turned[s] for s in sides]) + [v for _, v, _ in visitors]
     aliases = {}
     if not last:
         aliases = {len(operands) + n: sides.index(s) for n, s in enumerate(started)}
@@ -169,10 +172,11 @@
         scratch = [pltpu.VMEM((nvir, nvir), jnp.float32)]
     else:
         out_shape = [jax.ShapeDtypeStruct((nvir, nvir), jnp.float32)] * len(sides)
+        out_shape += [jax.ShapeDtypeStruct((nvir, naux), jnp.bfloat16)] * turn
         scratch = []
     pairs = sum(len(w) for _, w in plan)
     results = pl.pallas_call(
-        lambda *refs: pair_kernel(sides, plan, started, last, lax.axis_size("aux"), *refs),
+        lambda *refs: pair_kernel(sides, plan, started, last, turn, lax.axis_size("aux"), *refs),
         in_specs=specs,
         out_specs=[whole] * len(out_shape),
         out_shape=out_shape,
@@ -186,31 +190,38 @@
         ),
         name="pairs",
     )(*operands)
-    return results if last else dict(zip(sides, results))
-
-
-def finish_kernel(kept_own, kept_other, *refs):
-    *came_refs, out_ref = refs
+    return results if last or turn else dict(zip(sides, results))
+
+
+def finish_kernel(other, kept_ref, *refs):
+    came_refs, (out_ref, held_ref, semaphore) = refs[: len(refs) - 3 - other], refs[-3:]
     block, side = lax.axis_index("aux"), lax.axis_index("ao")
     parity = lax.rem(side + lax.rem(lax.div(block, ROW), 2), 2)
-    out_ref[parity] = kept_own[...] + came_refs[0][...].astype(jnp.float32)
     start = 0
-    for came_ref in came_refs[1:]:
+    for came_ref in came_refs:
         rows = came_ref.shape[0]
-        out_ref[1 - parity, start : start + rows] = kept_other[
-            start : start + rows
-        ] + came_ref[...].astype(jnp.float32)
+        here = slice(start, start + rows)
+        held_ref[here] = kept_ref[here] + came_ref[...].astype(jnp.float32)
         start += rows
-
-
-def finish(*operands):
-    rows, nvir = operands[0].shape
-    whole = pl.BlockSpec(memory_space=pltpu.VMEM)
+    target = out_ref.at[1 - parity if other else parity]
+    copy = pltpu.make_async_copy(held_ref, target, semaphore)
+    copy.start()
+    copy.wait()
+
+
+def finish(other, kept, came, output):
+    rows, nvir = kept.shape
+    whole, anywhere = pl.BlockSpec(memory_space=pltpu.VMEM), pl.BlockSpec(memory_space=pl.ANY)
+    operands, specs = [kept, *came], [whole] * (1 + len(came))
+    if other:
+        operands, specs = operands + [output], specs + [anywhere]
     return pl.pallas_call(
-        finish_kernel,
-        in_specs=[whole] * len(operands),
-        out_specs=whole,
+        lambda *refs: finish_kernel(other, *refs),
+        in_specs=specs,
+        out_specs=anywhere,
         out_shape=jax.ShapeDtypeStruct((2, rows, nvir), jnp.float32),
+        scratch_shapes=[pltpu.VMEM((rows, nvir), jnp.float32), pltpu.SemaphoreType.DMA],
+        input_output_aliases={len(operands) - 1: 0} if other else {},
         compiler_params=params(16),
         name="finish",
     )(*operands)
@@ -243,13 +254,14 @@
     arrived = arrived.reshape(aux_count, ao_count, *arrived.shape[1:])
     arrived, vir_other = hold((arrived, vir_other))
     row = vir_energy[None, :]
-    own, turned, column = combine(arrived, vir_coef, vir_other, row)
+    own, column = combine(arrived, vir_coef, vir_other, row)
     energies = (occ_energy, column, row)
 
     below, above = shifted(own, 2), shifted(own, -2)
-    neighbour, turned_other = across(own), over(turned)
+    neighbour = across(own)
     own_pairs = [((0, 0), own), ((1, -1), neighbour)]
-    mine = add_pairs(energies, {0: turned}, [(*v, (0,)) for v in own_pairs], {})
+    mine, turned = add_pairs(energies, {}, [(*v, (0,)) for v in own_pairs], {}, turn=True)
+    mine, turned_other = {0: mine}, over(turned)
     below, above, mine = hold((below, above, mine))
     far_below, far_above = shifted(below, 2), shifted(above, -2)
     next_below, next_above = across(below), across(above)
@@ -274,7 +286,10 @@
     kept_own, *sent = add_pairs(
         energies, {0: turned}, [(*v, (0,)) for v in far + final], {0: density[0]}, last=2
     )
-    return finish(kept_own, kept_other, came_own, *[over(piece) for piece in sent])
+    came_other = [over(piece) for piece in sent]
+    output = finish(0, kept_own, [came_own], None)
+    came_other, output = hold((came_other, output))
+    return finish(1, kept_other, came_other, output)
 
 
 def solution(mesh):

time: 131 us -> 130 us (level)
  Pallas kernels: 33.5 us -> 32 us
    pallas_call x6 -> x7, Pallas kernels: 24.1 us -> 23.7 us  [the longest x5 21.9 us: add_pairs(): pl.pallas_call(lambda *refs: pair_kernel(sides, plan, started, last, turn...]
  transfers between devices with their start and end apart: 14 -> 14, of which waited for: 6 -> 7; matrix products, arithmetic and copies ran while one was open for 0% -> 0% of each run, Pallas kernels for 16% -> 16%
where the time goes in v5:
time: 130 us; the launch traced here: 129 us
  waiting for transfers between devices  60.8 us (47%)
  Pallas kernels  32 us (25%)
  starting transfers between devices  30.4 us (23%)
  local copies, waits for them, and re-layouts  5.62 us (4%)
    ppermute x5, waiting for transfers between devices, over(): return lax.ppermute(value, 'ao', SWAP)  32.9 us
    ppermute x4, waiting for transfers between devices, shifted(): return lax.ppermute(value, BOTH, route)  27.6 us
    pallas_call x5, Pallas kernels, add_pairs(): pl.pallas_call(lambda *refs: pair_kernel(sides, plan, started, last, turn...  21.9 us
    ppermute x4, starting transfers between devices, shifted(): return lax.ppermute(value, BOTH, route)  15 us
    all_to_all x1, starting transfers between devices, shards(): lax.all_to_all(tiles, BOTH, split_axis=0, concat_axis=0, tiled=True)  11.1 us
    pallas_call x1, Pallas kernels, transform(): pl.pallas_call(lambda *refs: transform_kernel(slots, group, *refs), grid=...  7.1 us
    unnamed x22, local copies, waits for them, and re-layouts  5.62 us
    ppermute x5, starting transfers between devices, over(): return lax.ppermute(value, 'ao', SWAP)  3.64 us
  transfers between devices with their start and end apart: 14, of which 7 were waited for; matrix products, arithmetic and copies ran while one was open for 0% of the time, Pallas kernels for 16%

profile of v5, /device:TPU:0, one launch (start us, length us, event | category | flops | bytes accessed | tf_op | source)
XLA Modules:
  0.0 129.3 jit_solution(16019845937111787379)
XLA Ops:
  0.0 7.1 %transform.1 = bf16[128,16,384]{2,1,0:T(8,128)(2,1)} custom-call(bf16[16,384,768]{2,1,0:T(8,128)(2,1)} %refs_0_.6, bf16[768,128]{1,0:T(8,128)(2,1)} %refs_1_.1), custom_call_target="tpu_custom_call" | custom-call | tf_op jit(solution)/shard_map/transform/pallas_call | solution.py:52
  7.1 11.1 %all-to-all-start = ((bf16[128,16,384]{2,1,0:T(8,128)(2,1)}), bf16[128,16,384]{2,1,0:T(8,128)(2,1)S(1)}, u32[]{:S(2)}, u32[]{:S(2)}) async-start(bf16[128,16,384]{2,1,0:T(8,128)(2,1)} %transform.1), calls=%async_computation | async-start | bytes 3145728 | tf_op jit(solution)/shard_map/all_to_all | solution.py:253
  18.3 0.0 copy-done
  18.3 0.0 copy-start.2
  18.3 1.2 collective-permute-start
  19.4 25.9 %collective-permute-done.vir_other_ref = bf16[384,512]{1,0:T(8,128)(2,1)S(1)} collective-permute-done((bf16[384,512]{1,0:T(8,128)(2,1)S(1)}, bf16[384,512]{1,0:T(8,128)(2,1)S(1)}, u32[]{:S(2)}, u32[]{:S(2)}) %collective-permute-start) | collective-permute-done | bytes 393248 | tf_op jit(solution)/shard_map/ppermute | solution.py:247
  45.4 0.0 all-to-all-done
  45.4 0.0 copy-done.1
  45.4 1.2 combine.1
  46.6 0.1 collective-permute-start.1
  46.7 1.5 %collective-permute-start.3 = (bf16[1024,512]{1,0:T(8,128)(2,1)S(1)}, bf16[1024,512]{1,0:T(8,128)(2,1)}, u32[]{:S(2)}, u32[]{:S(2)}) collective-permute-start(bf16[1024,512]{1,0:T(8,128)(2,1)S(1)} %get-tuple-element.35.refs_3_.refs_5_), channel_id=1, source_target_pairs={{125,0},{124,1},{127,2},{126,3},{0,4},{1,5},{2,6},{3,7},{4,8},{5,9... | collective-permute-start | bytes 3145736 | tf_op jit(solution)/shard_map/ppermute | solution.py:241
  48.3 6.0 %collective-permute-start.4 = (bf16[1024,512]{1,0:T(8,128)(2,1)S(1)}, bf16[1024,512]{1,0:T(8,128)(2,1)}, u32[]{:S(2)}, u32[]{:S(2)}) collective-permute-start(bf16[1024,512]{1,0:T(8,128)(2,1)S(1)} %get-tuple-element.35.refs_3_.refs_5_), channel_id=1, source_target_pairs={{4,0},{5,1},{6,2},{7,3},{8,4},{9,5},{10,6},{11,7},{12,8},{13,9},{1... | collective-permute-start | bytes 3145736 | tf_op jit(solution)/shard_map/ppermute | solution.py:241
  54.3 0.0 collective-permute-done.1.refs_4_.refs_6_
  54.3 0.0 copy-done.2
  54.3 2.6 %pairs.5 = (f32[512,512]{1,0:T(8,128)S(1)}, bf16[512,1024]{1,0:T(8,128)(2,1)}) custom-call(f32[128]{0:T(128)S(1)} %copy-done.2, f32[512,128]{1,0:T(8,128)S(1)} %get-tuple-element.34.refs_1_, f32[1,512]{1,0:T(1,128)S(1)} %bitcast.4, bf16[1024,512]{1,0:T(8,128)(2,1)S(1)} %get-tuple-element.35.refs_3_.refs_5_, ...), custom_call_target="tpu_custom_call" | custom-call | flops 1610612736 | bytes 2097152 | tf_op jit(solution)/shard_map/pairs/pallas_call | solution.py:178
  56.9 0.9 copy-done.7
  57.9 0.0 collective-permute-start.2
  57.9 19.9 %collective-permute-done.3.refs_7_ = bf16[1024,512]{1,0:T(8,128)(2,1)} collective-permute-done((bf16[1024,512]{1,0:T(8,128)(2,1)S(1)}, bf16[1024,512]{1,0:T(8,128)(2,1)}, u32[]{:S(2)}, u32[]{:S(2)}) %collective-permute-start.3) | collective-permute-done | bytes 1048608 | tf_op jit(solution)/shard_map/ppermute | solution.py:241
  77.8 0.0 collective-permute-done.4.refs_8_
  77.8 0.0 collective-permute-start.7
  77.8 0.5 collective-permute-start.8
  78.4 0.0 collective-permute-start.5
  78.4 7.5 %collective-permute-start.6 = (bf16[1024,512]{1,0:T(8,128)(2,1)}, bf16[1024,512]{1,0:T(8,128)(2,1)S(1)}, u32[]{:S(2)}, u32[]{:S(2)}) collective-permute-start(bf16[1024,512]{1,0:T(8,128)(2,1)} %collective-permute-done.4.refs_8_), channel_id=1, source_target_pairs={{4,0},{5,1},{6,2},{7,3},{8,4},{9,5},{10,6},{11,7},{12,8},{13,9},{1... | collective-permute-start | bytes 3145736 | tf_op jit(solution)/shard_map/ppermute | solution.py:241
  85.8 0.0 collective-permute-done.2.refs_4_.refs_3_
  85.8 0.0 collective-permute-done.7.refs_9_
  85.8 0.0 collective-permute-done.8.refs_10_
  85.8 1.2 copy-done.4
  87.1 1.2 copy-done.6
  88.3 1.2 copy-done.8
  89.5 10.9 %pairs.6 = (f32[512,512]{1,0:T(8,128)S(1)}, f32[512,512]{1,0:T(8,128)S(1)}) custom-call(f32[128]{0:T(128)S(1)} %copy-done.2, f32[512,128]{1,0:T(8,128)S(1)} %get-tuple-element.34.refs_1_, f32[1,512]{1,0:T(1,128)S(1)} %bitcast.5, bf16[512,1024]{1,0:T(8,128)(2,1)} %get-tuple-element.51.refs_3_, ...), custom_call_target="tpu_custom_call", output_to_operand_aliasing={{0}: (11, {})} | custom-call | flops 8053063680 | bytes 10485760 | tf_op jit(solution)/shard_map/pairs/pallas_call | solution.py:178
  100.5 1.0 copy-done.9
  101.4 7.6 %collective-permute-done.5.refs_4_ = bf16[1024,512]{1,0:T(8,128)(2,1)S(1)} collective-permute-done((bf16[1024,512]{1,0:T(8,128)(2,1)}, bf16[1024,512]{1,0:T(8,128)(2,1)S(1)}, u32[]{:S(2)}, u32[]{:S(2)}) %collective-permute-start.5) | collective-permute-done | bytes 1048608 | tf_op jit(solution)/shard_map/ppermute | solution.py:241
  109.1 0.0 collective-permute-done.6.refs_5_
  109.1 0.1 broadcast_select_fusion
  109.2 0.1 collective-permute-start.9
  109.3 2.4 %pairs.7.refs_5_ = f32[512,512]{1,0:T(8,128)S(1)} custom-call(f32[128]{0:T(128)S(1)} %copy-done.2, f32[512,128]{1,0:T(8,128)S(1)} %get-tuple-element.34.refs_1_, f32[1,512]{1,0:T(1,128)S(1)} %bitcast.6, bf16[512,1024]{1,0:T(8,128)(2,1)S(1)} %collective-permute-done.2.refs_4_.refs_3_, ...), custom_call_target="tpu_custom_call", output_to_operand_aliasing={{}: (6, {})} | custom-call | flops 1610612736 | bytes 2097152 | tf_op jit(solution)/shard_map/pairs/pallas_call | solution.py:178
  111.7 0.0 copy-start.10
  111.7 0.3 collective-permute-done.9.refs_4_.refs_6_
  111.9 2.0 %pairs.8 = (f32[256,512]{1,0:T(8,128)S(1)}, bf16[256,512]{1,0:T(8,128)(2,1)S(1)}) custom-call(f32[128]{0:T(128)S(1)} %copy-done.2, f32[512,128]{1,0:T(8,128)S(1)} %get-tuple-element.34.refs_1_, f32[1,512]{1,0:T(1,128)S(1)} %bitcast.7, bf16[512,1024]{1,0:T(8,128)(2,1)S(1)} %collective-permute-done.2.refs_4_.refs_3_, ...), custom_call_target="tpu_custom_call" | custom-call | flops 805306368 | bytes 1048576 | tf_op jit(solution)/shard_map/pairs/pallas_call | solution.py:178
  113.9 0.3 collective-permute-start.12
  114.2 4.0 %pairs.9 = (f32[256,512]{1,0:T(8,128)S(1)}, bf16[128,512]{1,0:T(8,128)(2,1)S(1)}, bf16[128,512]{1,0:T(8,128)(2,1)S(1)}) custom-call(f32[128]{0:T(128)S(1)} %copy-done.2, f32[512,128]{1,0:T(8,128)S(1)} %get-tuple-element.34.refs_1_, f32[1,512]{1,0:T(1,128)S(1)} %bitcast.8, bf16[512,1024]{1,0:T(8,128)(2,1)} %get-tuple-element.51.refs_3_, ...), custom_call_target="tpu_custom_call" | custom-call | flops 2415919104 | bytes 3145728 | tf_op jit(solution)/shard_map/pairs/pallas_call | solution.py:178
  118.2 2.1 %collective-permute-start.10 = (bf16[128,512]{1,0:T(8,128)(2,1)S(1)}, bf16[128,512]{1,0:T(8,128)(2,1)S(1)}, u32[]{:S(2)}, u32[]{:S(2)}) collective-permute-start(bf16[128,512]{1,0:T(8,128)(2,1)S(1)} %get-tuple-element.53), channel_id=1, source_target_pairs={{0,1},{1,0},{2,3},{3,2},{4,5},{5,4},{6,7},{7,6},{8,9},{9,8},{10,11... | collective-permute-start | bytes 393224 | tf_op jit(solution)/shard_map/ppermute | solution.py:247
  120.3 0.1 collective-permute-start.11
  120.4 2.9 %collective-permute-done.12.refs_1_ = bf16[256,512]{1,0:T(8,128)(2,1)S(1)} collective-permute-done((bf16[256,512]{1,0:T(8,128)(2,1)S(1)}, bf16[256,512]{1,0:T(8,128)(2,1)S(1)}, u32[]{:S(2)}, u32[]{:S(2)}) %collective-permute-start.12) | collective-permute-done | bytes 262176 | tf_op jit(solution)/shard_map/ppermute | solution.py:247
  123.3 0.8 finish.2.refs_3_
  124.2 2.0 %collective-permute-done.10.refs_1_ = bf16[128,512]{1,0:T(8,128)(2,1)S(1)} collective-permute-done((bf16[128,512]{1,0:T(8,128)(2,1)S(1)}, bf16[128,512]{1,0:T(8,128)(2,1)S(1)}, u32[]{:S(2)}, u32[]{:S(2)}) %collective-permute-start.10) | collective-permute-done | bytes 131104 | tf_op jit(solution)/shard_map/ppermute | solution.py:247
  126.1 2.1 %collective-permute-done.11.refs_2_ = bf16[128,512]{1,0:T(8,128)(2,1)S(1)} collective-permute-done((bf16[128,512]{1,0:T(8,128)(2,1)S(1)}, bf16[128,512]{1,0:T(8,128)(2,1)S(1)}, u32[]{:S(2)}, u32[]{:S(2)}) %collective-permute-start.11) | collective-permute-done | bytes 131104 | tf_op jit(solution)/shard_map/ppermute | solution.py:247
  128.3 0.9 finish.3
  (12 shorter events, 0.0 us)
Async XLA Ops:
  7.1 11.2 %copy-start = (bf16[384,512]{1,0:T(8,128)(2,1)S(1)}, bf16[384,512]{1,0:T(8,128)(2,1)}, u32[]{:S(2)}) copy-start(bf16[384,512]{1,0:T(8,128)(2,1)} %vir_ref.1) | copy-start | bytes 1179652
  7.1 38.3 %copy-start.1 = (f32[512]{0:T(512)S(1)}, f32[512]{0:T(512)}, u32[]{:S(2)}) copy-start(f32[512]{0:T(512)} %param.9) | copy-start | bytes 6148
  7.1 38.3 %all-to-all-start = ((bf16[128,16,384]{2,1,0:T(8,128)(2,1)}), bf16[128,16,384]{2,1,0:T(8,128)(2,1)S(1)}, u32[]{:S(2)}, u32[]{:S(2)}) async-start(bf16[128,16,384]{2,1,0:T(8,128)(2,1)} %transform.1), calls=%async_computation | async-start | bytes 3145728 | tf_op jit(solution)/shard_map/all_to_all | solution.py:253
  18.3 36.0 %copy-start.2 = (f32[128]{0:T(128)S(1)}, f32[128]{0:T(128)}, u32[]{:S(2)}) copy-start(f32[128]{0:T(128)} %refs_0_.11) | copy-start | bytes 1540
  18.3 27.1 %collective-permute-start = (bf16[384,512]{1,0:T(8,128)(2,1)S(1)}, bf16[384,512]{1,0:T(8,128)(2,1)S(1)}, u32[]{:S(2)}, u32[]{:S(2)}) collective-permute-start(bf16[384,512]{1,0:T(8,128)(2,1)S(1)} %copy-done), channel_id=1, source_target_pairs={{0,1},{1,0},{2,3},{3,2},{4,5},{5,4},{6,7},{7,6},{8,9},{9,8},{10,11... | collective-permute-start | bytes 1179656 | tf_op jit(solution)/shard_map/ppermute | solution.py:247
  46.6 10.3 %copy-start.3 = (bf16[1024,512]{1,0:T(8,128)(2,1)}, bf16[1024,512]{1,0:T(8,128)(2,1)S(1)}, u32[]{:S(2)}) copy-start(bf16[1024,512]{1,0:T(8,128)(2,1)S(1)} %get-tuple-element.35.refs_3_.refs_5_) | copy-start | bytes 3145732
  46.6 7.6 %collective-permute-start.1 = (bf16[1024,512]{1,0:T(8,128)(2,1)S(1)}, bf16[1024,512]{1,0:T(8,128)(2,1)S(1)}, u32[]{:S(2)}, u32[]{:S(2)}) collective-permute-start(bf16[1024,512]{1,0:T(8,128)(2,1)S(1)} %get-tuple-element.35.refs_3_.refs_5_), channel_id=1, source_target_pairs={{2,0},{0,2},{6,4},{4,6},{10,8},{8,10},{14,12},{12,14},{18,16},{16,... | collective-permute-start | bytes 3145736 | tf_op jit(solution)/shard_map/ppermute | solution.py:244
  46.7 31.1 %collective-permute-start.3 = (bf16[1024,512]{1,0:T(8,128)(2,1)S(1)}, bf16[1024,512]{1,0:T(8,128)(2,1)}, u32[]{:S(2)}, u32[]{:S(2)}) collective-permute-start(bf16[1024,512]{1,0:T(8,128)(2,1)S(1)} %get-tuple-element.35.refs_3_.refs_5_), channel_id=1, source_target_pairs={{125,0},{124,1},{127,2},{126,3},{0,4},{1,5},{2,6},{3,7},{4,8},{5,9... | collective-permute-start | bytes 3145736 | tf_op jit(solution)/shard_map/ppermute | solution.py:241
  48.3 29.6 %collective-permute-start.4 = (bf16[1024,512]{1,0:T(8,128)(2,1)S(1)}, bf16[1024,512]{1,0:T(8,128)(2,1)}, u32[]{:S(2)}, u32[]{:S(2)}) collective-permute-start(bf16[1024,512]{1,0:T(8,128)(2,1)S(1)} %get-tuple-element.35.refs_3_.refs_5_), channel_id=1, source_target_pairs={{4,0},{5,1},{6,2},{7,3},{8,4},{9,5},{10,6},{11,7},{12,8},{13,9},{1... | collective-permute-start | bytes 3145736 | tf_op jit(solution)/shard_map/ppermute | solution.py:241
  54.3 2.7 %copy-start.5 = (bf16[1024,512]{1,0:T(8,128)(2,1)}, bf16[1024,512]{1,0:T(8,128)(2,1)S(1)}, u32[]{:S(2)}) copy-start(bf16[1024,512]{1,0:T(8,128)(2,1)S(1)} %collective-permute-done.1.refs_4_.refs_6_) | copy-start | bytes 3145732
  56.9 1.0 copy-start.7
  57.9 27.9 %collective-permute-start.2 = (bf16[512,1024]{1,0:T(8,128)(2,1)}, bf16[512,1024]{1,0:T(8,128)(2,1)S(1)}, u32[]{:S(2)}, u32[]{:S(2)}) collective-permute-start(bf16[512,1024]{1,0:T(8,128)(2,1)} %get-tuple-element.51.refs_3_), channel_id=1, source_target_pairs={{0,1},{1,0},{2,3},{3,2},{4,5},{5,4},{6,7},{7,6},{8,9},{9,8},{10,11... | collective-permute-start | bytes 3145736 | tf_op jit(solution)/shard_map/ppermute | solution.py:247
  77.8 8.0 %collective-permute-start.7 = (bf16[1024,512]{1,0:T(8,128)(2,1)}, bf16[1024,512]{1,0:T(8,128)(2,1)}, u32[]{:S(2)}, u32[]{:S(2)}) collective-permute-start(bf16[1024,512]{1,0:T(8,128)(2,1)} %collective-permute-done.3.refs_7_), channel_id=1, source_target_pairs={{2,0},{0,2},{6,4},{4,6},{10,8},{8,10},{14,12},{12,14},{18,16},{16,... | collective-permute-start | bytes 3145736 | tf_op jit(solution)/shard_map/ppermute | solution.py:244
  77.8 8.0 %collective-permute-start.8 = (bf16[1024,512]{1,0:T(8,128)(2,1)}, bf16[1024,512]{1,0:T(8,128)(2,1)}, u32[]{:S(2)}, u32[]{:S(2)}) collective-permute-start(bf16[1024,512]{1,0:T(8,128)(2,1)} %collective-permute-done.4.refs_8_), channel_id=1, source_target_pairs={{2,0},{0,2},{6,4},{4,6},{10,8},{8,10},{14,12},{12,14},{18,16},{16,... | collective-permute-start | bytes 3145736 | tf_op jit(solution)/shard_map/ppermute | solution.py:244
  78.4 30.7 %collective-permute-start.5 = (bf16[1024,512]{1,0:T(8,128)(2,1)}, bf16[1024,512]{1,0:T(8,128)(2,1)S(1)}, u32[]{:S(2)}, u32[]{:S(2)}) collective-permute-start(bf16[1024,512]{1,0:T(8,128)(2,1)} %collective-permute-done.3.refs_7_), channel_id=1, source_target_pairs={{125,0},{124,1},{127,2},{126,3},{0,4},{1,5},{2,6},{3,7},{4,8},{5,9... | collective-permute-start | bytes 3145736 | tf_op jit(solution)/shard_map/ppermute | solution.py:241
  78.4 30.7 %collective-permute-start.6 = (bf16[1024,512]{1,0:T(8,128)(2,1)}, bf16[1024,512]{1,0:T(8,128)(2,1)S(1)}, u32[]{:S(2)}, u32[]{:S(2)}) collective-permute-start(bf16[1024,512]{1,0:T(8,128)(2,1)} %collective-permute-done.4.refs_8_), channel_id=1, source_target_pairs={{4,0},{5,1},{6,2},{7,3},{8,4},{9,5},{10,6},{11,7},{12,8},{13,9},{1... | collective-permute-start | bytes 3145736 | tf_op jit(solution)/shard_map/ppermute | solution.py:241
  85.8 1.2 copy-start.4
  87.1 1.2 copy-start.6
  88.3 1.2 copy-start.8
  100.5 1.0 copy-start.9
  109.2 2.7 %collective-permute-start.9 = (bf16[1024,512]{1,0:T(8,128)(2,1)S(1)}, bf16[1024,512]{1,0:T(8,128)(2,1)S(1)}, u32[]{:S(2)}, u32[]{:S(2)}) collective-permute-start(bf16[1024,512]{1,0:T(8,128)(2,1)S(1)} %broadcast_select_fusion), channel_id=1, source_target_pairs={{2,0},{0,2},{6,4},{4,6},{10,8},{8,10},{14,12},{12,14},{18,16},{16,... | collective-permute-start | bytes 3145736 | tf_op jit(solution)/shard_map/ppermute | solution.py:244
  111.7 2.5 %copy-start.10 = (f32[512,512]{1,0:T(8,128)S(1)}, f32[512,512]{1,0:T(8,128)}, u32[]{:S(2)}) copy-start(f32[512,512]{1,0:T(8,128)} %copy-done.9) | copy-start | bytes 3145732
  113.9 9.4 %collective-permute-start.12 = (bf16[256,512]{1,0:T(8,128)(2,1)S(1)}, bf16[256,512]{1,0:T(8,128)(2,1)S(1)}, u32[]{:S(2)}, u32[]{:S(2)}) collective-permute-start(bf16[256,512]{1,0:T(8,128)(2,1)S(1)} %get-tuple-element.50), channel_id=1, source_target_pairs={{0,1},{1,0},{2,3},{3,2},{4,5},{5,4},{6,7},{7,6},{8,9},{9,8},{10,11... | collective-permute-start | bytes 786440 | tf_op jit(solution)/shard_map/ppermute | solution.py:247
  118.2 7.9 %collective-permute-start.10 = (bf16[128,512]{1,0:T(8,128)(2,1)S(1)}, bf16[128,512]{1,0:T(8,128)(2,1)S(1)}, u32[]{:S(2)}, u32[]{:S(2)}) collective-permute-start(bf16[128,512]{1,0:T(8,128)(2,1)S(1)} %get-tuple-element.53), channel_id=1, source_target_pairs={{0,1},{1,0},{2,3},{3,2},{4,5},{5,4},{6,7},{7,6},{8,9},{9,8},{10,11... | collective-permute-start | bytes 393224 | tf_op jit(solution)/shard_map/ppermute | solution.py:247
  120.3 7.9 %collective-permute-start.11 = (bf16[128,512]{1,0:T(8,128)(2,1)S(1)}, bf16[128,512]{1,0:T(8,128)(2,1)S(1)}, u32[]{:S(2)}, u32[]{:S(2)}) collective-permute-start(bf16[128,512]{1,0:T(8,128)(2,1)S(1)} %get-tuple-element.54), channel_id=1, source_target_pairs={{0,1},{1,0},{2,3},{3,2},{4,5},{5,4},{6,7},{7,6},{8,9},{9,8},{10,11... | collective-permute-start | bytes 393224 | tf_op jit(solution)/shard_map/ppermute | solution.py:247

commit v6 on v5

--- a/solution.py
+++ b/solution.py
@@ -284,7 +284,7 @@
     came_own = over(sent)
     turned, sent = hold((turned, sent))
     kept_own, *sent = add_pairs(
-        energies, {0: turned}, [(*v, (0,)) for v in far + final], {0: density[0]}, last=2
+        energies, {0: turned}, [(*v, (0,)) for v in far + final], {0: density[0]}, last=1
     )
     came_other = [over(piece) for piece in sent]
     output = finish(0, kept_own, [came_own], None)

time: 130 us -> 130 us (level)
    ppermute x5 -> x4, waiting for transfers between devices: 32.9 us -> 33.1 us  [over(): return lax.ppermute(value, 'ao', SWAP)]
    ppermute x5 -> x4, starting transfers between devices: 3.64 us -> 3.55 us  [over(): return lax.ppermute(value, 'ao', SWAP)]
  transfers between devices with their start and end apart: 14 -> 13, of which waited for: 7 -> 6; matrix products, arithmetic and copies ran while one was open for 0% -> 0% of each run, Pallas kernels for 16% -> 16%
where the time goes in v6:
time: 130 us; the launch traced here: 129 us
  waiting for transfers between devices  60.9 us (47%)
  Pallas kernels  31.9 us (25%)
  starting transfers between devices  30.4 us (23%)
  local copies, waits for them, and re-layouts  5.62 us (4%)
    ppermute x4, waiting for transfers between devices, over(): return lax.ppermute(value, 'ao', SWAP)  33.1 us
    ppermute x4, waiting for transfers between devices, shifted(): return lax.ppermute(value, BOTH, route)  27.6 us
    pallas_call x5, Pallas kernels, add_pairs(): pl.pallas_call(lambda *refs: pair_kernel(sides, plan, started, last, turn...  21.9 us
    ppermute x4, starting transfers between devices, shifted(): return lax.ppermute(value, BOTH, route)  15 us
    all_to_all x1, starting transfers between devices, shards(): lax.all_to_all(tiles, BOTH, split_axis=0, concat_axis=0, tiled=True)  11.1 us
    pallas_call x1, Pallas kernels, transform(): pl.pallas_call(lambda *refs: transform_kernel(slots, group, *refs), grid=...  7.09 us
    unnamed x22, local copies, waits for them, and re-layouts  5.62 us
    ppermute x4, starting transfers between devices, over(): return lax.ppermute(value, 'ao', SWAP)  3.55 us
  transfers between devices with their start and end apart: 13, of which 6 were waited for; matrix products, arithmetic and copies ran while one was open for 0% of the time, Pallas kernels for 16%

profile of v6, /device:TPU:0, one launch (start us, length us, event | category | flops | bytes accessed | tf_op | source)
XLA Modules:
  0.0 129.3 jit_solution(12191063773170158366)
XLA Ops:
  0.0 7.1 %transform.1 = bf16[128,16,384]{2,1,0:T(8,128)(2,1)} custom-call(bf16[16,384,768]{2,1,0:T(8,128)(2,1)} %refs_0_.6, bf16[768,128]{1,0:T(8,128)(2,1)} %refs_1_.1), custom_call_target="tpu_custom_call" | custom-call | tf_op jit(solution)/shard_map/transform/pallas_call | solution.py:52
  7.1 11.1 %all-to-all-start = ((bf16[128,16,384]{2,1,0:T(8,128)(2,1)}), bf16[128,16,384]{2,1,0:T(8,128)(2,1)S(1)}, u32[]{:S(2)}, u32[]{:S(2)}) async-start(bf16[128,16,384]{2,1,0:T(8,128)(2,1)} %transform.1), calls=%async_computation | async-start | bytes 3145728 | tf_op jit(solution)/shard_map/all_to_all | solution.py:253
  18.2 0.0 copy-done
  18.3 0.0 copy-start.2
  18.3 1.2 collective-permute-start
  19.4 25.9 %collective-permute-done.vir_other_ref = bf16[384,512]{1,0:T(8,128)(2,1)S(1)} collective-permute-done((bf16[384,512]{1,0:T(8,128)(2,1)S(1)}, bf16[384,512]{1,0:T(8,128)(2,1)S(1)}, u32[]{:S(2)}, u32[]{:S(2)}) %collective-permute-start) | collective-permute-done | bytes 393248 | tf_op jit(solution)/shard_map/ppermute | solution.py:247
  45.4 0.0 all-to-all-done
  45.4 0.0 copy-done.1
  45.4 1.2 combine.1
  46.6 0.0 copy-start.3
  46.6 0.1 collective-permute-start.1
  46.7 1.5 %collective-permute-start.3 = (bf16[1024,512]{1,0:T(8,128)(2,1)S(1)}, bf16[1024,512]{1,0:T(8,128)(2,1)}, u32[]{:S(2)}, u32[]{:S(2)}) collective-permute-start(bf16[1024,512]{1,0:T(8,128)(2,1)S(1)} %get-tuple-element.33.refs_3_.refs_5_), channel_id=1, source_target_pairs={{125,0},{124,1},{127,2},{126,3},{0,4},{1,5},{2,6},{3,7},{4,8},{5,9... | collective-permute-start | bytes 3145736 | tf_op jit(solution)/shard_map/ppermute | solution.py:241
  48.3 6.0 %collective-permute-start.4 = (bf16[1024,512]{1,0:T(8,128)(2,1)S(1)}, bf16[1024,512]{1,0:T(8,128)(2,1)}, u32[]{:S(2)}, u32[]{:S(2)}) collective-permute-start(bf16[1024,512]{1,0:T(8,128)(2,1)S(1)} %get-tuple-element.33.refs_3_.refs_5_), channel_id=1, source_target_pairs={{4,0},{5,1},{6,2},{7,3},{8,4},{9,5},{10,6},{11,7},{12,8},{13,9},{1... | collective-permute-start | bytes 3145736 | tf_op jit(solution)/shard_map/ppermute | solution.py:241
  54.2 0.0 collective-permute-done.1.refs_4_.refs_6_
  54.2 0.0 copy-done.2
  54.2 2.6 %pairs.5 = (f32[512,512]{1,0:T(8,128)S(1)}, bf16[512,1024]{1,0:T(8,128)(2,1)}) custom-call(f32[128]{0:T(128)S(1)} %copy-done.2, f32[512,128]{1,0:T(8,128)S(1)} %get-tuple-element.32.refs_1_, f32[1,512]{1,0:T(1,128)S(1)} %bitcast.4, bf16[1024,512]{1,0:T(8,128)(2,1)S(1)} %get-tuple-element.33.refs_3_.refs_5_, ...), custom_call_target="tpu_custom_call" | custom-call | flops 1610612736 | bytes 2097152 | tf_op jit(solution)/shard_map/pairs/pallas_call | solution.py:178
  56.9 0.9 copy-done.7
  57.9 0.0 collective-permute-start.2
  57.9 19.9 %collective-permute-done.3.refs_7_ = bf16[1024,512]{1,0:T(8,128)(2,1)} collective-permute-done((bf16[1024,512]{1,0:T(8,128)(2,1)S(1)}, bf16[1024,512]{1,0:T(8,128)(2,1)}, u32[]{:S(2)}, u32[]{:S(2)}) %collective-permute-start.3) | collective-permute-done | bytes 1048608 | tf_op jit(solution)/shard_map/ppermute | solution.py:241
  77.8 0.0 collective-permute-done.4.refs_8_
  77.8 0.0 collective-permute-start.7
  77.8 0.5 collective-permute-start.8
  78.3 0.0 collective-permute-start.5
  78.3 7.5 %collective-permute-start.6 = (bf16[1024,512]{1,0:T(8,128)(2,1)}, bf16[1024,512]{1,0:T(8,128)(2,1)S(1)}, u32[]{:S(2)}, u32[]{:S(2)}) collective-permute-start(bf16[1024,512]{1,0:T(8,128)(2,1)} %collective-permute-done.4.refs_8_), channel_id=1, source_target_pairs={{4,0},{5,1},{6,2},{7,3},{8,4},{9,5},{10,6},{11,7},{12,8},{13,9},{1... | collective-permute-start | bytes 3145736 | tf_op jit(solution)/shard_map/ppermute | solution.py:241
  85.8 0.0 collective-permute-done.2.refs_4_.refs_3_
  85.8 0.0 collective-permute-done.7.refs_9_
  85.8 0.0 collective-permute-done.8.refs_10_
  85.8 1.2 copy-done.4
  87.0 1.2 copy-done.6
  88.3 1.2 copy-done.8
  89.5 10.9 %pairs.6 = (f32[512,512]{1,0:T(8,128)S(1)}, f32[512,512]{1,0:T(8,128)S(1)}) custom-call(f32[128]{0:T(128)S(1)} %copy-done.2, f32[512,128]{1,0:T(8,128)S(1)} %get-tuple-element.32.refs_1_, f32[1,512]{1,0:T(1,128)S(1)} %bitcast.5, bf16[512,1024]{1,0:T(8,128)(2,1)} %get-tuple-element.49.refs_3_, ...), custom_call_target="tpu_custom_call", output_to_operand_aliasing={{0}: (11, {})} | custom-call | flops 8053063680 | bytes 10485760 | tf_op jit(solution)/shard_map/pairs/pallas_call | solution.py:178
  100.4 1.0 copy-done.9
  101.4 7.6 %collective-permute-done.5.refs_4_ = bf16[1024,512]{1,0:T(8,128)(2,1)S(1)} collective-permute-done((bf16[1024,512]{1,0:T(8,128)(2,1)}, bf16[1024,512]{1,0:T(8,128)(2,1)S(1)}, u32[]{:S(2)}, u32[]{:S(2)}) %collective-permute-start.5) | collective-permute-done | bytes 1048608 | tf_op jit(solution)/shard_map/ppermute | solution.py:241
  109.0 0.0 collective-permute-done.6.refs_5_
  109.1 0.1 broadcast_select_fusion
  109.2 0.1 collective-permute-start.9
  109.3 2.4 %pairs.7.refs_5_ = f32[512,512]{1,0:T(8,128)S(1)} custom-call(f32[128]{0:T(128)S(1)} %copy-done.2, f32[512,128]{1,0:T(8,128)S(1)} %get-tuple-element.32.refs_1_, f32[1,512]{1,0:T(1,128)S(1)} %bitcast.6, bf16[512,1024]{1,0:T(8,128)(2,1)S(1)} %collective-permute-done.2.refs_4_.refs_3_, ...), custom_call_target="tpu_custom_call", output_to_operand_aliasing={{}: (6, {})} | custom-call | flops 1610612736 | bytes 2097152 | tf_op jit(solution)/shard_map/pairs/pallas_call | solution.py:178
  111.6 0.0 copy-start.10
  111.6 0.3 collective-permute-done.9.refs_4_.refs_6_
  111.9 2.0 %pairs.8 = (f32[256,512]{1,0:T(8,128)S(1)}, bf16[256,512]{1,0:T(8,128)(2,1)S(1)}) custom-call(f32[128]{0:T(128)S(1)} %copy-done.2, f32[512,128]{1,0:T(8,128)S(1)} %get-tuple-element.32.refs_1_, f32[1,512]{1,0:T(1,128)S(1)} %bitcast.7, bf16[512,1024]{1,0:T(8,128)(2,1)S(1)} %collective-permute-done.2.refs_4_.refs_3_, ...), custom_call_target="tpu_custom_call" | custom-call | flops 805306368 | bytes 1048576 | tf_op jit(solution)/shard_map/pairs/pallas_call | solution.py:178
  113.9 0.3 collective-permute-start.11
  114.2 0.0 copy-done.10
  114.2 4.0 %pairs.9 = (f32[256,512]{1,0:T(8,128)S(1)}, bf16[256,512]{1,0:T(8,128)(2,1)S(1)}) custom-call(f32[128]{0:T(128)S(1)} %copy-done.2, f32[512,128]{1,0:T(8,128)S(1)} %get-tuple-element.32.refs_1_, f32[1,512]{1,0:T(1,128)S(1)} %bitcast.8, bf16[512,1024]{1,0:T(8,128)(2,1)} %get-tuple-element.49.refs_3_, bf16[1024,512]{1,0:T(8,128)(2,1)S(1)} %collective-permute-done.5.refs_4_, ...), custom_call_target="tpu_custom_call" | custom-call | flops 2415919104 | bytes 3145728 | tf_op jit(solution)/shard_map/pairs/pallas_call | solution.py:178
  118.2 2.1 %collective-permute-start.10 = (bf16[256,512]{1,0:T(8,128)(2,1)S(1)}, bf16[256,512]{1,0:T(8,128)(2,1)S(1)}, u32[]{:S(2)}, u32[]{:S(2)}) collective-permute-start(bf16[256,512]{1,0:T(8,128)(2,1)S(1)} %get-tuple-element.51), channel_id=1, source_target_pairs={{0,1},{1,0},{2,3},{3,2},{4,5},{5,4},{6,7},{7,6},{8,9},{9,8},{10,11... | collective-permute-start | bytes 786440 | tf_op jit(solution)/shard_map/ppermute | solution.py:247
  120.3 3.0 %collective-permute-done.11.refs_1_ = bf16[256,512]{1,0:T(8,128)(2,1)S(1)} collective-permute-done((bf16[256,512]{1,0:T(8,128)(2,1)S(1)}, bf16[256,512]{1,0:T(8,128)(2,1)S(1)}, u32[]{:S(2)}, u32[]{:S(2)}) %collective-permute-start.11) | collective-permute-done | bytes 262176 | tf_op jit(solution)/shard_map/ppermute | solution.py:247
  123.3 0.8 finish.2.refs_2_
  124.2 4.1 %collective-permute-done.10.refs_1_ = bf16[256,512]{1,0:T(8,128)(2,1)S(1)} collective-permute-done((bf16[256,512]{1,0:T(8,128)(2,1)S(1)}, bf16[256,512]{1,0:T(8,128)(2,1)S(1)}, u32[]{:S(2)}, u32[]{:S(2)}) %collective-permute-start.10) | collective-permute-done | bytes 262176 | tf_op jit(solution)/shard_map/ppermute | solution.py:247
  128.2 0.9 finish.3
  (10 shorter events, 0.0 us)
Async XLA Ops:
  7.1 11.2 %copy-start = (bf16[384,512]{1,0:T(8,128)(2,1)S(1)}, bf16[384,512]{1,0:T(8,128)(2,1)}, u32[]{:S(2)}) copy-start(bf16[384,512]{1,0:T(8,128)(2,1)} %vir_ref.1) | copy-start | bytes 1179652
  7.1 38.3 %copy-start.1 = (f32[512]{0:T(512)S(1)}, f32[512]{0:T(512)}, u32[]{:S(2)}) copy-start(f32[512]{0:T(512)} %param.9) | copy-start | bytes 6148
  7.1 38.3 %all-to-all-start = ((bf16[128,16,384]{2,1,0:T(8,128)(2,1)}), bf16[128,16,384]{2,1,0:T(8,128)(2,1)S(1)}, u32[]{:S(2)}, u32[]{:S(2)}) async-start(bf16[128,16,384]{2,1,0:T(8,128)(2,1)} %transform.1), calls=%async_computation | async-start | bytes 3145728 | tf_op jit(solution)/shard_map/all_to_all | solution.py:253
  18.3 36.0 %copy-start.2 = (f32[128]{0:T(128)S(1)}, f32[128]{0:T(128)}, u32[]{:S(2)}) copy-start(f32[128]{0:T(128)} %refs_0_.11) | copy-start | bytes 1540
  18.3 27.1 %collective-permute-start = (bf16[384,512]{1,0:T(8,128)(2,1)S(1)}, bf16[384,512]{1,0:T(8,128)(2,1)S(1)}, u32[]{:S(2)}, u32[]{:S(2)}) collective-permute-start(bf16[384,512]{1,0:T(8,128)(2,1)S(1)} %copy-done), channel_id=1, source_target_pairs={{0,1},{1,0},{2,3},{3,2},{4,5},{5,4},{6,7},{7,6},{8,9},{9,8},{10,11... | collective-permute-start | bytes 1179656 | tf_op jit(solution)/shard_map/ppermute | solution.py:247
  46.6 10.3 %copy-start.3 = (bf16[1024,512]{1,0:T(8,128)(2,1)}, bf16[1024,512]{1,0:T(8,128)(2,1)S(1)}, u32[]{:S(2)}) copy-start(bf16[1024,512]{1,0:T(8,128)(2,1)S(1)} %get-tuple-element.33.refs_3_.refs_5_) | copy-start | bytes 3145732
  46.6 7.6 %collective-permute-start.1 = (bf16[1024,512]{1,0:T(8,128)(2,1)S(1)}, bf16[1024,512]{1,0:T(8,128)(2,1)S(1)}, u32[]{:S(2)}, u32[]{:S(2)}) collective-permute-start(bf16[1024,512]{1,0:T(8,128)(2,1)S(1)} %get-tuple-element.33.refs_3_.refs_5_), channel_id=1, source_target_pairs={{2,0},{0,2},{6,4},{4,6},{10,8},{8,10},{14,12},{12,14},{18,16},{16,... | collective-permute-start | bytes 3145736 | tf_op jit(solution)/shard_map/ppermute | solution.py:244
  46.7 31.1 %collective-permute-start.3 = (bf16[1024,512]{1,0:T(8,128)(2,1)S(1)}, bf16[1024,512]{1,0:T(8,128)(2,1)}, u32[]{:S(2)}, u32[]{:S(2)}) collective-permute-start(bf16[1024,512]{1,0:T(8,128)(2,1)S(1)} %get-tuple-element.33.refs_3_.refs_5_), channel_id=1, source_target_pairs={{125,0},{124,1},{127,2},{126,3},{0,4},{1,5},{2,6},{3,7},{4,8},{5,9... | collective-permute-start | bytes 3145736 | tf_op jit(solution)/shard_map/ppermute | solution.py:241
  48.3 29.6 %collective-permute-start.4 = (bf16[1024,512]{1,0:T(8,128)(2,1)S(1)}, bf16[1024,512]{1,0:T(8,128)(2,1)}, u32[]{:S(2)}, u32[]{:S(2)}) collective-permute-start(bf16[1024,512]{1,0:T(8,128)(2,1)S(1)} %get-tuple-element.33.refs_3_.refs_5_), channel_id=1, source_target_pairs={{4,0},{5,1},{6,2},{7,3},{8,4},{9,5},{10,6},{11,7},{12,8},{13,9},{1... | collective-permute-start | bytes 3145736 | tf_op jit(solution)/shard_map/ppermute | solution.py:241
  54.2 2.7 %copy-start.5 = (bf16[1024,512]{1,0:T(8,128)(2,1)}, bf16[1024,512]{1,0:T(8,128)(2,1)S(1)}, u32[]{:S(2)}) copy-start(bf16[1024,512]{1,0:T(8,128)(2,1)S(1)} %collective-permute-done.1.refs_4_.refs_6_) | copy-start | bytes 3145732
  56.9 1.0 copy-start.7
  57.9 27.9 %collective-permute-start.2 = (bf16[512,1024]{1,0:T(8,128)(2,1)}, bf16[512,1024]{1,0:T(8,128)(2,1)S(1)}, u32[]{:S(2)}, u32[]{:S(2)}) collective-permute-start(bf16[512,1024]{1,0:T(8,128)(2,1)} %get-tuple-element.49.refs_3_), channel_id=1, source_target_pairs={{0,1},{1,0},{2,3},{3,2},{4,5},{5,4},{6,7},{7,6},{8,9},{9,8},{10,11... | collective-permute-start | bytes 3145736 | tf_op jit(solution)/shard_map/ppermute | solution.py:247
  77.8 8.0 %collective-permute-start.7 = (bf16[1024,512]{1,0:T(8,128)(2,1)}, bf16[1024,512]{1,0:T(8,128)(2,1)}, u32[]{:S(2)}, u32[]{:S(2)}) collective-permute-start(bf16[1024,512]{1,0:T(8,128)(2,1)} %collective-permute-done.3.refs_7_), channel_id=1, source_target_pairs={{2,0},{0,2},{6,4},{4,6},{10,8},{8,10},{14,12},{12,14},{18,16},{16,... | collective-permute-start | bytes 3145736 | tf_op jit(solution)/shard_map/ppermute | solution.py:244
  77.8 8.0 %collective-permute-start.8 = (bf16[1024,512]{1,0:T(8,128)(2,1)}, bf16[1024,512]{1,0:T(8,128)(2,1)}, u32[]{:S(2)}, u32[]{:S(2)}) collective-permute-start(bf16[1024,512]{1,0:T(8,128)(2,1)} %collective-permute-done.4.refs_8_), channel_id=1, source_target_pairs={{2,0},{0,2},{6,4},{4,6},{10,8},{8,10},{14,12},{12,14},{18,16},{16,... | collective-permute-start | bytes 3145736 | tf_op jit(solution)/shard_map/ppermute | solution.py:244
  78.3 30.7 %collective-permute-start.5 = (bf16[1024,512]{1,0:T(8,128)(2,1)}, bf16[1024,512]{1,0:T(8,128)(2,1)S(1)}, u32[]{:S(2)}, u32[]{:S(2)}) collective-permute-start(bf16[1024,512]{1,0:T(8,128)(2,1)} %collective-permute-done.3.refs_7_), channel_id=1, source_target_pairs={{125,0},{124,1},{127,2},{126,3},{0,4},{1,5},{2,6},{3,7},{4,8},{5,9... | collective-permute-start | bytes 3145736 | tf_op jit(solution)/shard_map/ppermute | solution.py:241
  78.3 30.7 %collective-permute-start.6 = (bf16[1024,512]{1,0:T(8,128)(2,1)}, bf16[1024,512]{1,0:T(8,128)(2,1)S(1)}, u32[]{:S(2)}, u32[]{:S(2)}) collective-permute-start(bf16[1024,512]{1,0:T(8,128)(2,1)} %collective-permute-done.4.refs_8_), channel_id=1, source_target_pairs={{4,0},{5,1},{6,2},{7,3},{8,4},{9,5},{10,6},{11,7},{12,8},{13,9},{1... | collective-permute-start | bytes 3145736 | tf_op jit(solution)/shard_map/ppermute | solution.py:241
  85.8 1.2 copy-start.4
  87.0 1.2 copy-start.6
  88.3 1.2 copy-start.8
  100.4 1.0 copy-start.9
  109.2 2.7 %collective-permute-start.9 = (bf16[1024,512]{1,0:T(8,128)(2,1)S(1)}, bf16[1024,512]{1,0:T(8,128)(2,1)S(1)}, u32[]{:S(2)}, u32[]{:S(2)}) collective-permute-start(bf16[1024,512]{1,0:T(8,128)(2,1)S(1)} %broadcast_select_fusion), channel_id=1, source_target_pairs={{2,0},{0,2},{6,4},{4,6},{10,8},{8,10},{14,12},{12,14},{18,16},{16,... | collective-permute-start | bytes 3145736 | tf_op jit(solution)/shard_map/ppermute | solution.py:244
  111.6 2.5 %copy-start.10 = (f32[512,512]{1,0:T(8,128)S(1)}, f32[512,512]{1,0:T(8,128)}, u32[]{:S(2)}) copy-start(f32[512,512]{1,0:T(8,128)} %copy-done.9) | copy-start | bytes 3145732
  113.9 9.4 %collective-permute-start.11 = (bf16[256,512]{1,0:T(8,128)(2,1)S(1)}, bf16[256,512]{1,0:T(8,128)(2,1)S(1)}, u32[]{:S(2)}, u32[]{:S(2)}) collective-permute-start(bf16[256,512]{1,0:T(8,128)(2,1)S(1)} %get-tuple-element.48), channel_id=1, source_target_pairs={{0,1},{1,0},{2,3},{3,2},{4,5},{5,4},{6,7},{7,6},{8,9},{9,8},{10,11... | collective-permute-start | bytes 786440 | tf_op jit(solution)/shard_map/ppermute | solution.py:247
  118.2 10.1 %collective-permute-start.10 = (bf16[256,512]{1,0:T(8,128)(2,1)S(1)}, bf16[256,512]{1,0:T(8,128)(2,1)S(1)}, u32[]{:S(2)}, u32[]{:S(2)}) collective-permute-start(bf16[256,512]{1,0:T(8,128)(2,1)S(1)} %get-tuple-element.51), channel_id=1, source_target_pairs={{0,1},{1,0},{2,3},{3,2},{4,5},{5,4},{6,7},{7,6},{8,9},{9,8},{10,11... | collective-permute-start | bytes 786440 | tf_op jit(solution)/shard_map/ppermute | solution.py:247
